TPU v7x, 32 devices: a whole 2x2x4 slice. The times are simulated.
32 devices in a mesh: fsdp: 8 (over z, core), seq: 4 (over y, x).
Axes of the slice: x: 2, y: 2, z: 4, core: 2. Of those that a mesh axis runs over, the one named last changes fastest.
Arguments:
- inputs: bfloat16 [8, 1024, 2048], P('fsdp', 'seq'), may hold values from -6 to 6
- cotangent: bfloat16 [8, 1024, 2048], P('fsdp', 'seq'), may hold values from -6 to 6
- norm1_gain: bfloat16 [2048], P('fsdp'), may hold values from 0.5 to 1.5
- w_qkv: bfloat16 [2048, 6144], P('fsdp'), may hold values from -0.125 to 0.125
- w_beta: bfloat16 [2048, 16], P('fsdp'), may hold values from -0.125 to 0.125
- conv_weight: bfloat16 [2048, 12], P('fsdp'), may hold values from -3 to 3
- out_gain: bfloat16 [128], replicated, may hold values from 0.5 to 1.5
- w_out: bfloat16 [2048, 2048], P('fsdp'), may hold values from -0.125 to 0.125
- norm2_gain: bfloat16 [2048], P('fsdp'), may hold values from 0.5 to 1.5
- w_gate_up: bfloat16 [2048, 11264], P('fsdp'), may hold values from -0.125 to 0.125
- w_down: bfloat16 [5632, 2048], P('fsdp'), may hold values from -0.15625 to 0.15625
Outputs:
- output: bfloat16 [8, 1024, 2048], P('fsdp', 'seq')
- grad_input: float32 [8, 1024, 2048], P('fsdp', 'seq')
- grad_norm1_gain: float32 [2048], P('fsdp')
- grad_w_qkv: float32 [2048, 6144], P('fsdp')
- grad_w_beta: float32 [2048, 16], P('fsdp')
- grad_conv_weight: float32 [2048, 12], P('fsdp')
- grad_out_gain: float32 [128], replicated
- grad_w_out: float32 [2048, 2048], P('fsdp')
- grad_norm2_gain: float32 [2048], P('fsdp')
- grad_w_gate_up: float32 [2048, 11264], P('fsdp')
- grad_w_down: float32 [5632, 2048], P('fsdp')
All inputs are finite; a program needn't handle non-finite values.
Results may differ from a plain program's by a relative error of at most 0.023.
Values may be sent and summed in bfloat16 or wider, within the bound.
A program may use at most 448 MiB of HBM per device.

v0:
```python
import jax
import jax.numpy as jnp
from jax import lax
from jax.sharding import PartitionSpec as P

H = 16
DK = 128
SPAN = 64


EPS = 1e-06
HIGH = lax.Precision.HIGHEST


def from_behind(array, axis, by):
    devices = lax.axis_size(axis)
    pairs = [(i, i + by) for i in range(devices) if 0 <= i + by < devices]
    return lax.ppermute(array, axis, pairs)


def rms_scale(values, gain):
    return values * lax.rsqrt(jnp.mean(values * values, axis=-1, keepdims=True) + EPS) * gain


def conv_table(conv_full):
    width = conv_full.shape[0]
    tap_count = conv_full.shape[1] // 3
    return (
        conv_full.astype(jnp.float32)
        .reshape(width, 3, tap_count)
        .transpose(1, 0, 2)
        .reshape(3 * width, tap_count)
    )


def pre_mix(extended, table, beta_logits):
    tap_count = table.shape[1]
    length = extended.shape[1] - tap_count + 1
    sequences = extended.shape[0]
    width = extended.shape[2] // 3
    mixed = extended[:, 0:length, :] * table[:, 0]
    for tap_index in range(1, tap_count):
        mixed = mixed + extended[:, tap_index : tap_index + length, :] * table[:, tap_index]
    active = jax.nn.silu(mixed)
    query = active[:, :, :width].reshape(sequences, length, H, DK) * DK ** (-0.5)
    key = active[:, :, width : 2 * width].reshape(sequences, length, H, DK)
    key = key * lax.rsqrt(jnp.sum(key * key, axis=-1, keepdims=True) + EPS)
    value = active[:, :, 2 * width :].reshape(sequences, length, H, DK)
    return (query, key, value, jax.nn.sigmoid(beta_logits))


def delta_rule(query, key, value, beta):
    sequences, length, heads, depth = query.shape
    count = length // SPAN

    def blocks(array):
        return array.reshape(sequences, count, SPAN, heads, -1).transpose(1, 0, 3, 2, 4)

    q_blocks = blocks(query)
    k_blocks = blocks(key)
    v_blocks = blocks(value)
    b_blocks = blocks(beta[..., None])
    gram = jnp.einsum("nshcd,nshmd->nshcm", k_blocks, k_blocks, precision=HIGH)
    below = jnp.tril(jnp.ones((SPAN, SPAN), jnp.float32), -1)
    inclusive = jnp.tril(jnp.ones((SPAN, SPAN), jnp.float32))
    system = jnp.eye(SPAN, dtype=jnp.float32) + below * (b_blocks * gram)
    targets = jnp.concatenate([b_blocks * k_blocks, b_blocks * v_blocks], axis=-1)
    solved = lax.linalg.triangular_solve(
        system, targets, left_side=True, lower=True, unit_diagonal=True
    )
    wy_key = solved[..., :depth]
    wy_value = solved[..., depth:]
    within = inclusive * jnp.einsum("nshcd,nshmd->nshcm", q_blocks, k_blocks, precision=HIGH)

    def advance(state, pieces):
        key_part, value_part, query_part, key_raw, attend = pieces
        fresh = value_part - jnp.einsum("shcd,shde->shce", key_part, state, precision=HIGH)
        result = jnp.einsum("shcd,shde->shce", query_part, state, precision=HIGH)
        result = result + jnp.einsum("shcm,shme->shce", attend, fresh, precision=HIGH)
        state = state + jnp.einsum("shcd,shce->shde", key_raw, fresh, precision=HIGH)
        return (state, result)

    start = jnp.zeros((sequences, heads, depth, value.shape[-1]), jnp.float32)
    final, outputs = lax.scan(advance, start, (wy_key, wy_value, q_blocks, k_blocks, within))
    return outputs.transpose(1, 0, 3, 2, 4).reshape(sequences, length, heads, -1)


def row_term(left, right):

    def term(start, count):
        return lax.dot_general(
            left, right, (((0,), (0,)), ((), ())), preferred_element_type=jnp.float32
        )

    return term


def reduce_rows(term, total_rows):
    shards = lax.axis_size("fsdp")
    summed = lax.psum_scatter(
        term(jnp.int32(0), total_rows // shards * lax.axis_size("fsdp")).astype(jnp.bfloat16),
        "fsdp",
        scatter_dimension=0,
        tiled=True,
    )
    return lax.psum(summed, "seq").astype(jnp.float32)


def against(left, right):
    return lax.dot_general(
        left, right, (((1,), (1,)), ((), ())), preferred_element_type=jnp.float32
    )


def per_device(
    inputs,
    cotangent,
    norm1_gain,
    w_qkv,
    w_beta,
    conv_weight,
    out_gain,
    w_out,
    norm2_gain,
    w_gate_up,
    w_down,
):
    gathered = (
        lax.all_gather(norm1_gain, "fsdp", axis=0, tiled=True),
        lax.all_gather(w_qkv, "fsdp", axis=0, tiled=True),
        lax.all_gather(w_beta, "fsdp", axis=0, tiled=True),
        lax.all_gather(conv_weight, "fsdp", axis=0, tiled=True),
        lax.all_gather(w_out, "fsdp", axis=0, tiled=True),
        lax.all_gather(norm2_gain, "fsdp", axis=0, tiled=True),
        lax.all_gather(w_gate_up, "fsdp", axis=0, tiled=True),
    )
    gain_first, qkv_full, beta_full, conv_full, out_full, gain_second, gate_up_full = gathered
    down_full = lax.all_gather(w_down, "fsdp", axis=0, tiled=True)
    sequences, block, width = inputs.shape
    tokens = sequences * block
    hidden_width = down_full.shape[0]
    edge_rows = conv_full.shape[1] // 3 - 1
    residual = inputs.astype(jnp.float32).reshape(tokens, width)
    first_normed, first_back = jax.vjp(rms_scale, residual, gain_first.astype(jnp.float32))
    normed_first = first_normed.astype(jnp.bfloat16)
    projected = jnp.dot(normed_first, qkv_full, preferred_element_type=jnp.float32)
    projected = projected.astype(jnp.bfloat16).reshape(sequences, block, 3 * width)
    beta_logits = jnp.dot(normed_first, beta_full, preferred_element_type=jnp.float32).reshape(
        sequences, block, -1
    )
    before = from_behind(projected[:, block - edge_rows :, :], "seq", 1)
    extended = jnp.concatenate([before, projected], axis=1).astype(jnp.float32)
    table = conv_table(conv_full)
    mixer_inputs, mixer_back = jax.vjp(pre_mix, extended, table, beta_logits)
    sent_query = mixer_inputs[0].astype(jnp.bfloat16)
    sent_key = mixer_inputs[1].astype(jnp.bfloat16)
    sent_value = mixer_inputs[2].astype(jnp.bfloat16)
    sent_beta = mixer_inputs[3].astype(jnp.bfloat16)
    query, key, value, beta = (
        lax.all_to_all(sent_query, "seq", split_axis=2, concat_axis=1, tiled=True),
        lax.all_to_all(sent_key, "seq", split_axis=2, concat_axis=1, tiled=True),
        lax.all_to_all(sent_value, "seq", split_axis=2, concat_axis=1, tiled=True),
        lax.all_to_all(sent_beta, "seq", split_axis=2, concat_axis=1, tiled=True),
    )
    heads_out, delta_back = jax.vjp(
        delta_rule,
        query.astype(jnp.float32),
        key.astype(jnp.float32),
        value.astype(jnp.float32),
        beta.astype(jnp.float32),
    )
    returned = lax.all_to_all(
        heads_out.astype(jnp.bfloat16), "seq", split_axis=1, concat_axis=2, tiled=True
    )
    normed_heads, heads_back = jax.vjp(
        rms_scale, returned.astype(jnp.float32), out_gain.astype(jnp.float32)
    )
    attn_in = normed_heads.astype(jnp.bfloat16).reshape(tokens, width)
    middle = residual + jnp.dot(attn_in, out_full, preferred_element_type=jnp.float32)
    second_normed, second_back = jax.vjp(rms_scale, middle, gain_second.astype(jnp.float32))
    ffn_in = second_normed.astype(jnp.bfloat16)
    gate_up = jnp.dot(ffn_in, gate_up_full, preferred_element_type=jnp.float32)
    gate = gate_up[:, :hidden_width]
    upward = gate_up[:, hidden_width:]
    sigma = jax.nn.sigmoid(gate)
    hidden = (gate * sigma * upward).astype(jnp.bfloat16)
    result = middle + jnp.dot(hidden, down_full, preferred_element_type=jnp.float32)
    output = result.astype(jnp.bfloat16).reshape(sequences, block, width)
    upstream = cotangent.reshape(tokens, width)
    grad_down = reduce_rows(row_term(hidden, upstream), hidden_width)
    grad_hidden = against(upstream, down_full)
    grad_gate = grad_hidden * upward * sigma * (1.0 + gate * (1.0 - sigma))
    grad_up = grad_hidden * gate * sigma
    grad_gate_up = jnp.concatenate([grad_gate, grad_up], axis=1).astype(jnp.bfloat16)
    grad_w_gate_up = reduce_rows(row_term(ffn_in, grad_gate_up), width)
    grad_ffn_in = against(grad_gate_up, gate_up_full)
    grad_middle_norm, grad_gain_second = second_back(grad_ffn_in)
    grad_middle = upstream.astype(jnp.float32) + grad_middle_norm
    grad_branch = grad_middle.astype(jnp.bfloat16)
    grad_w_out = reduce_rows(row_term(attn_in, grad_branch), width)
    grad_attn_in = against(grad_branch, out_full).reshape(sequences, block, H, DK)
    grad_returned, grad_gain_heads = heads_back(grad_attn_in)
    grad_heads = lax.all_to_all(
        grad_returned.astype(jnp.bfloat16), "seq", split_axis=2, concat_axis=1, tiled=True
    )
    grad_query, grad_key, grad_value, grad_beta = delta_back(grad_heads.astype(jnp.float32))
    back_query, back_key, back_value, back_beta = (
        lax.all_to_all(
            grad_query.astype(jnp.bfloat16), "seq", split_axis=1, concat_axis=2, tiled=True
        ),
        lax.all_to_all(
            grad_key.astype(jnp.bfloat16), "seq", split_axis=1, concat_axis=2, tiled=True
        ),
        lax.all_to_all(
            grad_value.astype(jnp.bfloat16), "seq", split_axis=1, concat_axis=2, tiled=True
        ),
        lax.all_to_all(
            grad_beta.astype(jnp.bfloat16), "seq", split_axis=1, concat_axis=2, tiled=True
        ),
    )
    grad_extended, grad_table, grad_logits = mixer_back(
        (
            back_query.astype(jnp.float32),
            back_key.astype(jnp.float32),
            back_value.astype(jnp.float32),
            back_beta.astype(jnp.float32),
        )
    )
    after = from_behind(grad_extended[:, :edge_rows, :].astype(jnp.bfloat16), "seq", -1).astype(
        jnp.float32
    )
    grad_projected = grad_extended[:, edge_rows:, :]
    grad_projected = grad_projected.at[:, block - edge_rows :, :].add(after)
    grad_proj_low = grad_projected.astype(jnp.bfloat16).reshape(tokens, 3 * width)
    grad_logits_low = grad_logits.astype(jnp.bfloat16).reshape(tokens, -1)
    grad_w_qkv = reduce_rows(row_term(normed_first, grad_proj_low), width)
    grad_beta_full = lax.dot_general(
        normed_first, grad_logits_low, (((0,), (0,)), ((), ())), preferred_element_type=jnp.float32
    )
    grad_normed_first = against(grad_proj_low, qkv_full) + against(grad_logits_low, beta_full)
    grad_residual_norm, grad_gain_first = first_back(grad_normed_first)
    grad_input = (grad_middle + grad_residual_norm).reshape(sequences, block, width)
    grad_conv = grad_table.reshape(3, width, -1).transpose(1, 0, 2).reshape(width, -1)
    summed = lax.psum(
        (grad_gain_first, grad_beta_full, grad_conv, grad_gain_heads, grad_gain_second),
        ("fsdp", "seq"),
    )
    share = width // lax.axis_size("fsdp")
    offset = lax.axis_index("fsdp") * share

    def own_rows(array):
        return lax.dynamic_slice_in_dim(array, offset, share, 0)

    return (
        output,
        grad_input,
        own_rows(summed[0]),
        grad_w_qkv,
        own_rows(summed[1]),
        own_rows(summed[2]),
        summed[3],
        grad_w_out,
        own_rows(summed[4]),
        grad_w_gate_up,
        grad_down,
    )


def solution(mesh):
    in_specs = (
        P("fsdp", "seq", None),
        P("fsdp", "seq", None),
        P("fsdp"),
        P("fsdp", None),
        P("fsdp", None),
        P("fsdp", None),
        P(),
        P("fsdp", None),
        P("fsdp"),
        P("fsdp", None),
        P("fsdp", None),
    )
    out_specs = (
        P("fsdp", "seq", None),
        P("fsdp", "seq", None),
        P("fsdp"),
        P("fsdp", None),
        P("fsdp", None),
        P("fsdp", None),
        P(),
        P("fsdp", None),
        P("fsdp"),
        P("fsdp", None),
        P("fsdp", None),
    )
    return jax.shard_map(
        per_device, mesh=mesh, in_specs=in_specs, out_specs=out_specs, check_vma=False
    )
```

profile of v0, /device:TPU:0, one launch (start us, length us, event | category | flops | bytes accessed | tf_op | source)
XLA Modules:
  0.0 2502.5 jit_solution(38190960428922679)
XLA Ops:
  10.1 13.6 all-gather
  23.7 24.1 all_gather.27
  54.7 25.3 %all_gather.26 = bf16[2048,12]{0,1:T(8,128)(2,1)S(1)} all-gather(bf16[256,12]{0,1:T(8,128)(2,1)S(1)} %copy-done.77), channel_id=1, replica_groups=mesh['fsdp'=8,'seq'=4] {'fsdp'}, dimensions={0}, use_global_device_ids=true | all-gather | bytes 55296 | tf_op jit(solution)/shard_map/all_gather | solution.py:132
  80.0 153.2 %all-gather.7.cloned.1.call-done = bf16[2048,6144]{1,0:T(8,128)(2,1)} async-done(((bf16[256,6144]{1,0:T(8,128)(2,1)}), bf16[2048,6144]{1,0:T(8,128)(2,1)}) %all-gather.7.cloned.1.call-update) | async-done | bytes 25165840 | tf_op jit(solution)/shard_map/all_gather | solution.py:130
  233.2 12.3 fusion.79
  251.5 5.4 fusion.82
  262.7 4.5 all-to-all-start
  268.5 12.8 all-to-all-done
  287.6 11.2 all-to-all-done.3
  306.6 10.2 all-to-all-done.2
  322.1 315.2 %custom-call.7 = f32[16,1,4,1,64,64]{4,5,3,2,1,0:T(8,128)S(1)} custom-call(f32[16,1,4,1,64,64]{5,4,3,2,1,0:T(8,128)} %add_bitcast_fusion), custom_call_target="InvertDiagBlocksLowerTriangular" | custom-call | tf_op jit(solution)/shard_map/jvp()/triangular_solve | solution.py:68
  637.4 4.7 multiply_bitcast_fusion.1
  652.7 107.0 %while.43 = (s32[]{:T(128)}, f32[1,4,128,128]{3,2,1,0:T(8,128)S(1)}, bf16[16,1,4,64,128]{4,3,0,2,1:T(8,128)(2,1)}, f32[16,1,4,128,128]{4,3,2,1,0:T(8,128)}, f32[...) while((s32[]{:T(128)}, ...), condition=%wide.region_3.4_spmd.clone, body=%wide.region_2.3_spmd.clone.sunk | while | flops 176553984 | bytes 3148948 | solution.py:84
  763.5 4.3 all-to-all-start.4
  767.9 9.1 all-gather.1
  777.0 4.1 all-to-all-done.4
  796.3 6.5 multiply_reduce_fusion.8
  802.8 24.2 fusion.211
  827.1 84.3 %all-gather.13.cloned.1.call-done = bf16[5632,2048]{1,0:T(8,128)(2,1)} async-done(((bf16[704,2048]{1,0:T(8,128)(2,1)}), bf16[5632,2048]{1,0:T(8,128)(2,1)}) %all-gather.13.cloned.1.call-update) | async-done | bytes 23068688 | tf_op jit(solution)/shard_map/all_gather | solution.py:138
  911.3 18.8 multiply_convert_fusion.1
  930.1 22.3 multiply_reduce_fusion.4
  955.6 5.8 convolution_convert_fusion.4
  961.5 12.8 convolution_convert_fusion.1
  977.7 8.4 multiply_reduce_fusion.5
  1002.1 14.2 all-to-all-done.5
  1026.0 241.0 %while.44 = (s32[]{:T(128)}, f32[1,4,128,128]{2,3,1,0:T(8,128)S(1)}, f32[16,1,4,64,128]{4,3,2,1,0:T(8,128)}, f32[16,1,4,64,128]{4,3,2,1,0:T(8,128)}, f32[16,1,4,...) while((s32[]{:T(128)}, ...), condition=%wide.region_9.10_spmd.clone, body=%wide.region_8.9_spmd.clone.sunk | while | flops 352747520 | bytes 4728510 | solution.py:84
  1267.0 5.8 fusion.106
  1272.9 4.7 fusion.86
  1290.9 4.2 all-to-all-start.7
  1300.0 8.8 all-to-all-done.7
  1308.8 4.3 all-to-all-start.8
  1329.5 4.2 all-to-all-start.6
  1356.1 5.9 add_add_fusion.1
  1362.1 10.6 multiply_reduce_fusion.3
  1372.7 6.3 broadcast_multiply_fusion
  1379.0 6.5 pad_add_fusion
  1394.1 14.0 convolution_convert_fusion.2
  1409.8 21.2 convolution_convert_fusion
  1436.5 8.9 all_to_all.105
  1450.7 203.7 %reduce-scatter.7.cloned.1.call-done = bf16[256,6144]{1,0:T(8,128)(2,1)} async-done(((bf16[2048,6144]{1,0:T(8,128)(2,1)}), bf16[256,6144]{1,0:T(8,128)(2,1)}) %reduce-scatter.7.cloned.1.call-update) | async-done | bytes 3145744 | tf_op jit(solution)/shard_map/reduce_scatter | solution.py:100
  1654.5 444.5 %reduce-scatter.13.cloned.1.call-done = bf16[256,11264]{1,0:T(8,128)(2,1)} async-done(((bf16[2048,11264]{1,0:T(8,128)(2,1)}), bf16[256,11264]{1,0:T(8,128)(2,1)}) %reduce-scatter.13.cloned.1.call-update) | async-done | bytes 5767184
  2099.7 12.6 fusion.105
  2114.1 14.4 fusion.110
  2128.5 38.2 %all-reduce.14 = (f32[2048]{0:T(1024)S(1)}, f32[128]{0:T(128)}, f32[2048]{0:T(1024)S(1)}) all-reduce(f32[2048]{0:T(1024)S(1)} %get-tuple-element.617, f32[128]{0:T(128)S(1)} %bitcast_reduce_fusion, f32[2048]{0:T(1024)S(1)} %copy-done.78), channel_id=1, replica_groups=mesh['fsdp'=8,'seq'=4] {'fsdp','seq'}, use_global_device_ids=true, to_apply=%region_16.17 | all-reduce | flops 4224 | bytes 33792 | tf_op jit(solution)/shard_map/psum | solution.py:244
  2171.5 58.3 %all-reduce.20.cloned.1.call-done = (f32[2048,16]{0,1:T(8,128)}, f32[2048,12]{0,1:T(8,128)}) async-done(((f32[2048,16]{0,1:T(8,128)}, f32[2048,12]{0,1:T(8,128)}), (f32[2048,16]{0,1:T(8,128)}, f32[2048,12]{0,1:T(8,128)})) %all-reduce.20.cloned.1.call-update) | async-done | bytes 229392 | tf_op jit(solution)/shard_map/psum | solution.py:244
  2232.4 246.7 %all-reduce.22.cloned.1.call-done = (bf16[256,6144]{1,0:T(8,128)(2,1)}, bf16[256,2048]{1,0:T(8,128)(2,1)}, bf16[256,11264]{1,0:T(8,128)(2,1)}, bf16[704,2048]{1,0:T(8,128)(2,1)}) async-done(((bf16[256,6144]{1,0:T(8,128)(2,1)}, bf16[256,2048]{1,0:T(8,128)(2,1)}, bf16[256,11264]{1,0:T(8,128)(2,1)}, bf16[704,2048]{1,0:T(8,128)(2,1)}), (bf16[256,6144]{1,0:T(8,128)(2,1)}, bf16[256,2048]{1,0:T(8,128)(2,1)}, ...) | async-done | bytes 12845072 | tf_op jit(solution)/shard_map/psum | solution.py:106
  2479.1 5.5 convert_element_type.516
  2486.1 5.8 convert_element_type.520
  (556 shorter events, 543.3 us)
Async XLA Ops:
  7.2 226.0 %all-gather.7.cloned.1.call-start = ((), (), s32[]{:S(2)}) async-start(), calls=%async_computation.14 | async-start | bytes 28311552 | tf_op jit(solution)/shard_map/all_gather | solution.py:130
  7.9 788.4 %all-gather.9.cloned.1.call-start = ((), (), s32[]{:S(2)}) async-start(), calls=%async_computation.15 | async-start | bytes 9437184 | tf_op jit(solution)/shard_map/all_gather | solution.py:133
  8.7 794.2 %all-gather.11.cloned.1.call-start = ((), (), s32[]{:S(2)}) async-start(), calls=%async_computation.16 | async-start | bytes 51904512 | tf_op jit(solution)/shard_map/all_gather | solution.py:135
  9.4 14.2 copy-start.76
  9.4 38.4 %copy-start.27 = (bf16[1,256,2048]{2,1,0:T(8,128)(2,1)S(1)}, bf16[1,256,2048]{2,1,0:T(8,128)(2,1)}, u32[]{:S(2)}) copy-start(bf16[1,256,2048]{2,1,0:T(8,128)(2,1)} %param.17) | copy-start | bytes 3145732
  9.4 901.9 %all-gather.13.cloned.1.call-start = ((), (), s32[]{:S(2)}) async-start(), calls=%async_computation.17 | async-start | bytes 25952256 | tf_op jit(solution)/shard_map/all_gather | solution.py:138
  10.1 44.6 %copy-start.77 = (bf16[256,12]{0,1:T(8,128)(2,1)S(1)}, bf16[256,12]{0,1:T(8,128)(2,1)}, u32[]{:S(2)}) copy-start(bf16[256,12]{0,1:T(8,128)(2,1)} %param.22) | copy-start | bytes 18436
  23.7 221.9 %copy-start.46 = (f32[8,1,256]{2,1,0:T(1,128)}, f32[8,1,256]{2,1,0:T(1,128)S(1)}, u32[]{:S(2)}) copy-start(f32[8,1,256]{2,1,0:T(1,128)S(1)} %convert_element_type.540) | copy-start | bytes 24580
  48.7 196.9 %copy-start.70 = (f32[256]{0:T(256)}, f32[256]{0:T(256)S(1)}, u32[]{:S(2)}) copy-start(f32[256]{0:T(256)S(1)} %fusion.204) | copy-start | bytes 3076
  51.0 211.7 %all-to-all-start.1 = ((bf16[4,2,512]{2,1,0:T(2,128)(2,1)}), bf16[4,2,512]{2,1,0:T(2,128)(2,1)S(1)}, u32[]{:S(2)}, u32[]{:S(2)}) async-start(bf16[4,2,512]{2,1,0:T(2,128)(2,1)} %reshape.1133), calls=%async_computation.1 | async-start | bytes 16384 | tf_op jit(solution)/shard_map/all_to_all | solution.py:163
  245.6 4.9 collective-permute-start
  262.7 18.6 all-to-all-start
  281.3 17.5 all-to-all-start.3
  299.8 17.0 all-to-all-start.2
  303.5 333.8 %copy-start.44 = (f32[64,64]{1,0:T(8,128)}, f32[64,64]{1,0:T(8,128)S(1)}, u32[]{:S(2)}) copy-start(f32[64,64]{1,0:T(8,128)S(1)} %fusion.200) | copy-start | bytes 49156
  763.5 17.6 all-to-all-start.4
  767.8 682.9 %reduce-scatter.9.cloned.1.call-start = ((), (), s32[]{:S(2)}) async-start(), calls=%async_computation.19 | async-start | bytes 9437184 | tf_op jit(solution)/shard_map/reduce_scatter | solution.py:100
  802.8 127.3 %copy-start.30 = (f32[256,2048]{1,0:T(8,128)}, f32[256,2048]{1,0:T(8,128)S(1)}, u32[]{:S(2)}) copy-start(f32[256,2048]{1,0:T(8,128)S(1)} %get-tuple-element.707) | copy-start | bytes 6291460
  955.6 22.0 copy-start.3
  961.4 489.3 %reduce-scatter.11.cloned.1.call-start = ((), (), s32[]{:S(2)}) async-start(), calls=%async_computation.20 | async-start | bytes 25952256 | tf_op jit(solution)/shard_map/reduce_scatter | solution.py:100
  998.2 18.0 all-to-all-start.5
  1026.0 241.0 %copy-start.8 = (f32[16,1,4,1,64,64]{4,5,3,2,1,0:T(8,128)S(1)}, f32[16,1,4,1,64,64]{4,5,3,2,1,0:T(8,128)}, u32[]{:S(2)}) copy-start(f32[16,1,4,1,64,64]{4,5,3,2,1,0:T(8,128)} %copy-done.7) | copy-start | bytes 3145732
  1272.9 12.3 copy-start.6
  1290.9 17.8 all-to-all-start.7
  1298.2 14.8 copy-start.59
  1308.8 20.7 all-to-all-start.8
  1329.5 20.7 all-to-all-start.6
  1333.8 320.7 %reduce-scatter.7.cloned.1.call-start = ((), (), s32[]{:S(2)}) async-start(), calls=%async_computation.18 | async-start | bytes 28311552 | tf_op jit(solution)/shard_map/reduce_scatter | solution.py:100
  1350.2 11.9 slice-start
  1362.0 10.7 copy-start.51
  1362.1 10.7 copy-start.53
  1362.1 10.6 copy-start.55
  1362.1 10.6 copy-start.57
  1386.5 6.0 collective-permute-start.1
  1394.1 14.0 copy-start.26
  1408.2 690.8 %reduce-scatter.13.cloned.1.call-start = ((), (), s32[]{:S(2)}) async-start(), calls=%async_computation.21 | async-start | bytes 51904512
  1431.0 17.0 copy-start.69
  1431.0 17.0 copy-start.28
  1431.0 798.7 %all-reduce.20.cloned.1.call-start = ((), (), s32[]{:S(2)}) async-start(), calls=%async_computation.22 | async-start | bytes 524288 | tf_op jit(solution)/shard_map/psum | solution.py:244
  1433.0 16.8 copy-start.64
  1433.0 16.8 copy-start.65
  1433.0 16.8 copy-start.66
  1433.0 16.8 copy-start.67
  1450.6 1028.4 %all-reduce.22.cloned.1.call-start = ((), (), s32[]{:S(2)}) async-start(), calls=%async_computation.23 | async-start | bytes 25690112 | tf_op jit(solution)/shard_map/psum | solution.py:106
  2099.7 12.6 copy-start.49
  2114.1 14.4 copy-start.78
  2114.1 53.9 %copy-start.75 = (f32[256]{0:T(256)S(1)}, f32[256]{0:T(256)}, u32[]{:S(2)}) copy-start(f32[256]{0:T(256)} %copy-done.74) | copy-start | bytes 3076
  2114.1 53.9 %copy-start.4 = (f32[256,2048]{1,0:T(8,128)S(1)}, f32[256,2048]{1,0:T(8,128)}, u32[]{:S(2)}) copy-start(f32[256,2048]{1,0:T(8,128)} %copy-done.3) | copy-start | bytes 6291460
  (59 other events, 213.4 us)
Sparse Core Ops, SparseCore 0:
  9.7 223.4 all-gather.6
  234.8 80.2 all-gather.8
  316.8 391.8 all-gather.10
  710.2 201.0 all-gather.12
  961.6 87.7 reduce-scatter.8
  1051.6 225.7 reduce-scatter.10
  1408.3 246.1 reduce-scatter.6
  1656.9 442.0 reduce-scatter.12
  2106.2 123.5 all-reduce.19
  2234.1 244.9 all-reduce.21
where the time goes:
time: 2520 us; the launch traced here: 2500 us
  waiting for transfers between devices  1260 us (50%)
  matrix products  547 us (22%)
  other arithmetic  419 us (17%)
  blocking collectives  119 us (5%)
  local copies, waits for them, and re-layouts  102 us (4%)
  starting transfers between devices  41.1 us (2%)
    unnamed x11, waiting for transfers between devices  447 us
    another operation x5, other arithmetic, delta_rule(): lax.linalg.triangular_solve(system, targets, left_side=True, lower=True,...  318 us
    psum x1, waiting for transfers between devices, reduce_rows(): return lax.psum(summed, 'seq').astype(jnp.float32)  247 us
    reduce_scatter x3, waiting for transfers between devices, reduce_rows(): lax.psum_scatter(term(jnp.int32(0), total_rows // shards * lax.axis_size(...  204 us
    all_gather x1, waiting for transfers between devices, per_device(): lax.all_gather(w_qkv, 'fsdp', axis=0, tiled=True)  153 us
    dot_general x48, matrix products, advance(): result = jnp.einsum('shcd,shde->shce', query_part, state, precision=HIGH)  92.6 us
    dot_general x48, matrix products, advance(): jnp.einsum('shcd,shce->shde', key_raw, fresh, precision=HIGH)  90.1 us
    all_gather x1, waiting for transfers between devices, per_device(): down_full = lax.all_gather(w_down, 'fsdp', axis=0, tiled=True)  84.3 us
  transfers between devices with their start and end apart: 21, of which 14 were waited for; matrix products, arithmetic and copies ran while one was open for 39% of the time, Pallas kernels for 0%

commit v1 on v0

v1 whole, which is shorter than its diff:
```python
import functools

import jax
import jax.numpy as jnp
from jax import lax
from jax.experimental import pallas as pl
from jax.experimental.pallas import tpu as pltpu
from jax.sharding import PartitionSpec as P

H = 16
DK = 128
EPS = 1e-06
CHUNK = 128
HEAD_ROOM = 8


def dotf(left, right, dims):
    return lax.dot_general(left, right, (dims, ((), ())), preferred_element_type=jnp.float32)


NN = ((1,), (0,))
NT = ((1,), (1,))
TN = ((0,), (0,))


def low(value):
    return value.astype(jnp.bfloat16)


def square_iota(axis):
    return lax.broadcasted_iota(jnp.int32, (CHUNK, CHUNK), axis)


def sigmoid(value):
    return 1.0 / (1.0 + jnp.exp(-value))


def conv_chunk(window, taps, count):
    mixed = window[HEAD_ROOM:] * taps[count - 1]
    for back in range(1, count):
        mixed = mixed + pltpu.roll(window, back, 0)[HEAD_ROOM:] * taps[count - 1 - back]
    return mixed


def window_of(proj_ref, chunk, column):
    lanes = pl.ds(column, DK)
    start = pl.multiple_of(chunk * CHUNK, CHUNK)
    ahead = pl.multiple_of(jnp.maximum(start - 16, 0), 16)
    before = proj_ref[pl.ds(ahead, 16), lanes].astype(jnp.float32)[8:]
    before = jnp.where(chunk > 0, before, 0.0)
    return jnp.concatenate(
        [before, proj_ref[pl.ds(start, CHUNK), lanes].astype(jnp.float32)], axis=0
    )


def head_inputs(proj_ref, table_ref, chunk, head, heads, taps):
    wide = heads * DK
    found = []
    for part in range(3):
        window = window_of(proj_ref, chunk, part * wide + head * DK)
        weights = [
            table_ref[pl.ds(part * taps + tap, 1), pl.ds(head * DK, DK)] for tap in range(taps)
        ]
        mixed = conv_chunk(window, weights, taps)
        gate = sigmoid(mixed)
        found.append((window, weights, mixed, gate, mixed * gate))
    active_key = found[1][4]
    scale = lax.rsqrt(jnp.sum(active_key * active_key, axis=-1, keepdims=True) + EPS)
    key = active_key * scale
    return found, found[0][4] * DK**-0.5, key, scale, found[2][4]


def inverse_of(strict):
    row, column = square_iota(0), square_iota(1)
    eye = (row == column).astype(jnp.float32)
    solved = eye - jnp.where(row // 2 == column // 2, strict, 0.0)
    half = 2
    while half < CHUNK:
        below = (row // (2 * half) == column // (2 * half)) & (row // half != column // half)
        off = low(jnp.where(below, strict, 0.0))
        known = low(solved)
        solved = solved - dotf(low(dotf(known, off, NN)), known, NN)
        half *= 2
    return solved


def forward_kernel(
    heads, taps, proj_ref, logit_ref, table_ref, gain_ref,
    normed_ref, raw_ref, fresh_ref, solve_ref, state_ref, carry,
):
    length = proj_ref.shape[0]
    carry[...] = jnp.zeros_like(carry)

    def step(chunk, _):
        start = pl.multiple_of(chunk * CHUNK, CHUNK)
        here = pl.ds(start, CHUNK)
        row, column = square_iota(0), square_iota(1)
        beta_all = low(sigmoid(logit_ref[here, :])).astype(jnp.float32)
        for head in range(heads):
            lanes = pl.ds(head * DK, DK)
            _, query, key, _, value = head_inputs(proj_ref, table_ref, chunk, head, heads, taps)
            query, key, value = low(query), low(key), low(value).astype(jnp.float32)
            beta = beta_all[:, head : head + 1]
            strict = jnp.where(row > column, dotf(key, key, NT) * beta, 0.0)
            solved = low(inverse_of(strict))
            within = low(jnp.where(row >= column, dotf(query, key, NT), 0.0))
            state = carry[head]
            state_low = low(state)
            rest = value - dotf(key, state_low, NN)
            fresh = low(dotf(solved, low(beta * rest), NN))
            raw = low(dotf(query, state_low, NN) + dotf(within, fresh, NN))
            carry[head] = state + dotf(key, fresh, TN)
            wide_raw = raw.astype(jnp.float32)
            normed = wide_raw * lax.rsqrt(
                jnp.mean(wide_raw * wide_raw, axis=-1, keepdims=True) + EPS
            )
            normed_ref[here, lanes] = low(normed * gain_ref[...])
            raw_ref[here, lanes] = raw
            fresh_ref[here, lanes] = fresh
            solve_ref[chunk, head] = solved
            state_ref[chunk, head] = state_low
        return 0

    lax.fori_loop(0, length // CHUNK, step, 0)


def backward_kernel(
    heads, taps, proj_ref, logit_ref, table_ref, gain_ref, raw_ref, fresh_ref, solve_ref,
    state_ref, grad_ref, gproj_ref, gtable_ref, ggain_ref, carry, after,
):
    length = proj_ref.shape[0]
    count = length // CHUNK
    wide = heads * DK
    carry[...] = jnp.zeros_like(carry)
    after[...] = jnp.zeros_like(after)
    gtable_ref[...] = jnp.zeros_like(gtable_ref)
    ggain_ref[...] = jnp.zeros_like(ggain_ref)

    def step(index, _):
        chunk = count - 1 - index
        start = pl.multiple_of(chunk * CHUNK, CHUNK)
        here = pl.ds(start, CHUNK)
        row, column = square_iota(0), square_iota(1)
        beta_wide = sigmoid(logit_ref[here, :])
        beta_all = low(beta_wide).astype(jnp.float32)
        lane = lax.broadcasted_iota(jnp.int32, (CHUNK, DK), 1)
        glogit = jnp.zeros((CHUNK, DK), jnp.float32)
        for head in range(heads):
            lanes = pl.ds(head * DK, DK)
            found, query_wide, key_wide, scale, value_wide = head_inputs(
                proj_ref, table_ref, chunk, head, heads, taps
            )
            query, key, value = low(query_wide), low(key_wide), low(value_wide)
            beta = beta_all[:, head : head + 1]
            raw = raw_ref[here, lanes].astype(jnp.float32)
            grad_normed = grad_ref[here, lanes].astype(jnp.float32)
            r = lax.rsqrt(jnp.mean(raw * raw, axis=-1, keepdims=True) + EPS)
            scaled = grad_normed * gain_ref[...]
            grad_out = low(
                r * (scaled - raw * (r * r) * jnp.mean(scaled * raw, axis=-1, keepdims=True))
            )
            ggain_ref[...] += jnp.sum(grad_normed * raw * r, axis=0, keepdims=True)

            state, solved, fresh = state_ref[chunk, head], solve_ref[chunk, head], fresh_ref[here, lanes]
            later = carry[head]
            later_low = low(later)
            gram = dotf(key, key, NT)
            within = low(jnp.where(row >= column, dotf(query, key, NT), 0.0))
            grad_fresh = dotf(within, grad_out, TN) + dotf(key, later_low, NN)
            grad_solved = dotf(solved, low(grad_fresh), TN)
            grad_value = beta * grad_solved
            grad_rest = low(grad_value)
            carry[head] = later + dotf(query, grad_out, TN) - dotf(key, grad_rest, TN)
            rest = value.astype(jnp.float32) - dotf(key, state, NN)
            grad_within = low(jnp.where(row >= column, dotf(grad_out, fresh, NT), 0.0))
            grad_strict = jnp.where(row > column, -dotf(low(grad_solved), fresh, NT), 0.0)
            grad_beta = jnp.sum(grad_solved * rest, axis=-1, keepdims=True) + jnp.sum(
                grad_strict * gram, axis=-1, keepdims=True
            )
            mixing = low(beta * grad_strict)
            grad_query = dotf(grad_out, state, NT) + dotf(grad_within, key, NN)
            grad_key = (
                dotf(grad_within, query, TN)
                + dotf(fresh, later_low, NT)
                - dotf(grad_rest, state, NT)
                + dotf(mixing, key, NN)
                + dotf(mixing, key, TN)
            )
            bw = beta_wide[:, head : head + 1]
            grad_beta = low(grad_beta).astype(jnp.float32) * bw * (1.0 - bw)
            glogit = glogit + jnp.where(lane == head, grad_beta, 0.0)

            grad_query = low(grad_query).astype(jnp.float32) * DK**-0.5
            grad_key = low(grad_key).astype(jnp.float32)
            grad_key = scale * (
                grad_key - key_wide * jnp.sum(grad_key * key_wide, axis=-1, keepdims=True)
            )
            grad_value = low(grad_value).astype(jnp.float32)
            for part, grad_active in enumerate((grad_query, grad_key, grad_value)):
                window, weights, mixed, gate, _ = found[part]
                grad_conv = grad_active * (gate * (1.0 + mixed * (1.0 - gate)))
                columns = pl.ds(part * wide + head * DK, DK)
                tail = jnp.concatenate([grad_conv, after[:, columns]], axis=0)
                size = CHUNK + HEAD_ROOM
                total = grad_conv * weights[taps - 1]
                for back in range(1, taps):
                    total = total + pltpu.roll(tail, size - back, 0)[:CHUNK] * weights[taps - 1 - back]
                gproj_ref[here, columns] = low(total)
                after[:, columns] = grad_conv[:HEAD_ROOM]
                for back in range(taps):
                    shifted = pltpu.roll(window, back, 0)[HEAD_ROOM:] if back else window[HEAD_ROOM:]
                    spot = pl.ds(part * taps + taps - 1 - back, 1)
                    gtable_ref[spot, lanes] += jnp.sum(grad_conv * shifted, axis=0, keepdims=True)
        gproj_ref[here, pl.ds(3 * wide, DK)] = low(glogit)
        return 0

    lax.fori_loop(0, count, step, 0)


def in_vmem(count):
    return [pl.BlockSpec(memory_space=pltpu.VMEM)] * count


def mix_forward(proj, logits, table, gain):
    length = proj.shape[0]
    heads = table.shape[1] // DK
    taps = table.shape[0] // 3
    count = length // CHUNK
    wide = heads * DK
    shape = jax.ShapeDtypeStruct
    return pl.pallas_call(
        functools.partial(forward_kernel, heads, taps),
        out_shape=(
            shape((length, wide), jnp.bfloat16),
            shape((length, wide), jnp.bfloat16),
            shape((length, wide), jnp.bfloat16),
            shape((count, heads, CHUNK, CHUNK), jnp.bfloat16),
            shape((count, heads, DK, DK), jnp.bfloat16),
        ),
        in_specs=in_vmem(4),
        out_specs=tuple(in_vmem(5)),
        scratch_shapes=[pltpu.VMEM((heads, DK, DK), jnp.float32)],
        compiler_params=pltpu.CompilerParams(vmem_limit_bytes=40 * 2**20),
        cost_estimate=pl.CostEstimate(
            flops=length * heads * DK * 8000, bytes_accessed=16 * length * wide, transcendentals=3 * length * wide
        ),
        name="mix_forward",
    )(proj, logits, table, gain)


def mix_backward(proj, logits, table, gain, raw, fresh, solved, states, grad):
    length = proj.shape[0]
    heads = table.shape[1] // DK
    taps = table.shape[0] // 3
    wide = heads * DK
    shape = jax.ShapeDtypeStruct
    return pl.pallas_call(
        functools.partial(backward_kernel, heads, taps),
        out_shape=(
            shape((length, 3 * wide + DK), jnp.bfloat16),
            shape((3 * taps, wide), jnp.float32),
            shape((1, DK), jnp.float32),
        ),
        in_specs=in_vmem(9),
        out_specs=tuple(in_vmem(3)),
        scratch_shapes=[
            pltpu.VMEM((heads, DK, DK), jnp.float32),
            pltpu.VMEM((HEAD_ROOM, 3 * wide), jnp.float32),
        ],
        compiler_params=pltpu.CompilerParams(vmem_limit_bytes=40 * 2**20),
        cost_estimate=pl.CostEstimate(
            flops=length * heads * DK * 10000, bytes_accessed=26 * length * wide, transcendentals=3 * length * wide
        ),
        name="mix_backward",
    )(proj, logits, table, gain, raw, fresh, solved, states, grad)


def neighbours():
    me = lax.axis_index("seq")
    return me, me + 1 - 2 * (me % 2), me + 2 - 4 * (me // 2), 3 - me


def greet(across, along):
    barrier = pltpu.get_barrier_semaphore()
    for other in (across, along):
        pl.semaphore_signal(
            barrier, inc=1, device_id={"seq": other}, device_id_type=pl.DeviceIdType.MESH
        )
    pl.semaphore_wait(barrier, 2)


def remote(source, target, send, arrive, slot, other):
    return pltpu.make_async_remote_copy(
        src_ref=source,
        dst_ref=target,
        send_sem=send.at[slot],
        recv_sem=arrive.at[slot],
        device_id={"seq": other},
        device_id_type=pl.DeviceIdType.MESH,
    )


def half_of(rows):
    return (rows // 2 + 15) // 16 * 16


def gather_start(source, target, near, send, arrive, keep):
    me, across, along, _ = near
    own = pltpu.make_async_copy(source, target.at[me], keep)
    first = remote(source, target.at[me], send, arrive, 0, across)
    second = remote(source, target.at[me], send, arrive, 1, along)
    own.start()
    first.start()
    second.start()
    return own, first, second


def gather_finish(started, target, near, send, arrive):
    _, across, along, _ = near
    own, first, second = started
    rows = target.shape[1]
    split = half_of(rows)
    head, rest = pl.ds(0, split), pl.ds(split, rows - split)
    first.wait_recv()
    third = remote(target.at[across, head], target.at[across, head], send, arrive, 2, along)
    third.start()
    second.wait_recv()
    fourth = remote(target.at[along, rest], target.at[along, rest], send, arrive, 3, across)
    fourth.start()
    third.wait_recv()
    fourth.wait_recv()
    for copy in (first, second, third, fourth):
        copy.wait_send()
    own.wait()


def gather_kernel(count, *refs):
    sources, targets = refs[:count], refs[count : 2 * count]
    send, arrive, keep = refs[2 * count :]
    near = neighbours()
    greet(near[1], near[2])
    started = [
        gather_start(sources[i], targets[i], near, send.at[i], arrive.at[i], keep.at[i])
        for i in range(count)
    ]
    for i in range(count):
        gather_finish(started[i], targets[i], near, send.at[i], arrive.at[i])


def seq_gather(name, number, *blocks):
    count = len(blocks)
    side = lax.axis_size("seq")
    if side != 4:
        return [lax.all_gather(block, "seq", axis=0) for block in blocks]
    moved = sum(block.size for block in blocks)
    return pl.pallas_call(
        functools.partial(gather_kernel, count),
        out_shape=[
            jax.ShapeDtypeStruct((side,) + block.shape, block.dtype) for block in blocks
        ],
        in_specs=[pl.BlockSpec(memory_space=pl.ANY)] * count,
        out_specs=[pl.BlockSpec(memory_space=pl.ANY)] * count,
        scratch_shapes=[
            pltpu.SemaphoreType.DMA((count, 4)),
            pltpu.SemaphoreType.DMA((count, 4)),
            pltpu.SemaphoreType.DMA((count,)),
        ],
        compiler_params=pltpu.CompilerParams(collective_id=number, has_side_effects=True),
        cost_estimate=pl.CostEstimate(flops=0, bytes_accessed=160 * moved, transcendentals=0),
        name=name,
    )(*blocks)


TILE = 256
STEP = 16


def reduce_rows_kernel(flip, gathers, epilogue, in_count, out_count, *refs):
    left_ref, right_ref, *extra = refs[:in_count]
    outs = refs[in_count : in_count + out_count]
    far, wide_x, wide_y, own, get_a, get_b, get_x, get_y, send, arrive = refs[
        in_count + out_count : in_count + out_count + 10
    ]
    rest_refs = refs[in_count + out_count + 10 :]
    near = neighbours()
    me, across, along, opposite = near
    greet(across, along)
    rows, width = own.shape
    split = half_of(rows)
    head, rest = pl.ds(0, split), pl.ds(split, rows - split)

    def part(block, store):
        here = pl.ds(pl.multiple_of(block * rows, rows), rows)

        @pl.loop(0, width // TILE)
        def _(tile):
            columns = pl.ds(pl.multiple_of(tile * TILE, TILE), TILE)
            if flip:
                value = dotf(left_ref[here, :], right_ref[columns, :], NT)
            else:
                value = dotf(left_ref[here, :], right_ref[:, columns], NN)
            store[:, columns] = value.astype(store.dtype)

    def add_into(store, base, source):
        @pl.loop(0, source.shape[0] // STEP)
        def _(index):
            start = pl.multiple_of(index * STEP, STEP)
            there = pl.ds(pl.multiple_of(base + start, STEP), STEP)
            total = store[there, :].astype(jnp.float32) + source[pl.ds(start, STEP), :].astype(
                jnp.float32
            )
            store[there, :] = low(total)

    part(opposite, far)
    copies = [
        remote(far.at[head], get_a, send, arrive, 0, across),
        remote(far.at[rest], get_b, send, arrive, 1, along),
    ]
    copies[0].start()
    copies[1].start()
    part(across, wide_x)
    copies.append(remote(wide_x.at[head], get_x.at[head], send, arrive, 2, across))
    copies[2].start()
    part(along, wide_y)
    copies.append(remote(wide_y.at[rest], get_y.at[rest], send, arrive, 3, along))
    copies[3].start()
    copies[0].wait_recv()
    add_into(wide_y, 0, get_a)
    copies.append(remote(wide_y.at[head], get_y.at[head], send, arrive, 4, along))
    copies[4].start()
    copies[1].wait_recv()
    add_into(wide_x, split, get_b)
    copies.append(remote(wide_x.at[rest], get_x.at[rest], send, arrive, 5, across))
    copies[5].start()
    part(me, own)
    for copy in copies[2:]:
        copy.wait_recv()
    epilogue_prepare = rest_refs[0] if gathers else None

    @pl.loop(0, rows // STEP)
    def _(index):
        here = pl.ds(pl.multiple_of(index * STEP, STEP), STEP)
        total = (
            own[here, :] + get_x[here, :].astype(jnp.float32) + get_y[here, :].astype(jnp.float32)
        )
        epilogue(index, here, total, extra, outs, epilogue_prepare)

    for copy in copies:
        copy.wait_send()
    if gathers:
        block, send_2, arrive_2, keep = rest_refs
        target = outs[0]
        started = gather_start(block, target, near, send_2, arrive_2, keep.at[0])
        gather_finish(started, target, near, send_2, arrive_2)


def rms_back(grad, values, gain):
    r = lax.rsqrt(jnp.mean(values * values, axis=-1, keepdims=True) + EPS)
    scaled = grad * gain
    change = r * (scaled - values * (r * r) * jnp.mean(scaled * values, axis=-1, keepdims=True))
    return change, jnp.sum(grad * values * r, axis=0, keepdims=True)


def middle_epilogue(index, here, total, extra, outs, block):
    source_ref, gain_ref = extra
    middle = source_ref[here, :].astype(jnp.float32) + total
    outs[1][here, :] = middle
    r = lax.rsqrt(jnp.mean(middle * middle, axis=-1, keepdims=True) + EPS)
    block[here, :] = low(middle * r * gain_ref[...])


def output_epilogue(index, here, total, extra, outs, block):
    outs[0][here, :] = low(extra[0][here, :] + total)


def branch_epilogue(index, here, total, extra, outs, block):
    middle_ref, upstream_ref, gain_ref = extra
    change, gain_part = rms_back(total, middle_ref[here, :], gain_ref[...])
    grad = upstream_ref[here, :].astype(jnp.float32) + change
    outs[1][here, :] = grad
    block[here, :] = low(grad)
    outs[2][...] = jnp.where(index > 0, outs[2][...], 0.0) + gain_part


def input_epilogue(index, here, total, extra, outs, block):
    source_ref, carried_ref, gain_ref = extra
    change, gain_part = rms_back(total, source_ref[here, :].astype(jnp.float32), gain_ref[...])
    outs[0][here, :] = carried_ref[here, :] + change
    outs[1][...] = jnp.where(index > 0, outs[1][...], 0.0) + gain_part


def fused_reduce(name, number, flip, gathers, epilogue, outs, left, right, *extra):
    side = lax.axis_size("seq")
    length = left.shape[0]
    rows = length // side
    width = right.shape[0] if flip else right.shape[1]
    split = half_of(rows)
    scratch = [
        pltpu.VMEM((rows, width), jnp.bfloat16),
        pltpu.VMEM((rows, width), jnp.bfloat16),
        pltpu.VMEM((rows, width), jnp.bfloat16),
        pltpu.VMEM((rows, width), jnp.float32),
        pltpu.VMEM((split, width), jnp.bfloat16),
        pltpu.VMEM((rows - split, width), jnp.bfloat16),
        pltpu.VMEM((rows, width), jnp.bfloat16),
        pltpu.VMEM((rows, width), jnp.bfloat16),
        pltpu.SemaphoreType.DMA((6,)),
        pltpu.SemaphoreType.DMA((6,)),
    ]
    out_specs = in_vmem(len(outs))
    if gathers:
        scratch += [
            pltpu.VMEM((rows, width), jnp.bfloat16),
            pltpu.SemaphoreType.DMA((4,)),
            pltpu.SemaphoreType.DMA((4,)),
            pltpu.SemaphoreType.DMA((1,)),
        ]
        out_specs[0] = pl.BlockSpec(memory_space=pl.ANY)
    return pl.pallas_call(
        functools.partial(
            reduce_rows_kernel, flip, gathers, epilogue, 2 + len(extra), len(outs)
        ),
        out_shape=outs,
        in_specs=in_vmem(2 + len(extra)),
        out_specs=out_specs,
        scratch_shapes=scratch,
        compiler_params=pltpu.CompilerParams(
            collective_id=number, has_side_effects=True, vmem_limit_bytes=50 * 2**20
        ),
        cost_estimate=pl.CostEstimate(
            flops=2 * left.size * width,
            bytes_accessed=(320 if gathers else 160) * rows * width,
            transcendentals=0,
        ),
        name=name,
    )(left, right, *extra)


def seq_sum(partial, side):
    block = low(partial).reshape(side, -1, partial.shape[-1])
    return lax.psum_scatter(block, "seq", scatter_dimension=0).astype(jnp.float32)


def out_and_norm(attn_in, weight, source, gain):
    side = lax.axis_size("seq")
    rows, width = source.shape
    if side != 4:
        middle = source.astype(jnp.float32) + seq_sum(dotf(attn_in, weight, NN), side)
        r = lax.rsqrt(jnp.mean(middle * middle, axis=-1, keepdims=True) + EPS)
        return lax.all_gather(low(middle * r * gain), "seq", axis=0), middle
    outs = (
        jax.ShapeDtypeStruct((side, rows, width), jnp.bfloat16),
        jax.ShapeDtypeStruct((rows, width), jnp.float32),
    )
    return fused_reduce(
        "out_and_norm", 2, False, True, middle_epilogue, outs, attn_in, weight, source, gain
    )


def down_and_add(hidden, weight, middle):
    side = lax.axis_size("seq")
    if side != 4:
        return low(middle + seq_sum(dotf(hidden, weight, NN), side))
    outs = (jax.ShapeDtypeStruct(middle.shape, jnp.bfloat16),)
    return fused_reduce(
        "down_and_add", 3, False, False, output_epilogue, outs, hidden, weight, middle
    )[0]


def branch_grad(grad, weight, middle, upstream, gain):
    side = lax.axis_size("seq")
    rows, width = middle.shape
    if side != 4:
        change, gain_part = rms_back(seq_sum(dotf(grad, weight, NT), side), middle, gain)
        total = upstream.astype(jnp.float32) + change
        return lax.all_gather(low(total), "seq", axis=0), total, gain_part
    outs = (
        jax.ShapeDtypeStruct((side, rows, width), jnp.bfloat16),
        jax.ShapeDtypeStruct((rows, width), jnp.float32),
        jax.ShapeDtypeStruct((1, width), jnp.float32),
    )
    return fused_reduce(
        "branch_grad", 4, True, True, branch_epilogue, outs, grad, weight, middle, upstream, gain
    )


def input_grad(grad, weight, source, carried, gain):
    side = lax.axis_size("seq")
    if side != 4:
        change, gain_part = rms_back(
            seq_sum(dotf(grad, weight, NT), side), source.astype(jnp.float32), gain
        )
        return carried + change, gain_part
    outs = (
        jax.ShapeDtypeStruct(carried.shape, jnp.float32),
        jax.ShapeDtypeStruct(gain.shape, jnp.float32),
    )
    return fused_reduce(
        "input_grad", 5, True, False, input_epilogue, outs, grad, weight, source, carried, gain
    )


def pick_kernel(side, share, source_ref, target_ref):
    me = lax.axis_index("seq")
    count = target_ref.shape[1] // share
    for index in range(side):

        @pl.when(me == index)
        def _():
            pieces = [
                source_ref[:, pl.ds((k * side + index) * share, share)].astype(jnp.float32)
                for k in range(count)
            ]
            target_ref[...] = low(jnp.concatenate(pieces, axis=1))


def pick_columns(weight, share):
    side = lax.axis_size("seq")
    rows, width = weight.shape
    tile = 32
    return pl.pallas_call(
        functools.partial(pick_kernel, side, share),
        grid=(rows // tile,),
        out_shape=jax.ShapeDtypeStruct((rows, width // side), weight.dtype),
        in_specs=[pl.BlockSpec((tile, width), lambda i: (i, 0))],
        out_specs=pl.BlockSpec((tile, width // side), lambda i: (i, 0)),
        name="pick_columns",
    )(weight)


def spread_kernel(side, share, source_ref, target_ref):
    count = source_ref.shape[2] // share
    pieces = [
        source_ref[index, :, pl.ds(k * share, share)].astype(jnp.float32)
        for k in range(count)
        for index in range(side)
    ]
    target_ref[...] = jnp.concatenate(pieces, axis=1)


def spread_columns(parts, share):
    side, rows, width = parts.shape
    tile = 32
    return pl.pallas_call(
        functools.partial(spread_kernel, side, share),
        grid=(rows // tile,),
        out_shape=jax.ShapeDtypeStruct((rows, width * side), jnp.float32),
        in_specs=[pl.BlockSpec((side, tile, width), lambda i: (0, i, 0))],
        out_specs=pl.BlockSpec((tile, width * side), lambda i: (i, 0)),
        name="spread_columns",
    )(parts)


def fsdp_sum(term):
    return lax.psum_scatter(low(term), "fsdp", scatter_dimension=0, tiled=True)


def per_device(
    inputs,
    cotangent,
    norm1_gain,
    w_qkv,
    w_beta,
    conv_weight,
    out_gain,
    w_out,
    norm2_gain,
    w_gate_up,
    w_down,
):
    side = lax.axis_size("seq")
    s = lax.axis_index("seq")
    f = lax.axis_index("fsdp")
    shape = inputs.shape
    width = shape[2]
    source = inputs.reshape(-1, width)
    upstream = cotangent.reshape(-1, width)
    length = source.shape[0] * side
    heads = H // side
    wide = heads * DK
    rows = w_qkv.shape[0]
    share = w_down.shape[0] // side
    taps = conv_weight.shape[1] // 3

    def everywhere(block):
        return lax.all_gather(block, "fsdp", axis=0, tiled=True)

    qkv_part = lax.dynamic_slice_in_dim(w_qkv.reshape(rows, 3, width), s * wide, wide, 2)
    beta_part = lax.dynamic_slice_in_dim(w_beta, s * heads, heads, 1)
    qkv_part = everywhere(
        jnp.concatenate(
            [qkv_part.reshape(rows, 3 * wide), jnp.pad(beta_part, ((0, 0), (0, DK - heads)))],
            axis=1,
        )
    )
    small = jnp.concatenate([norm1_gain[None], norm2_gain[None], conv_weight.T], axis=0)
    small = lax.all_gather(small, "fsdp", axis=0)
    small = small.transpose(1, 0, 2).reshape(small.shape[1], width).astype(jnp.float32)
    gain_first = small[0:1]
    gain_second = small[1:2]
    table = lax.dynamic_slice_in_dim(small[2:], s * wide, wide, 1)
    gain_heads = out_gain.astype(jnp.float32)[None]

    out_part = everywhere(lax.dynamic_slice_in_dim(w_out, s * wide, wide, 1))
    out_part = lax.all_to_all(out_part, "seq", split_axis=0, concat_axis=1, tiled=True)
    gate_up_part = everywhere(pick_columns(w_gate_up, share))
    down_part = everywhere(lax.dynamic_slice_in_dim(w_down, s * share, share, 0))

    source_all, upstream_all = seq_gather("gather_tokens", 1, source, upstream)
    source_all = source_all.reshape(length, width).astype(jnp.float32)
    upstream_all = upstream_all.reshape(length, width)
    normed_first = low(
        source_all
        * lax.rsqrt(jnp.mean(source_all * source_all, axis=-1, keepdims=True) + EPS)
        * gain_first
    )
    projected = low(dotf(normed_first, qkv_part[:, : 3 * wide], NN))
    beta_logits = dotf(normed_first, qkv_part[:, 3 * wide :], NN)
    attn_in, *kept = mix_forward(projected, beta_logits, table, gain_heads)
    ffn_in, middle = out_and_norm(attn_in, out_part, source, gain_second)
    ffn_in = ffn_in.reshape(length, width)
    gate_up = dotf(ffn_in, gate_up_part, NN)
    hidden_width = gate_up.shape[1] // 2
    gate = gate_up[:, :hidden_width]
    upward = gate_up[:, hidden_width:]
    sigma = jax.nn.sigmoid(gate)
    hidden = low(gate * sigma * upward)

    grad_down = fsdp_sum(dotf(hidden, upstream_all, TN))
    grad_hidden = dotf(upstream_all, down_part, NT)
    grad_gate = grad_hidden * upward * sigma * (1.0 + gate * (1.0 - sigma))
    grad_up = grad_hidden * gate * sigma
    grad_gate_up = low(jnp.concatenate([grad_gate, grad_up], axis=1))
    grad_w_gate_up = fsdp_sum(dotf(ffn_in, grad_gate_up, TN))
    grad_branch, grad_middle, grad_gain_second = branch_grad(
        grad_gate_up, gate_up_part, middle, upstream, gain_second
    )
    grad_branch = grad_branch.reshape(length, width)
    output = down_and_add(hidden, down_part, middle)

    grad_w_out = low(dotf(attn_in, grad_branch, TN))
    grad_w_out = lax.all_to_all(grad_w_out, "seq", split_axis=1, concat_axis=0, tiled=True)
    grad_w_out = fsdp_sum(grad_w_out)
    grad_proj, grad_table, grad_gain_heads = mix_backward(
        projected, beta_logits, table, gain_heads, *kept, dotf(grad_branch, out_part, NT)
    )
    grad_qkv = low(dotf(normed_first, grad_proj, TN))
    grad_qkv = lax.dynamic_update_slice(
        grad_qkv, low(grad_table.T), (s * wide, 3 * wide + heads)
    )
    grad_qkv = fsdp_sum(grad_qkv)
    grad_input, grad_gain_first = input_grad(
        grad_proj, qkv_part, source, grad_middle, gain_first
    )
    gains = jnp.concatenate(
        [grad_gain_first, grad_gain_second, jnp.pad(grad_gain_heads, ((0, 0), (0, width - DK)))]
    )
    summed = lax.psum(gains, ("fsdp", "seq"))
    own = lax.dynamic_slice_in_dim(summed, f * rows, rows, 1)

    (grad_down,) = seq_gather("gather_down", 6, grad_down)
    (grad_w_gate_up,) = seq_gather("gather_gate_up", 7, grad_w_gate_up)
    (grad_w_out,) = seq_gather("gather_out", 8, grad_w_out)
    (grad_qkv,) = seq_gather("gather_qkv", 9, grad_qkv)
    grad_w_qkv = jnp.concatenate(
        [grad_qkv[i, :, j * wide : (j + 1) * wide] for j in range(3) for i in range(side)], axis=1
    )
    sides = grad_qkv[:, :, 3 * wide :].astype(jnp.float32)
    grad_w_beta = jnp.concatenate([sides[i, :, :heads] for i in range(side)], axis=1)
    grad_conv = jnp.sum(sides[:, :, heads : heads + 3 * taps], axis=0)
    return (
        output.reshape(shape),
        grad_input.reshape(shape),
        own[0],
        grad_w_qkv.astype(jnp.float32),
        grad_w_beta,
        grad_conv,
        summed[2, :DK],
        jnp.concatenate([grad_w_out[i] for i in range(side)], axis=1).astype(jnp.float32),
        own[1],
        spread_columns(grad_w_gate_up, share),
        grad_down.reshape(-1, width).astype(jnp.float32),
    )


def solution(mesh):
    by_row = P("fsdp", None)
    tokens = P("fsdp", "seq", None)
    specs = (tokens, tokens, P("fsdp"), by_row, by_row, by_row, P(), by_row, P("fsdp"))
    specs = specs + (by_row, by_row)
    return jax.shard_map(per_device, mesh=mesh, in_specs=specs, out_specs=specs, check_vma=False)
```

time: 2520 us -> 815 us (0.32)
  waiting for transfers between devices: 1260 us -> 3.31 us
  Pallas kernels: 0 us -> 533 us
  matrix products: 547 us -> 99.8 us
  other arithmetic: 419 us -> 25.6 us
  local copies, waits for them, and re-layouts: 102 us -> 47.4 us
  starting transfers between devices: 41.1 us -> 4.41 us
  blocking collectives: 119 us -> 82.4 us
    pallas_call x0 -> x13, Pallas kernels: none -> 533 us  [the longest x4 242 us: fused_reduce(): pl.pallas_call(functools.partial(reduce_rows_kernel, flip, gathers, epilo...]
    unnamed x11 -> x8, waiting for transfers between devices: 447 us -> 0.13 us
    dot_general x214 -> x9, matrix products: 533 us -> 99.8 us  [dotf(): lax.dot_general(left, right, (dims, ((), ())), preferred_element_type=jnp...]
    another operation x6 -> x0, other arithmetic: 318 us -> none  [the longest x5 318 us: delta_rule(): lax.linalg.triangular_solve(system, targets, left_side=True, lower=True,...]
    psum x2 -> x0, waiting for transfers between devices: 305 us -> none  [the longest x1 247 us: reduce_rows(): return lax.psum(summed, 'seq').astype(jnp.float32)]
    all_gather x4, waiting for transfers between devices: 238 us -> 0.04 us  [everywhere(): return lax.all_gather(block, 'fsdp', axis=0, tiled=True)]
    reduce_scatter x3 -> x4, waiting for transfers between devices: 204 us -> 0.01 us  [fsdp_sum(): return lax.psum_scatter(low(term), 'fsdp', scatter_dimension=0, tiled=True)]
    all_to_all x9 -> x1, waiting for transfers between devices: 61.2 us -> 3.13 us  [per_device(): lax.all_to_all(out_part, 'seq', split_axis=0, concat_axis=1, tiled=True)]
  transfers between devices with their start and end apart: 21 -> 9, of which waited for: 14 -> 1; matrix products, arithmetic and copies ran while one was open for 39% -> 16% of each run, Pallas kernels for 0% -> 49%
where the time goes in v1:
time: 815 us; the launch traced here: 811 us
  Pallas kernels  533 us (65%)
  matrix products  99.8 us (12%)
  blocking collectives  82.4 us (10%)
  local copies, waits for them, and re-layouts  47.4 us (6%)
  other arithmetic  25.6 us (3%)
  between operations  15.3 us (2%)
    pallas_call x4, Pallas kernels, fused_reduce(): pl.pallas_call(functools.partial(reduce_rows_kernel, flip, gathers, epilo...  242 us
    pallas_call x5, Pallas kernels, seq_gather(): pl.pallas_call(functools.partial(gather_kernel, count), out_shape=[jax.Sh...  186 us
    dot_general x9, matrix products, dotf(): lax.dot_general(left, right, (dims, ((), ())), preferred_element_type=jnp...  99.8 us
    pallas_call x1, Pallas kernels, mix_forward(): pl.pallas_call(functools.partial(forward_kernel, heads, taps), out_shape=...  59.7 us
    psum x1, blocking collectives, per_device(): summed = lax.psum(gains, ('fsdp', 'seq'))  40.8 us
    unnamed x73, local copies, waits for them, and re-layouts  30.5 us
    pallas_call x1, Pallas kernels, mix_backward(): pl.pallas_call(functools.partial(backward_kernel, heads, taps), out_shape...  29.3 us
    all_to_all x1, blocking collectives, per_device(): lax.all_to_all(grad_w_out, 'seq', split_axis=1, concat_axis=0, tiled=True)  27 us
  transfers between devices with their start and end apart: 9, of which 1 were waited for; matrix products, arithmetic and copies ran while one was open for 16% of the time, Pallas kernels for 49%

profile of v1, /device:TPU:0, one launch (start us, length us, event | category | flops | bytes accessed | tf_op | source)
XLA Modules:
  0.0 810.8 jit_solution(6935775273856143821)
XLA Ops:
  7.2 1.8 constant_dynamic-slice_fusion.2
  10.0 4.6 copy.36
  14.6 2.1 constant_dynamic-slice_fusion.5
  16.7 2.3 copy.38
  19.0 2.1 fusion.8
  21.2 6.7 pick_columns.1
  29.0 73.5 %gather_tokens.1 = (bf16[4,256,2048]{2,1,0:T(8,128)(2,1)}, bf16[4,256,2048]{2,1,0:T(8,128)(2,1)}) custom-call(bf16[256,2048]{1,0:T(8,128)(2,1)} %bitcast.109, bf16[256,2048]{1,0:T(8,128)(2,1)} %bitcast.107), custom_call_target="tpu_custom_call" | custom-call | bytes 167772160 | tf_op jit(solution)/shard_map/gather_tokens/pallas_call | solution.py:356
  102.5 3.2 multiply_reduce_fusion
  105.8 3.6 all-to-all-start
  109.5 14.7 %all-gather.1 = bf16[8,14,256]{2,1,0:T(8,128)(2,1)S(1)} all-gather(bf16[1,14,256]{2,1,0:T(8,128)(2,1)S(1)} %maximum_bitcast_fusion), channel_id=2, replica_groups=mesh['fsdp'=8,'seq'=4] {'fsdp'}, dimensions={0}, use_global_device_ids=true | all-gather | bytes 64512 | tf_op jit(solution)/shard_map/all_gather | solution.py:697
  124.4 5.4 fusion.1
  129.8 3.1 all-to-all-done
  132.9 1.6 copy.50
  134.5 3.8 fusion.9.logit_ref
  138.3 8.8 %fusion.4.proj_ref = bf16[1024,1536]{1,0:T(8,128)(2,1)S(1)} fusion(bf16[1024,2048]{1,0:T(8,128)(2,1)S(1)} %copy-done.20, bf16[2048,1664]{1,0:T(8,128)(2,1)} %all-gather.7.cloned.1.call-done.refs_1_), kind=kOutput, calls=%fused_computation.14 | convolution fusion | flops 6444023808 | bytes 13631488 | tf_op jit(solution)/shard_map/dot_general | solution.py:18
  147.1 59.7 %mix_forward.1 = (bf16[1024,512]{1,0:T(8,128)(2,1)S(1)}, bf16[1024,512]{1,0:T(8,128)(2,1)S(1)}, bf16[1024,512]{1,0:T(8,128)(2,1)S(1)}, bf16[8,4,128,128]{3,2,1,0:T(8,128)(2,1)S(1)}, bf16[8,4,128,128]{3,2,1,0:T(8,128)(2,1)S(1)}) custom-call(bf16[1024,1536]{1,0:T(8,128)(2,1)S(1)} %fusion.4.proj_ref, f32[1024,128]{1,0:T(8,128)S(1)} %fusion.9.logit_ref, ...), custom_call_target="tpu_custom_call" | custom-call | flops 4194304000 | bytes 8388608 | tf_op jit(solution)/shard_map/mix_forward/pallas_call | solution.py:231
  207.8 1.0 copy-done.14
  210.7 76.2 %out_and_norm.1 = (bf16[4,256,2048]{2,1,0:T(8,128)(2,1)}, f32[256,2048]{1,0:T(8,128)}) custom-call(bf16[1024,512]{1,0:T(8,128)(2,1)S(1)} %get-tuple-element.29.refs_0_, bf16[512,2048]{1,0:T(8,128)(2,1)} %bitcast.123, bf16[256,2048]{1,0:T(8,128)(2,1)S(1)} %bitcast.110, f32[1,2048]{1,0:T(1,128)S(1)} %bitcast.115), custom_call_target="tpu_custom_call" | custom-call | flops 2147483648 | bytes 167772160 | tf_op jit(solution)/shard_map/out_and_norm/pallas_call | solution.py:519
  287.0 18.7 %fusion.13 = f32[1024,2816]{1,0:T(8,128)} fusion(bf16[1024,2048]{1,0:T(8,128)(2,1)} %bitcast.135, bf16[2048,2816]{1,0:T(8,128)(2,1)} %all-gather.11.cloned.1.call-done.refs_1_), kind=kOutput, calls=%fused_computation.62 | convolution fusion | flops 11811160064 | bytes 27262976 | tf_op jit(solution)/shard_map/dot_general | solution.py:18
  305.6 16.4 %multiply_convert_fusion.1 = (bf16[1024,1408]{1,0:T(8,128)(2,1)S(1)}, bf16[1024,1408]{1,0:T(8,128)(2,1)S(1)}, bf16[1024,1408]{1,0:T(8,128)(2,1)}) fusion(f32[1024,2816]{1,0:T(8,128)} %fusion.13, bf16[1024,2048]{1,0:T(8,128)(2,1)} %bitcast.133, bf16[1408,2048]{1,0:T(8,128)(2,1)} %all-gather.13.cloned.1.call-done.refs_1_), kind=kOutput, calls=%fused_computation.11 | convolution fusion | flops 5928648704 | bytes 30146560 | tf_op jit(solution)/shard_map/dot_general | solution.py:18
  322.1 2.9 pad_maximum_fusion.refs_0_
  326.3 81.8 %branch_grad.1 = (bf16[4,256,2048]{2,1,0:T(8,128)(2,1)}, f32[256,2048]{1,0:T(8,128)S(1)}, f32[1,2048]{1,0:T(1,128)S(1)}) custom-call(bf16[1024,2816]{1,0:T(8,128)(2,1)} %pad_maximum_fusion.refs_0_, bf16[2048,2816]{1,0:T(8,128)(2,1)} %all-gather.11.cloned.1.call-done.refs_1_, f32[256,2048]{1,0:T(8,128)} %get-tuple-element.31.refs_2_, ...), custom_call_target="tpu_custom_call" | custom-call | flops 11811160064 | bytes 167772160 | tf_op jit(solution)/shard_map/branch_grad/pallas_call | solution.py:519
  408.2 5.4 convolution_convert_fusion.3
  413.8 27.0 %all_to_all.38 = bf16[512,4,512]{2,0,1:T(8,128)(2,1)} all-to-all(bf16[512,4,512]{2,0,1:T(8,128)(2,1)S(1)} %bitcast.119), channel_id=1, replica_groups=mesh['fsdp'=8,'seq'=4] {'seq'}, dimensions={1} | all-to-all | bytes 4194304 | tf_op jit(solution)/shard_map/all_to_all | solution.py:742
  440.8 10.4 %convolution_convert_fusion.1 = bf16[1408,2048]{1,0:T(8,128)(2,1)} fusion(bf16[1024,1408]{1,0:T(8,128)(2,1)} %get-tuple-element.80.refs_0_, bf16[1024,2048]{1,0:T(8,128)(2,1)} %bitcast.134), kind=kOutput, calls=%fused_computation.5 | convolution fusion | flops 5908463616 | bytes 12845056 | tf_op jit(solution)/shard_map/dot_general | solution.py:18
  451.6 5.4 fusion.14.grad_ref
  457.1 29.3 %mix_backward.1 = (bf16[1024,1664]{1,0:T(8,128)(2,1)S(1)}, f32[12,512]{1,0:T(8,128)S(1)}, f32[1,128]{1,0:T(1,128)S(1)}) custom-call(bf16[1024,1536]{1,0:T(8,128)(2,1)S(1)} %copy-done.10, f32[1024,128]{1,0:T(8,128)S(1)} %fusion.9.logit_ref, f32[12,512]{1,0:T(8,128)S(1)} %constant_dynamic-slice_fusion.3.table_ref, ...), custom_call_target="tpu_custom_call" | custom-call | flops 5242880000 | bytes 13631488 | tf_op jit(solution)/shard_map/mix_backward/pallas_call | solution.py:257
  486.4 1.8 copy-done.8
  488.4 12.5 %convolution_convert_fusion.2 = bf16[2048,1664]{1,0:T(8,128)(2,1)} fusion(bf16[1024,2048]{1,0:T(8,128)(2,1)} %fusion.1, bf16[1024,1664]{1,0:T(8,128)(2,1)} %copy-done.8), kind=kOutput, calls=%fused_computation.6 | convolution fusion | flops 6982729728 | bytes 14417920 | tf_op jit(solution)/shard_map/dot_general | solution.py:18
  500.8 3.3 dynamic_update_slice.3
  504.4 18.4 %convolution_convert_fusion = bf16[2048,2816]{1,0:T(8,128)(2,1)} fusion(bf16[1024,2048]{1,0:T(8,128)(2,1)} %bitcast.136, bf16[1024,1408]{1,0:T(8,128)(2,1)} %copy-done.22, bf16[1024,1408]{1,0:T(8,128)(2,1)} %copy-done.21), kind=kOutput, calls=%fused_computation | convolution fusion | flops 11828461568 | bytes 21495808 | tf_op jit(solution)/shard_map/dot_general | solution.py:18
  522.8 1.6 copy-done.7
  524.5 40.5 %down_and_add.1 = bf16[256,2048]{1,0:T(8,128)(2,1)S(1)} custom-call(bf16[1024,1408]{1,0:T(8,128)(2,1)} %get-tuple-element.80.refs_0_, bf16[1408,2048]{1,0:T(8,128)(2,1)} %all-gather.13.cloned.1.call-done.refs_1_, f32[256,2048]{1,0:T(8,128)S(1)} %copy-done.7), custom_call_target="tpu_custom_call" | custom-call | flops 5905580032 | bytes 83886080 | tf_op jit(solution)/shard_map/down_and_add/pallas_call | solution.py:519
  564.9 43.2 %input_grad.1 = (f32[256,2048]{1,0:T(8,128)S(1)}, f32[1,2048]{1,0:T(1,128)S(1)}) custom-call(bf16[1024,1664]{1,0:T(8,128)(2,1)} %copy-done.8, bf16[2048,1664]{1,0:T(8,128)(2,1)} %all-gather.7.cloned.1.call-done.refs_1_, bf16[256,2048]{1,0:T(8,128)(2,1)S(1)} %bitcast.111, f32[256,2048]{1,0:T(8,128)} %copy-done.11, f32[1,2048]{1,0:T(1,128)S(1)} %bitcast.114), custom_call_target="tpu_custom_call" | custom-call | flops 6979321856 | bytes 83886080 | tf_op jit(solution)/shard_map/input_grad/pallas_call | solution.py:519
  608.1 40.8 %psum.7 = f32[3,2048]{1,0:T(4,128)S(1)} all-reduce(f32[3,2048]{1,0:T(4,128)S(1)} %select_maximum_fusion), channel_id=1, replica_groups=mesh['fsdp'=8,'seq'=4] {'fsdp','seq'}, use_global_device_ids=true, to_apply=%region_1.2 | all-reduce | flops 6144 | bytes 49152 | tf_op jit(solution)/shard_map/psum | solution.py:758
  650.1 14.7 %gather_out.1 = bf16[4,256,512]{2,1,0:T(8,128)(2,1)} custom-call(bf16[256,512]{1,0:T(8,128)(2,1)} %reduce-scatter.7.cloned.1.call-done.refs_0_), custom_call_target="tpu_custom_call" | custom-call | bytes 20971520 | tf_op jit(solution)/shard_map/gather_out/pallas_call | solution.py:356
  664.8 1.3 slice_bitcast_fusion.3
  666.0 1.6 maximum_convert_fusion
  667.6 23.6 %gather_down.1 = bf16[4,176,2048]{2,1,0:T(8,128)(2,1)} custom-call(bf16[176,2048]{1,0:T(8,128)(2,1)} %reduce-scatter.11.cloned.1.call-done.refs_0_), custom_call_target="tpu_custom_call" | custom-call | bytes 57671680 | tf_op jit(solution)/shard_map/gather_down/pallas_call | solution.py:356
  691.2 5.1 bitcast_convert_fusion
  696.3 28.8 %gather_qkv.1 = bf16[4,256,1664]{2,1,0:T(8,128)(2,1)} custom-call(bf16[256,1664]{1,0:T(8,128)(2,1)} %reduce-scatter.5.cloned.1.call-done.refs_0_), custom_call_target="tpu_custom_call" | custom-call | bytes 68157440 | tf_op jit(solution)/shard_map/gather_qkv/pallas_call | solution.py:356
  731.1 1.0 bitcast_dynamic-update-slice_fusion.5
  735.0 1.0 bitcast_dynamic-update-slice_fusion.1
  737.0 3.5 convert_element_type.75
  743.3 45.2 %gather_gate_up.1.source_ref = bf16[4,256,2816]{2,1,0:T(8,128)(2,1)} custom-call(bf16[256,2816]{1,0:T(8,128)(2,1)} %reduce-scatter.9.cloned.1.call-done.refs_0_), custom_call_target="tpu_custom_call" | custom-call | bytes 115343360 | tf_op jit(solution)/shard_map/gather_gate_up/pallas_call | solution.py:356
  788.5 9.5 %spread_columns.1 = f32[256,11264]{1,0:T(8,128)} custom-call(bf16[4,256,2816]{2,1,0:T(8,128)(2,1)} %gather_gate_up.1.source_ref), custom_call_target="tpu_custom_call" | custom-call | tf_op jit(solution)/shard_map/spread_columns/pallas_call | solution.py:644
  798.0 2.3 copy.69
  800.3 3.1 copy.70
  (116 shorter events, 21.5 us)
Async XLA Ops:
  7.2 20.8 %copy-start = (bf16[704,2048]{1,0:T(8,128)(2,1)S(1)}, bf16[704,2048]{1,0:T(8,128)(2,1)}, u32[]{:S(2)}) copy-start(bf16[704,2048]{1,0:T(8,128)(2,1)} %param.21) | copy-start | bytes 8650756
  7.2 98.6 %all-gather.9.cloned.1.call-start = ((), (), s32[]{:S(2)}) async-start(), calls=%async_computation.7 | async-start | bytes 2359296 | tf_op jit(solution)/shard_map/all_gather | solution.py:686
  9.1 125.4 %all-gather.7.cloned.1.call-start = ((), (), s32[]{:S(2)}) async-start(), calls=%async_computation.6 | async-start | bytes 7667712 | tf_op jit(solution)/shard_map/all_gather | solution.py:686
  21.1 7.8 copy-start.24
  21.1 7.9 copy-start.25
  21.1 265.8 %all-gather.11.cloned.1.call-start = ((), (), s32[]{:S(2)}) async-start(), calls=%async_computation.8 | async-start | bytes 12976128 | tf_op jit(solution)/shard_map/all_gather | solution.py:686
  27.9 277.7 %all-gather.13.cloned.1.call-start = ((), (), s32[]{:S(2)}) async-start(), calls=%async_computation.9 | async-start | bytes 6488064 | tf_op jit(solution)/shard_map/all_gather | solution.py:686
  102.5 6.9 copy-start.23
  102.5 21.8 %copy-start.26 = (bf16[128]{0:T(256)(128)(2,1)S(1)}, bf16[128]{0:T(256)(128)(2,1)}, u32[]{:S(2)}) copy-start(bf16[128]{0:T(256)(128)(2,1)} %param.17) | copy-start | bytes 772
  105.8 27.1 %all-to-all-start = ((bf16[4,512,512]{2,1,0:T(8,128)(2,1)}), bf16[4,512,512]{2,1,0:T(8,128)(2,1)S(1)}, u32[]{:S(2)}, u32[]{:S(2)}) async-start(bf16[4,512,512]{2,1,0:T(8,128)(2,1)} %bitcast.122), calls=%async_computation | async-start | bytes 4194304 | tf_op jit(solution)/shard_map/all_to_all | solution.py:705
  109.4 540.7 %reduce-scatter.7.cloned.1.call-start = ((), (), s32[]{:S(2)}) async-start(), calls=%async_computation.11 | async-start | bytes 2359296 | tf_op jit(solution)/shard_map/reduce_scatter | solution.py:655
  134.5 3.8 copy-start.20
  147.1 59.7 %copy-start.9 = (bf16[1024,1536]{1,0:T(8,128)(2,1)}, bf16[1024,1536]{1,0:T(8,128)(2,1)S(1)}, u32[]{:S(2)}) copy-start(bf16[1024,1536]{1,0:T(8,128)(2,1)S(1)} %fusion.4.proj_ref) | copy-start | bytes 9437188
  147.1 63.7 %copy-start.4 = (bf16[1,256,2048]{2,1,0:T(8,128)(2,1)S(1)}, bf16[1,256,2048]{2,1,0:T(8,128)(2,1)}, u32[]{:S(2)}) copy-start(bf16[1,256,2048]{2,1,0:T(8,128)(2,1)} %param.11) | copy-start | bytes 3145732
  206.8 1.0 copy-start.12
  207.8 1.0 copy-start.14
  208.8 1.0 copy-start.16
  209.8 1.0 copy-start.18
  322.1 3.3 copy-start.21
  322.1 4.2 copy-start.22
  322.1 4.2 copy-start.3
  408.2 5.4 copy-start.11
  440.8 226.8 %reduce-scatter.11.cloned.1.call-start = ((), (), s32[]{:S(2)}) async-start(), calls=%async_computation.13 | async-start | bytes 6488064 | tf_op jit(solution)/shard_map/reduce_scatter | solution.py:655
  451.3 245.0 %reduce-scatter.5.cloned.1.call-start = ((), (), s32[]{:S(2)}) async-start(), calls=%async_computation.10 | async-start | bytes 7667712 | tf_op jit(solution)/shard_map/reduce_scatter | solution.py:655
  451.6 5.5 copy-start.10
  451.6 5.5 copy-start.13
  451.6 5.5 copy-start.15
  451.6 5.5 copy-start.17
  451.6 5.5 copy-start.19
  486.4 1.8 copy-start.8
  504.1 239.2 %reduce-scatter.9.cloned.1.call-start = ((), (), s32[]{:S(2)}) async-start(), calls=%async_computation.12 | async-start | bytes 12976128 | tf_op jit(solution)/shard_map/reduce_scatter | solution.py:655
  522.8 1.6 copy-start.7
  524.5 40.5 %copy-start.5 = (bf16[1,256,2048]{2,1,0:T(8,128)(2,1)S(1)}, bf16[1,256,2048]{2,1,0:T(8,128)(2,1)}, u32[]{:S(2)}) copy-start(bf16[1,256,2048]{2,1,0:T(8,128)(2,1)} %param.11) | copy-start | bytes 3145732
  564.9 43.2 %copy-start.6 = (bf16[256,2048]{1,0:T(8,128)(2,1)}, bf16[256,2048]{1,0:T(8,128)(2,1)S(1)}, u32[]{:S(2)}) copy-start(bf16[256,2048]{1,0:T(8,128)(2,1)S(1)} %down_and_add.1) | copy-start | bytes 3145732
  608.1 83.1 %copy-start.2 = (f32[256,2048]{1,0:T(8,128)}, f32[256,2048]{1,0:T(8,128)S(1)}, u32[]{:S(2)}) copy-start(f32[256,2048]{1,0:T(8,128)S(1)} %get-tuple-element.40) | copy-start | bytes 6291460
  788.5 14.9 %copy-start.1 = (bf16[704,2048]{1,0:T(8,128)(2,1)S(1)}, bf16[704,2048]{1,0:T(8,128)(2,1)}, u32[]{:S(2)}) copy-start(bf16[704,2048]{1,0:T(8,128)(2,1)} %param.21) | copy-start | bytes 8650756
Sparse Core Ops, SparseCore 0:
  10.2 31.7 all-gather.8
  44.3 68.5 all-gather.6
  115.1 106.6 all-gather.10
  223.9 58.7 all-gather.12
  440.9 35.5 reduce-scatter.6
  479.2 63.5 reduce-scatter.10
  545.1 73.1 reduce-scatter.4
  621.2 118.4 reduce-scatter.8

commit v2 on v1

--- a/solution.py
+++ b/solution.py
@@ -70,18 +70,20 @@
     return found, found[0][4] * DK**-0.5, key, scale, found[2][4]
 
 
-def inverse_of(strict):
+def inverses_of(stricts):
     row, column = square_iota(0), square_iota(1)
     eye = (row == column).astype(jnp.float32)
-    solved = eye - jnp.where(row // 2 == column // 2, strict, 0.0)
+    solved = [eye - jnp.where(row // 2 == column // 2, strict, 0.0) for strict in stricts]
     half = 2
     while half < CHUNK:
         below = (row // (2 * half) == column // (2 * half)) & (row // half != column // half)
-        off = low(jnp.where(below, strict, 0.0))
-        known = low(solved)
-        solved = solved - dotf(low(dotf(known, off, NN)), known, NN)
+        off = [low(jnp.where(below, strict, 0.0)) for strict in stricts]
+        known = [low(item) for item in solved]
+        first = [low(dotf(k, o, NN)) for k, o in zip(known, off)]
+        second = [dotf(p, k, NN) for p, k in zip(first, known)]
+        solved = [item - change for item, change in zip(solved, second)]
         half *= 2
-    return solved
+    return [low(item) for item in solved]
 
 
 def forward_kernel(
@@ -90,35 +92,45 @@
 ):
     length = proj_ref.shape[0]
     carry[...] = jnp.zeros_like(carry)
+    every = range(heads)
 
     def step(chunk, _):
         start = pl.multiple_of(chunk * CHUNK, CHUNK)
         here = pl.ds(start, CHUNK)
         row, column = square_iota(0), square_iota(1)
         beta_all = low(sigmoid(logit_ref[here, :])).astype(jnp.float32)
-        for head in range(heads):
-            lanes = pl.ds(head * DK, DK)
-            _, query, key, _, value = head_inputs(proj_ref, table_ref, chunk, head, heads, taps)
-            query, key, value = low(query), low(key), low(value).astype(jnp.float32)
-            beta = beta_all[:, head : head + 1]
-            strict = jnp.where(row > column, dotf(key, key, NT) * beta, 0.0)
-            solved = low(inverse_of(strict))
-            within = low(jnp.where(row >= column, dotf(query, key, NT), 0.0))
-            state = carry[head]
-            state_low = low(state)
-            rest = value - dotf(key, state_low, NN)
-            fresh = low(dotf(solved, low(beta * rest), NN))
-            raw = low(dotf(query, state_low, NN) + dotf(within, fresh, NN))
-            carry[head] = state + dotf(key, fresh, TN)
+        beta = [beta_all[:, h : h + 1] for h in every]
+        ready = [head_inputs(proj_ref, table_ref, chunk, h, heads, taps) for h in every]
+        query = [low(item[1]) for item in ready]
+        key = [low(item[2]) for item in ready]
+        value = [low(item[4]) for item in ready]
+        gram = [dotf(key[h], key[h], NT) for h in every]
+        score = [dotf(query[h], key[h], NT) for h in every]
+        strict = [jnp.where(row > column, gram[h] * beta[h], 0.0) for h in every]
+        within = [low(jnp.where(row >= column, score[h], 0.0)) for h in every]
+        solved = inverses_of(strict)
+        state = [carry[h] for h in every]
+        state_low = [low(item) for item in state]
+        recalled = [dotf(key[h], state_low[h], NN) for h in every]
+        rest = [low(beta[h] * (value[h].astype(jnp.float32) - recalled[h])) for h in every]
+        fresh = [low(dotf(solved[h], rest[h], NN)) for h in every]
+        grown = [dotf(key[h], fresh[h], TN) for h in every]
+        for h in every:
+            carry[h] = state[h] + grown[h]
+        past = [dotf(query[h], state_low[h], NN) for h in every]
+        inner = [dotf(within[h], fresh[h], NN) for h in every]
+        for h in every:
+            lanes = pl.ds(h * DK, DK)
+            raw = low(past[h] + inner[h])
             wide_raw = raw.astype(jnp.float32)
             normed = wide_raw * lax.rsqrt(
                 jnp.mean(wide_raw * wide_raw, axis=-1, keepdims=True) + EPS
             )
             normed_ref[here, lanes] = low(normed * gain_ref[...])
             raw_ref[here, lanes] = raw
-            fresh_ref[here, lanes] = fresh
-            solve_ref[chunk, head] = solved
-            state_ref[chunk, head] = state_low
+            fresh_ref[here, lanes] = fresh[h]
+            solve_ref[chunk, h] = solved[h]
+            state_ref[chunk, h] = state_low[h]
         return 0
 
     lax.fori_loop(0, length // CHUNK, step, 0)
@@ -135,6 +147,7 @@
     after[...] = jnp.zeros_like(after)
     gtable_ref[...] = jnp.zeros_like(gtable_ref)
     ggain_ref[...] = jnp.zeros_like(ggain_ref)
+    every = range(heads)
 
     def step(index, _):
         chunk = count - 1 - index
@@ -143,75 +156,91 @@
         row, column = square_iota(0), square_iota(1)
         beta_wide = sigmoid(logit_ref[here, :])
         beta_all = low(beta_wide).astype(jnp.float32)
+        beta = [beta_all[:, h : h + 1] for h in every]
         lane = lax.broadcasted_iota(jnp.int32, (CHUNK, DK), 1)
-        glogit = jnp.zeros((CHUNK, DK), jnp.float32)
-        for head in range(heads):
-            lanes = pl.ds(head * DK, DK)
-            found, query_wide, key_wide, scale, value_wide = head_inputs(
-                proj_ref, table_ref, chunk, head, heads, taps
-            )
-            query, key, value = low(query_wide), low(key_wide), low(value_wide)
-            beta = beta_all[:, head : head + 1]
+        ready = [head_inputs(proj_ref, table_ref, chunk, h, heads, taps) for h in every]
+        query = [low(item[1]) for item in ready]
+        key = [low(item[2]) for item in ready]
+        value = [low(item[4]) for item in ready]
+        grad_out = []
+        for h in every:
+            lanes = pl.ds(h * DK, DK)
             raw = raw_ref[here, lanes].astype(jnp.float32)
             grad_normed = grad_ref[here, lanes].astype(jnp.float32)
             r = lax.rsqrt(jnp.mean(raw * raw, axis=-1, keepdims=True) + EPS)
             scaled = grad_normed * gain_ref[...]
-            grad_out = low(
-                r * (scaled - raw * (r * r) * jnp.mean(scaled * raw, axis=-1, keepdims=True))
+            mean = jnp.mean(scaled * raw, axis=-1, keepdims=True)
+            grad_out.append(low(r * (scaled - raw * (r * r) * mean)))
+            ggain_ref[...] += jnp.sum(grad_normed * raw * r, axis=0, keepdims=True)
+        state = [state_ref[chunk, h] for h in every]
+        solved = [solve_ref[chunk, h] for h in every]
+        fresh = [fresh_ref[here, pl.ds(h * DK, DK)] for h in every]
+        later = [carry[h] for h in every]
+        later_low = [low(item) for item in later]
+        score = [dotf(query[h], key[h], NT) for h in every]
+        onward = [dotf(key[h], later_low[h], NN) for h in every]
+        within = [low(jnp.where(row >= column, item, 0.0)) for item in score]
+        grad_fresh = [low(dotf(within[h], grad_out[h], TN) + onward[h]) for h in every]
+        grad_solved = [dotf(solved[h], grad_fresh[h], TN) for h in every]
+        grad_value = [beta[h] * grad_solved[h] for h in every]
+        grad_rest = [low(item) for item in grad_value]
+        asked = [dotf(query[h], grad_out[h], TN) for h in every]
+        taken = [dotf(key[h], grad_rest[h], TN) for h in every]
+        for h in every:
+            carry[h] = later[h] + asked[h] - taken[h]
+        gram = [dotf(key[h], key[h], NT) for h in every]
+        recalled = [dotf(key[h], state[h], NN) for h in every]
+        product = [dotf(grad_out[h], fresh[h], NT) for h in every]
+        cross = [dotf(low(grad_solved[h]), fresh[h], NT) for h in every]
+        grad_within = [low(jnp.where(row >= column, item, 0.0)) for item in product]
+        grad_strict = [jnp.where(row > column, -item, 0.0) for item in cross]
+        mixing = [low(beta[h] * grad_strict[h]) for h in every]
+        grad_query = [
+            dotf(grad_out[h], state[h], NT) + dotf(grad_within[h], key[h], NN) for h in every
+        ]
+        grad_key = [
+            dotf(grad_within[h], query[h], TN)
+            + dotf(fresh[h], later_low[h], NT)
+            - dotf(grad_rest[h], state[h], NT)
+            + dotf(mixing[h], key[h], NN)
+            + dotf(mixing[h], key[h], TN)
+            for h in every
+        ]
+        glogit = jnp.zeros((CHUNK, DK), jnp.float32)
+        for h in every:
+            rest = value[h].astype(jnp.float32) - recalled[h]
+            grad_beta = jnp.sum(grad_solved[h] * rest, axis=-1, keepdims=True) + jnp.sum(
+                grad_strict[h] * gram[h], axis=-1, keepdims=True
             )
-            ggain_ref[...] += jnp.sum(grad_normed * raw * r, axis=0, keepdims=True)
-
-            state, solved, fresh = state_ref[chunk, head], solve_ref[chunk, head], fresh_ref[here, lanes]
-            later = carry[head]
-            later_low = low(later)
-            gram = dotf(key, key, NT)
-            within = low(jnp.where(row >= column, dotf(query, key, NT), 0.0))
-            grad_fresh = dotf(within, grad_out, TN) + dotf(key, later_low, NN)
-            grad_solved = dotf(solved, low(grad_fresh), TN)
-            grad_value = beta * grad_solved
-            grad_rest = low(grad_value)
-            carry[head] = later + dotf(query, grad_out, TN) - dotf(key, grad_rest, TN)
-            rest = value.astype(jnp.float32) - dotf(key, state, NN)
-            grad_within = low(jnp.where(row >= column, dotf(grad_out, fresh, NT), 0.0))
-            grad_strict = jnp.where(row > column, -dotf(low(grad_solved), fresh, NT), 0.0)
-            grad_beta = jnp.sum(grad_solved * rest, axis=-1, keepdims=True) + jnp.sum(
-                grad_strict * gram, axis=-1, keepdims=True
+            bw = beta_wide[:, h : h + 1]
+            grad_beta = low(grad_beta).astype(jnp.float32) * bw * (1.0 - bw)
+            glogit = glogit + jnp.where(lane == h, grad_beta, 0.0)
+        gproj_ref[here, pl.ds(3 * wide, DK)] = low(glogit)
+        for h in every:
+            found, _, key_wide, scale, _ = ready[h]
+            lanes = pl.ds(h * DK, DK)
+            back_query = low(grad_query[h]).astype(jnp.float32) * DK**-0.5
+            back_key = low(grad_key[h]).astype(jnp.float32)
+            back_key = scale * (
+                back_key - key_wide * jnp.sum(back_key * key_wide, axis=-1, keepdims=True)
             )
-            mixing = low(beta * grad_strict)
-            grad_query = dotf(grad_out, state, NT) + dotf(grad_within, key, NN)
-            grad_key = (
-                dotf(grad_within, query, TN)
-                + dotf(fresh, later_low, NT)
-                - dotf(grad_rest, state, NT)
-                + dotf(mixing, key, NN)
-                + dotf(mixing, key, TN)
-            )
-            bw = beta_wide[:, head : head + 1]
-            grad_beta = low(grad_beta).astype(jnp.float32) * bw * (1.0 - bw)
-            glogit = glogit + jnp.where(lane == head, grad_beta, 0.0)
-
-            grad_query = low(grad_query).astype(jnp.float32) * DK**-0.5
-            grad_key = low(grad_key).astype(jnp.float32)
-            grad_key = scale * (
-                grad_key - key_wide * jnp.sum(grad_key * key_wide, axis=-1, keepdims=True)
-            )
-            grad_value = low(grad_value).astype(jnp.float32)
-            for part, grad_active in enumerate((grad_query, grad_key, grad_value)):
+            back_value = low(grad_value[h]).astype(jnp.float32)
+            for part, grad_active in enumerate((back_query, back_key, back_value)):
                 window, weights, mixed, gate, _ = found[part]
                 grad_conv = grad_active * (gate * (1.0 + mixed * (1.0 - gate)))
-                columns = pl.ds(part * wide + head * DK, DK)
+                columns = pl.ds(part * wide + h * DK, DK)
                 tail = jnp.concatenate([grad_conv, after[:, columns]], axis=0)
                 size = CHUNK + HEAD_ROOM
                 total = grad_conv * weights[taps - 1]
                 for back in range(1, taps):
-                    total = total + pltpu.roll(tail, size - back, 0)[:CHUNK] * weights[taps - 1 - back]
+                    ahead = pltpu.roll(tail, size - back, 0)[:CHUNK]
+                    total = total + ahead * weights[taps - 1 - back]
                 gproj_ref[here, columns] = low(total)
                 after[:, columns] = grad_conv[:HEAD_ROOM]
                 for back in range(taps):
                     shifted = pltpu.roll(window, back, 0)[HEAD_ROOM:] if back else window[HEAD_ROOM:]
                     spot = pl.ds(part * taps + taps - 1 - back, 1)
                     gtable_ref[spot, lanes] += jnp.sum(grad_conv * shifted, axis=0, keepdims=True)
-        gproj_ref[here, pl.ds(3 * wide, DK)] = low(glogit)
         return 0
 
     lax.fori_loop(0, count, step, 0)
@@ -371,12 +400,103 @@
     )(*blocks)
 
 
+def start_kernel(
+    source_ref, small_ref, sources, smalls,
+    send, arrive, keep, send_z, arrive_z, keep_z,
+):
+    near = neighbours()
+    _, across, along, _ = near
+    here, count = lax.axis_index("fsdp"), lax.axis_size("fsdp")
+    sibling = here + 1 - 2 * (here % 2)
+    others = [(here + 2 * step) % count for step in range(1, count // 2)]
+    barrier = pltpu.get_barrier_semaphore()
+    peers = [{"seq": across}, {"seq": along}, {"fsdp": sibling}]
+    peers += [{"fsdp": other} for other in others]
+    for peer in peers:
+        pl.semaphore_signal(barrier, inc=1, device_id=peer, device_id_type=pl.DeviceIdType.MESH)
+    pl.semaphore_wait(barrier, len(peers))
+
+    def send_to(source, target, row, slot, other):
+        return pltpu.make_async_remote_copy(
+            src_ref=source,
+            dst_ref=target,
+            send_sem=send_z.at[row, slot],
+            recv_sem=arrive_z.at[row, slot],
+            device_id={"fsdp": other},
+            device_id_type=pl.DeviceIdType.MESH,
+        )
+
+    flow = [(small_ref, smalls)]
+    first = []
+    for row, (source, target) in enumerate(flow):
+        own = pltpu.make_async_copy(source, target.at[here], keep_z.at[row])
+        own.start()
+        copies = [send_to(source, target.at[here], row, 0, sibling)]
+        copies += [
+            send_to(source, target.at[here], row, 1 + i, other) for i, other in enumerate(others)
+        ]
+        for copy in copies:
+            copy.start()
+        first.append((own, copies))
+    started = [
+        gather_start(block, target, near, send.at[i], arrive.at[i], keep.at[i])
+        for i, (block, target) in enumerate([(source_ref, sources)])
+    ]
+    gather_finish(started[0], sources, near, send.at[0], arrive.at[0])
+    for row, (source, target) in enumerate(flow):
+        own, copies = first[row]
+        passed = []
+        for i in range(len(others)):
+            copies[1 + i].wait_recv()
+            origin = target.at[(here + count - 2 * (i + 1)) % count]
+            passed.append(send_to(origin, origin, row, 1 + len(others) + i, sibling))
+            passed[-1].start()
+        copies[0].wait_recv()
+        for copy in passed:
+            copy.wait_recv()
+        for copy in copies + passed:
+            copy.wait_send()
+        own.wait()
+
+
+def start_gathers(source, small):
+    side, count = lax.axis_size("seq"), lax.axis_size("fsdp")
+    if side != 4:
+        return (
+            lax.all_gather(source, "seq", axis=0),
+            lax.all_gather(small, "fsdp", axis=0),
+        )
+    slots = count - 1
+    return pl.pallas_call(
+        start_kernel,
+        out_shape=[
+            jax.ShapeDtypeStruct((many,) + block.shape, block.dtype)
+            for block, many in ((source, side), (small, count))
+        ],
+        in_specs=[pl.BlockSpec(memory_space=pl.ANY)] * 2,
+        out_specs=[pl.BlockSpec(memory_space=pl.ANY)] * 2,
+        scratch_shapes=[
+            pltpu.SemaphoreType.DMA((2, 4)),
+            pltpu.SemaphoreType.DMA((2, 4)),
+            pltpu.SemaphoreType.DMA((2,)),
+            pltpu.SemaphoreType.DMA((2, slots)),
+            pltpu.SemaphoreType.DMA((2, slots)),
+            pltpu.SemaphoreType.DMA((2,)),
+        ],
+        compiler_params=pltpu.CompilerParams(collective_id=1, has_side_effects=True),
+        cost_estimate=pl.CostEstimate(
+            flops=0, bytes_accessed=160 * source.size, transcendentals=0
+        ),
+        name="start_gathers",
+    )(source, small)
+
+
 TILE = 256
 STEP = 16
 
 
-def reduce_rows_kernel(flip, gathers, epilogue, in_count, out_count, *refs):
-    left_ref, right_ref, *extra = refs[:in_count]
+def reduce_rows_kernel(flip, gathers, epilogue, lefts, in_count, out_count, *refs):
+    left_refs, right_ref, extra = refs[:lefts], refs[lefts], refs[lefts + 1 : in_count]
     outs = refs[in_count : in_count + out_count]
     far, wide_x, wide_y, own, get_a, get_b, get_x, get_y, send, arrive = refs[
         in_count + out_count : in_count + out_count + 10
@@ -395,10 +515,14 @@
         @pl.loop(0, width // TILE)
         def _(tile):
             columns = pl.ds(pl.multiple_of(tile * TILE, TILE), TILE)
-            if flip:
-                value = dotf(left_ref[here, :], right_ref[columns, :], NT)
-            else:
-                value = dotf(left_ref[here, :], right_ref[:, columns], NN)
+            value, base = 0.0, 0
+            for left_ref in left_refs:
+                depth = pl.ds(base, left_ref.shape[1])
+                if flip:
+                    value = value + dotf(left_ref[here, :], right_ref[columns, depth], NT)
+                else:
+                    value = value + dotf(left_ref[here, :], right_ref[depth, columns], NN)
+                base += left_ref.shape[1]
             store[:, columns] = value.astype(store.dtype)
 
     def add_into(store, base, source):
@@ -458,7 +582,7 @@
     r = lax.rsqrt(jnp.mean(values * values, axis=-1, keepdims=True) + EPS)
     scaled = grad * gain
     change = r * (scaled - values * (r * r) * jnp.mean(scaled * values, axis=-1, keepdims=True))
-    return change, jnp.sum(grad * values * r, axis=0, keepdims=True)
+    return change
 
 
 def middle_epilogue(index, here, total, extra, outs, block):
@@ -469,29 +593,23 @@
     block[here, :] = low(middle * r * gain_ref[...])
 
 
-def output_epilogue(index, here, total, extra, outs, block):
-    outs[0][here, :] = low(extra[0][here, :] + total)
-
-
 def branch_epilogue(index, here, total, extra, outs, block):
     middle_ref, upstream_ref, gain_ref = extra
-    change, gain_part = rms_back(total, middle_ref[here, :], gain_ref[...])
+    change = rms_back(total, middle_ref[here, :], gain_ref[...])
     grad = upstream_ref[here, :].astype(jnp.float32) + change
     outs[1][here, :] = grad
     block[here, :] = low(grad)
-    outs[2][...] = jnp.where(index > 0, outs[2][...], 0.0) + gain_part
 
 
 def input_epilogue(index, here, total, extra, outs, block):
     source_ref, carried_ref, gain_ref = extra
-    change, gain_part = rms_back(total, source_ref[here, :].astype(jnp.float32), gain_ref[...])
+    change = rms_back(total, source_ref[here, :].astype(jnp.float32), gain_ref[...])
     outs[0][here, :] = carried_ref[here, :] + change
-    outs[1][...] = jnp.where(index > 0, outs[1][...], 0.0) + gain_part
-
-
-def fused_reduce(name, number, flip, gathers, epilogue, outs, left, right, *extra):
+
+
+def fused_reduce(name, number, flip, gathers, epilogue, outs, lefts, right, *extra):
     side = lax.axis_size("seq")
-    length = left.shape[0]
+    length = lefts[0].shape[0]
     rows = length // side
     width = right.shape[0] if flip else right.shape[1]
     split = half_of(rows)
@@ -518,22 +636,28 @@
         out_specs[0] = pl.BlockSpec(memory_space=pl.ANY)
     return pl.pallas_call(
         functools.partial(
-            reduce_rows_kernel, flip, gathers, epilogue, 2 + len(extra), len(outs)
+            reduce_rows_kernel,
+            flip,
+            gathers,
+            epilogue,
+            len(lefts),
+            len(lefts) + 1 + len(extra),
+            len(outs),
         ),
         out_shape=outs,
-        in_specs=in_vmem(2 + len(extra)),
+        in_specs=in_vmem(len(lefts) + 1 + len(extra)),
         out_specs=out_specs,
         scratch_shapes=scratch,
         compiler_params=pltpu.CompilerParams(
             collective_id=number, has_side_effects=True, vmem_limit_bytes=50 * 2**20
         ),
         cost_estimate=pl.CostEstimate(
-            flops=2 * left.size * width,
+            flops=2 * sum(left.size for left in lefts) * width,
             bytes_accessed=(320 if gathers else 160) * rows * width,
             transcendentals=0,
         ),
         name=name,
-    )(left, right, *extra)
+    )(*lefts, right, *extra)
 
 
 def seq_sum(partial, side):
@@ -553,51 +677,152 @@
         jax.ShapeDtypeStruct((rows, width), jnp.float32),
     )
     return fused_reduce(
-        "out_and_norm", 2, False, True, middle_epilogue, outs, attn_in, weight, source, gain
-    )
-
-
-def down_and_add(hidden, weight, middle):
-    side = lax.axis_size("seq")
-    if side != 4:
-        return low(middle + seq_sum(dotf(hidden, weight, NN), side))
-    outs = (jax.ShapeDtypeStruct(middle.shape, jnp.bfloat16),)
-    return fused_reduce(
-        "down_and_add", 3, False, False, output_epilogue, outs, hidden, weight, middle
-    )[0]
-
-
-def branch_grad(grad, weight, middle, upstream, gain):
+        "out_and_norm", 2, False, True, middle_epilogue, outs, [attn_in], weight, source, gain
+    )
+
+
+def place_kernel(side, *refs):
+    target_ref = refs[side]
+    me = lax.axis_index("seq")
+    for spot in range(side):
+
+        @pl.when(me == spot)
+        def _():
+            for index in range(side):
+                target_ref[index] = refs[index ^ spot][...].astype(target_ref.dtype)
+
+
+def place(blocks, kind):
+    side = len(blocks)
+    rows, width = blocks[0].shape
+    tile = 512
+    return pl.pallas_call(
+        functools.partial(place_kernel, side),
+        grid=(width // tile,),
+        out_shape=jax.ShapeDtypeStruct((side, rows, width), kind),
+        in_specs=[pl.BlockSpec((rows, tile), lambda i: (0, i))] * side,
+        out_specs=pl.BlockSpec((side, rows, tile), lambda i: (0, 0, i)),
+        name="place",
+    )(*blocks)
+
+
+def swap(block, step):
+    pairs = [(i, i ^ step) for i in range(lax.axis_size("seq"))]
+    return lax.ppermute(block, "seq", pairs)
+
+
+def branch_grad(grads, weight, middle, upstream, gain):
     side = lax.axis_size("seq")
     rows, width = middle.shape
     if side != 4:
-        change, gain_part = rms_back(seq_sum(dotf(grad, weight, NT), side), middle, gain)
+        grad = jnp.concatenate(grads, axis=1)
+        change = rms_back(seq_sum(dotf(grad, weight, NT), side), middle, gain)
         total = upstream.astype(jnp.float32) + change
-        return lax.all_gather(low(total), "seq", axis=0), total, gain_part
+        return lax.all_gather(low(total), "seq", axis=0), total
     outs = (
         jax.ShapeDtypeStruct((side, rows, width), jnp.bfloat16),
         jax.ShapeDtypeStruct((rows, width), jnp.float32),
-        jax.ShapeDtypeStruct((1, width), jnp.float32),
     )
     return fused_reduce(
-        "branch_grad", 4, True, True, branch_epilogue, outs, grad, weight, middle, upstream, gain
+        "branch_grad", 4, True, True, branch_epilogue, outs, grads, weight, middle, upstream, gain
     )
 
 
 def input_grad(grad, weight, source, carried, gain):
     side = lax.axis_size("seq")
     if side != 4:
-        change, gain_part = rms_back(
-            seq_sum(dotf(grad, weight, NT), side), source.astype(jnp.float32), gain
+        return carried + rms_back(
+            seq_sum(dotf(grad, weight[:, : grad.shape[1]], NT), side), source.astype(jnp.float32), gain
         )
-        return carried + change, gain_part
-    outs = (
-        jax.ShapeDtypeStruct(carried.shape, jnp.float32),
-        jax.ShapeDtypeStruct(gain.shape, jnp.float32),
-    )
+    outs = (jax.ShapeDtypeStruct(carried.shape, jnp.float32),)
     return fused_reduce(
-        "input_grad", 5, True, False, input_epilogue, outs, grad, weight, source, carried, gain
-    )
+        "input_grad", 5, True, False, input_epilogue, outs, [grad], weight, source, carried, gain
+    )[0]
+
+
+def signal_all(peers):
+    barrier = pltpu.get_barrier_semaphore()
+    for peer in peers:
+        pl.semaphore_signal(barrier, inc=1, device_id=peer, device_id_type=pl.DeviceIdType.MESH)
+    pl.semaphore_wait(barrier, len(peers))
+
+
+def send_share(row, first, where, mine, boxes, send, arrive):
+    axis, spot, size = where
+    copies = []
+    for step in range(1, size):
+        copies.append(
+            pltpu.make_async_remote_copy(
+                src_ref=mine.at[row],
+                dst_ref=boxes.at[row, spot],
+                send_sem=send.at[first + step - 1],
+                recv_sem=arrive.at[first + step - 1],
+                device_id={axis: (spot + step) % size},
+                device_id_type=pl.DeviceIdType.MESH,
+            )
+        )
+        copies[-1].start()
+    boxes[row, spot] = mine[row]
+    return copies
+
+
+def add_shares(row, size, copies, boxes):
+    for copy in copies:
+        copy.wait()
+    total = boxes[row, 0]
+    for index in range(1, size):
+        total = total + boxes[row, index]
+    return total
+
+
+def gather_total_kernel(count, *refs):
+    sources, value_ref = refs[:count], refs[count]
+    targets, total_ref = refs[count + 1 : 2 * count + 1], refs[2 * count + 1]
+    mine, boxes, send_t, arrive_t, send, arrive, keep = refs[2 * count + 2 :]
+    near = neighbours()
+    spots = [(axis, lax.axis_index(axis), lax.axis_size(axis)) for axis in ("seq", "fsdp")]
+    signal_all(
+        [{axis: (spot + step) % size} for axis, spot, size in spots for step in range(1, size)]
+    )
+    mine[0] = value_ref[...]
+    copies = send_share(0, 0, spots[0], mine, boxes, send_t, arrive_t)
+    mine[1] = add_shares(0, spots[0][2], copies, boxes)
+    copies = send_share(1, spots[0][2] - 1, spots[1], mine, boxes, send_t, arrive_t)
+    started = [
+        gather_start(sources[i], targets[i], near, send.at[i], arrive.at[i], keep.at[i])
+        for i in range(count)
+    ]
+    for i in range(count):
+        gather_finish(started[i], targets[i], near, send.at[i], arrive.at[i])
+    total_ref[...] = add_shares(1, spots[1][2], copies, boxes)
+
+
+def gather_total(value, *blocks):
+    side, f_count = lax.axis_size("seq"), lax.axis_size("fsdp")
+    if side != 4:
+        summed = lax.psum(value, ("fsdp", "seq"))
+        return [lax.all_gather(block, "seq", axis=0) for block in blocks] + [summed]
+    count, peers = len(blocks), side + f_count - 2
+    moved = sum(block.size for block in blocks)
+    return pl.pallas_call(
+        functools.partial(gather_total_kernel, count),
+        out_shape=[jax.ShapeDtypeStruct((side,) + b.shape, b.dtype) for b in blocks]
+        + [jax.ShapeDtypeStruct(value.shape, value.dtype)],
+        in_specs=[pl.BlockSpec(memory_space=pl.ANY)] * count + in_vmem(1),
+        out_specs=[pl.BlockSpec(memory_space=pl.ANY)] * count + in_vmem(1),
+        scratch_shapes=[
+            pltpu.VMEM((3,) + value.shape, value.dtype),
+            pltpu.VMEM((2, max(side, f_count)) + value.shape, value.dtype),
+            pltpu.SemaphoreType.DMA((peers,)),
+            pltpu.SemaphoreType.DMA((peers,)),
+            pltpu.SemaphoreType.DMA((count, 4)),
+            pltpu.SemaphoreType.DMA((count, 4)),
+            pltpu.SemaphoreType.DMA((count,)),
+        ],
+        compiler_params=pltpu.CompilerParams(collective_id=7, has_side_effects=True),
+        cost_estimate=pl.CostEstimate(flops=0, bytes_accessed=160 * moved, transcendentals=0),
+        name="gather_total",
+    )(*blocks, value)
 
 
 def pick_kernel(side, share, source_ref, target_ref):
@@ -628,27 +853,73 @@
     )(weight)
 
 
-def spread_kernel(side, share, source_ref, target_ref):
-    count = source_ref.shape[2] // share
-    pieces = [
-        source_ref[index, :, pl.ds(k * share, share)].astype(jnp.float32)
-        for k in range(count)
-        for index in range(side)
-    ]
-    target_ref[...] = jnp.concatenate(pieces, axis=1)
-
-
-def spread_columns(parts, share):
-    side, rows, width = parts.shape
+def spread_kernel(side, share, *refs):
+    gate_refs, (up_ref, weight_ref, target_ref, total_ref) = refs[:side], refs[side:]
+    count = up_ref.shape[2] // share
+    me = lax.axis_index("seq")
+    half = target_ref.shape[1] // 2
+
+    def place(pieces, base):
+        grad = jnp.concatenate([piece.astype(jnp.float32) for piece in pieces], axis=1)
+        target_ref[:, pl.ds(base, half)] = grad
+        weight = weight_ref[:, pl.ds(base, half)].astype(jnp.float32)
+        return jnp.sum(grad * weight, axis=1, keepdims=True)
+
+    spans = [(pl.ds(k * share, share), index) for k in range(count) for index in range(side)]
+    total = place([up_ref[index, :, span] for span, index in spans], half)
+    for spot in range(side):
+
+        @pl.when(me == spot)
+        def _():
+            whole = total + place([gate_refs[index ^ spot][:, span] for span, index in spans], 0)
+            total_ref[...] = jnp.broadcast_to(whole, total_ref.shape)
+
+
+def spread_columns(gates, up, weight, share):
+    side, rows, width = up.shape
     tile = 32
+    by_row = pl.BlockSpec((tile, 2 * width * side), lambda i: (i, 0))
     return pl.pallas_call(
         functools.partial(spread_kernel, side, share),
         grid=(rows // tile,),
-        out_shape=jax.ShapeDtypeStruct((rows, width * side), jnp.float32),
-        in_specs=[pl.BlockSpec((side, tile, width), lambda i: (0, i, 0))],
-        out_specs=pl.BlockSpec((tile, width * side), lambda i: (i, 0)),
+        out_shape=(
+            jax.ShapeDtypeStruct((rows, 2 * width * side), jnp.float32),
+            jax.ShapeDtypeStruct((rows, DK), jnp.float32),
+        ),
+        in_specs=[pl.BlockSpec((tile, width), lambda i: (i, 0))] * side
+        + [pl.BlockSpec((side, tile, width), lambda i: (0, i, 0)), by_row],
+        out_specs=(by_row, pl.BlockSpec((tile, DK), lambda i: (i, 0))),
         name="spread_columns",
-    )(parts)
+    )(*gates, up, weight)
+
+
+def assemble_kernel(side, wide, grad_ref, weight_ref, target_ref, total_ref):
+    total = 0.0
+    for part in range(3):
+        for index in range(side):
+            columns = pl.ds((part * side + index) * wide, wide)
+            grad = grad_ref[index, :, pl.ds(part * wide, wide)].astype(jnp.float32)
+            target_ref[:, columns] = grad
+            weight = weight_ref[:, columns].astype(jnp.float32)
+            total = total + jnp.sum(grad * weight, axis=1, keepdims=True)
+    total_ref[...] = jnp.broadcast_to(total, total_ref.shape)
+
+
+def assemble_columns(grad, weight, wide):
+    side, rows, depth = grad.shape
+    tile = 32
+    by_row = pl.BlockSpec((tile, weight.shape[1]), lambda i: (i, 0))
+    return pl.pallas_call(
+        functools.partial(assemble_kernel, side, wide),
+        grid=(rows // tile,),
+        out_shape=(
+            jax.ShapeDtypeStruct(weight.shape, jnp.float32),
+            jax.ShapeDtypeStruct((rows, DK), jnp.float32),
+        ),
+        in_specs=[pl.BlockSpec((side, tile, depth), lambda i: (0, i, 0)), by_row],
+        out_specs=(by_row, pl.BlockSpec((tile, DK), lambda i: (i, 0))),
+        name="assemble_columns",
+    )(grad, weight)
 
 
 def fsdp_sum(term):
@@ -670,7 +941,6 @@
 ):
     side = lax.axis_size("seq")
     s = lax.axis_index("seq")
-    f = lax.axis_index("fsdp")
     shape = inputs.shape
     width = shape[2]
     source = inputs.reshape(-1, width)
@@ -682,41 +952,53 @@
     share = w_down.shape[0] // side
     taps = conv_weight.shape[1] // 3
 
+    f_count = lax.axis_size("fsdp")
+    depth = 3 * wide + DK
+    homes = [
+        (f * side + i, (side * (f % 2) + i) * side + f // 2)
+        for f in range(f_count)
+        for i in range(side)
+    ]
+    strip = rows // side
+
     def everywhere(block):
         return lax.all_gather(block, "fsdp", axis=0, tiled=True)
 
-    qkv_part = lax.dynamic_slice_in_dim(w_qkv.reshape(rows, 3, width), s * wide, wide, 2)
+    parts = [
+        lax.dynamic_slice_in_dim(w_qkv, part * width + s * wide, wide, 1) for part in range(3)
+    ]
     beta_part = lax.dynamic_slice_in_dim(w_beta, s * heads, heads, 1)
-    qkv_part = everywhere(
-        jnp.concatenate(
-            [qkv_part.reshape(rows, 3 * wide), jnp.pad(beta_part, ((0, 0), (0, DK - heads)))],
-            axis=1,
-        )
-    )
+    parts.append(jnp.pad(beta_part, ((0, 0), (0, DK - heads))))
+    qkv_part = everywhere(jnp.concatenate(parts, axis=1))
     small = jnp.concatenate([norm1_gain[None], norm2_gain[None], conv_weight.T], axis=0)
-    small = lax.all_gather(small, "fsdp", axis=0)
+    small = jnp.pad(small, ((0, 16 - small.shape[0]), (0, 0)))
+    piece = lax.dynamic_slice_in_dim(w_out, s * strip, strip, 0)
+    piece = lax.ppermute(piece, ("fsdp", "seq"), homes)
+    source_all, small = start_gathers(source, small)
+    sent, source_all = lax.optimization_barrier((upstream, source_all))
+    upstreams = [upstream] + [swap(sent, step) for step in range(1, side)]
+    out_part = everywhere(piece)
     small = small.transpose(1, 0, 2).reshape(small.shape[1], width).astype(jnp.float32)
     gain_first = small[0:1]
     gain_second = small[1:2]
-    table = lax.dynamic_slice_in_dim(small[2:], s * wide, wide, 1)
+    table = lax.dynamic_slice_in_dim(small[2 : 2 + 3 * taps], s * wide, wide, 1)
     gain_heads = out_gain.astype(jnp.float32)[None]
-
-    out_part = everywhere(lax.dynamic_slice_in_dim(w_out, s * wide, wide, 1))
-    out_part = lax.all_to_all(out_part, "seq", split_axis=0, concat_axis=1, tiled=True)
-    gate_up_part = everywhere(pick_columns(w_gate_up, share))
+    source_all = source_all.reshape(length, width).astype(jnp.float32)
+
+    picked = pick_columns(w_gate_up, share)
+    gate_up_part = everywhere(picked)
     down_part = everywhere(lax.dynamic_slice_in_dim(w_down, s * share, share, 0))
 
-    source_all, upstream_all = seq_gather("gather_tokens", 1, source, upstream)
-    source_all = source_all.reshape(length, width).astype(jnp.float32)
-    upstream_all = upstream_all.reshape(length, width)
     normed_first = low(
         source_all
         * lax.rsqrt(jnp.mean(source_all * source_all, axis=-1, keepdims=True) + EPS)
         * gain_first
     )
     projected = low(dotf(normed_first, qkv_part[:, : 3 * wide], NN))
-    beta_logits = dotf(normed_first, qkv_part[:, 3 * wide :], NN)
+    beta_logits = dotf(normed_first, qkv_part[:, 3 * wide : depth], NN)
     attn_in, *kept = mix_forward(projected, beta_logits, table, gain_heads)
+    attn_in, *upstreams = lax.optimization_barrier((attn_in, *upstreams))
+    upstream_all = place(upstreams, jnp.bfloat16).reshape(length, width)
     ffn_in, middle = out_and_norm(attn_in, out_part, source, gain_second)
     ffn_in = ffn_in.reshape(length, width)
     gate_up = dotf(ffn_in, gate_up_part, NN)
@@ -726,60 +1008,80 @@
     sigma = jax.nn.sigmoid(gate)
     hidden = low(gate * sigma * upward)
 
-    grad_down = fsdp_sum(dotf(hidden, upstream_all, TN))
+    down_term = low(dotf(hidden, upstream_all, TN))
+    grad_down = fsdp_sum(down_term)
+    hidden, _ = lax.optimization_barrier((hidden, down_term))
+    result = low(dotf(hidden, down_part, NN)).reshape((side, -1, width))
+    upstream_all, result = lax.optimization_barrier((upstream_all, result))
+    swapped = [
+        swap(lax.dynamic_index_in_dim(result, s ^ step, 0, keepdims=False), step)
+        for step in range(1, side)
+    ]
+    swapped.insert(0, lax.dynamic_index_in_dim(result, s, 0, keepdims=False))
     grad_hidden = dotf(upstream_all, down_part, NT)
-    grad_gate = grad_hidden * upward * sigma * (1.0 + gate * (1.0 - sigma))
-    grad_up = grad_hidden * gate * sigma
-    grad_gate_up = low(jnp.concatenate([grad_gate, grad_up], axis=1))
-    grad_w_gate_up = fsdp_sum(dotf(ffn_in, grad_gate_up, TN))
-    grad_branch, grad_middle, grad_gain_second = branch_grad(
-        grad_gate_up, gate_up_part, middle, upstream, gain_second
+    grad_gate = low(grad_hidden * upward * sigma * (1.0 + gate * (1.0 - sigma)))
+    grad_up = low(grad_hidden * gate * sigma)
+    grad_gate, *swapped[1:3] = lax.optimization_barrier((grad_gate, *swapped[1:3]))
+    gate_term = low(dotf(ffn_in, grad_gate, TN))
+    grad_up, swapped[3:], _ = lax.optimization_barrier((grad_up, swapped[3:], gate_term))
+    up_term = low(dotf(ffn_in, grad_up, TN))
+    gate_sum = fsdp_sum(gate_term)
+    up_sum = fsdp_sum(up_term)
+    grad_gate, grad_up, _, *swapped = lax.optimization_barrier(
+        (grad_gate, grad_up, up_term, *swapped)
+    )
+    output = low(middle + sum(block.astype(jnp.float32) for block in swapped))
+    grad_branch, grad_middle = branch_grad(
+        [grad_gate, grad_up], gate_up_part, middle, upstream, gain_second
+    )
+    grad_branch, grad_down, gate_sum = lax.optimization_barrier(
+        (grad_branch, grad_down, gate_sum)
     )
     grad_branch = grad_branch.reshape(length, width)
-    output = down_and_add(hidden, down_part, middle)
-
-    grad_w_out = low(dotf(attn_in, grad_branch, TN))
-    grad_w_out = lax.all_to_all(grad_w_out, "seq", split_axis=1, concat_axis=0, tiled=True)
-    grad_w_out = fsdp_sum(grad_w_out)
+    downs = [grad_down] + [swap(grad_down, step) for step in range(1, side)]
+    gates = [gate_sum] + [swap(gate_sum, step) for step in range(1, side)]
+
+    out_term = low(dotf(attn_in, grad_branch, TN))
+    out_sum = fsdp_sum(out_term)
+    grad_attn_in, _ = lax.optimization_barrier((dotf(grad_branch, out_part, NT), out_term))
     grad_proj, grad_table, grad_gain_heads = mix_backward(
-        projected, beta_logits, table, gain_heads, *kept, dotf(grad_branch, out_part, NT)
-    )
+        projected, beta_logits, table, gain_heads, *kept, grad_attn_in
+    )
+    grad_proj, up_sum, *downs = lax.optimization_barrier((grad_proj, up_sum, *downs))
     grad_qkv = low(dotf(normed_first, grad_proj, TN))
     grad_qkv = lax.dynamic_update_slice(
         grad_qkv, low(grad_table.T), (s * wide, 3 * wide + heads)
     )
+    grad_proj, grad_qkv, *gates = lax.optimization_barrier((grad_proj, grad_qkv, *gates))
     grad_qkv = fsdp_sum(grad_qkv)
-    grad_input, grad_gain_first = input_grad(
-        grad_proj, qkv_part, source, grad_middle, gain_first
-    )
-    gains = jnp.concatenate(
-        [grad_gain_first, grad_gain_second, jnp.pad(grad_gain_heads, ((0, 0), (0, width - DK)))]
-    )
-    summed = lax.psum(gains, ("fsdp", "seq"))
-    own = lax.dynamic_slice_in_dim(summed, f * rows, rows, 1)
-
-    (grad_down,) = seq_gather("gather_down", 6, grad_down)
-    (grad_w_gate_up,) = seq_gather("gather_gate_up", 7, grad_w_gate_up)
-    (grad_w_out,) = seq_gather("gather_out", 8, grad_w_out)
+    grad_input = input_grad(grad_proj, qkv_part, source, grad_middle, gain_first)
+    out_sum = lax.ppermute(out_sum, ("fsdp", "seq"), [(b, a) for a, b in homes])
+    up_sum, grad_input = lax.optimization_barrier((up_sum, grad_input))
+    up_sum, grad_w_out, grad_out_gain = gather_total(
+        jnp.broadcast_to(grad_gain_heads, (8, DK)), up_sum, out_sum
+    )
     (grad_qkv,) = seq_gather("gather_qkv", 9, grad_qkv)
-    grad_w_qkv = jnp.concatenate(
-        [grad_qkv[i, :, j * wide : (j + 1) * wide] for j in range(3) for i in range(side)], axis=1
-    )
+    grad_down = place(downs, jnp.float32).reshape(side * share, width)
+    grad_w_qkv, first_total = assemble_columns(grad_qkv, w_qkv, wide)
+    grad_w_gate_up, second_total = spread_columns(gates, up_sum, w_gate_up, share)
     sides = grad_qkv[:, :, 3 * wide :].astype(jnp.float32)
     grad_w_beta = jnp.concatenate([sides[i, :, :heads] for i in range(side)], axis=1)
     grad_conv = jnp.sum(sides[:, :, heads : heads + 3 * taps], axis=0)
+    first_total = first_total[:, 0] + jnp.sum(
+        w_beta.astype(jnp.float32) * grad_w_beta, axis=1
+    )
     return (
         output.reshape(shape),
         grad_input.reshape(shape),
-        own[0],
-        grad_w_qkv.astype(jnp.float32),
+        first_total / norm1_gain.astype(jnp.float32),
+        grad_w_qkv,
         grad_w_beta,
         grad_conv,
-        summed[2, :DK],
-        jnp.concatenate([grad_w_out[i] for i in range(side)], axis=1).astype(jnp.float32),
-        own[1],
-        spread_columns(grad_w_gate_up, share),
-        grad_down.reshape(-1, width).astype(jnp.float32),
+        grad_out_gain[0],
+        grad_w_out.reshape(rows, width).astype(jnp.float32),
+        second_total[:, 0] / norm2_gain.astype(jnp.float32),
+        grad_w_gate_up,
+        grad_down,
     )
 
 

time: 815 us -> 709 us (0.87)
  Pallas kernels: 533 us -> 427 us
  blocking collectives: 82.4 us -> 0 us
  waiting for transfers between devices: 3.31 us -> 80.8 us
  starting transfers between devices: 4.41 us -> 17.8 us
  local copies, waits for them, and re-layouts: 47.4 us -> 34.1 us
  matrix products: 99.8 us -> 110 us
    pallas_call x5 -> x1, Pallas kernels: 186 us -> 28.5 us  [seq_gather(): pl.pallas_call(functools.partial(gather_kernel, count), out_shape=[jax.Sh...]
    pallas_call x0 -> x5, Pallas kernels: none -> 126 us  [the longest x1 63.2 us: start_gathers(): pl.pallas_call(start_kernel, out_shape=[jax.ShapeDtypeStruct((many,) + bl...]
    ppermute x0 -> x14, waiting for transfers between devices: none -> 46.8 us  [the longest x12 46.8 us: swap(): return lax.ppermute(block, 'seq', pairs)]
    psum x1 -> x0, blocking collectives: 40.8 us -> none  [per_device(): summed = lax.psum(gains, ('fsdp', 'seq'))]
    pallas_call x1, Pallas kernels: 59.7 us -> 21.9 us  [mix_forward(): pl.pallas_call(functools.partial(forward_kernel, heads, taps), out_shape=...]
    all_gather x4, waiting for transfers between devices: 0.04 us -> 33.8 us  [everywhere(): return lax.all_gather(block, 'fsdp', axis=0, tiled=True)]
    pallas_call x4 -> x3, Pallas kernels: 242 us -> 212 us  [fused_reduce(): pl.pallas_call(functools.partial(reduce_rows_kernel, flip, gathers, epilo...]
    all_to_all x1 -> x0, blocking collectives: 27 us -> none  [per_device(): lax.all_to_all(grad_w_out, 'seq', split_axis=1, concat_axis=0, tiled=True)]
  transfers between devices with their start and end apart: 9 -> 23, of which waited for: 1 -> 8; matrix products, arithmetic and copies ran while one was open for 16% -> 19% of each run, Pallas kernels for 49% -> 55%
where the time goes in v2:
time: 709 us; the launch traced here: 704 us
  Pallas kernels  427 us (60%)
  matrix products  110 us (16%)
  waiting for transfers between devices  80.8 us (11%)
  local copies, waits for them, and re-layouts  34.1 us (5%)
  other arithmetic  19.4 us (3%)
  starting transfers between devices  17.8 us (3%)
  between operations  15.1 us (2%)
    pallas_call x3, Pallas kernels, fused_reduce(): pl.pallas_call(functools.partial(reduce_rows_kernel, flip, gathers, epilo...  212 us
    dot_general x11, matrix products, dotf(): lax.dot_general(left, right, (dims, ((), ())), preferred_element_type=jnp...  110 us
    pallas_call x1, Pallas kernels, start_gathers(): pl.pallas_call(start_kernel, out_shape=[jax.ShapeDtypeStruct((many,) + bl...  63.2 us
    ppermute x12, waiting for transfers between devices, swap(): return lax.ppermute(block, 'seq', pairs)  46.8 us
    pallas_call x1, Pallas kernels, gather_total(): pl.pallas_call(functools.partial(gather_total_kernel, count), out_shape=[...  44.3 us
    all_gather x4, waiting for transfers between devices, everywhere(): return lax.all_gather(block, 'fsdp', axis=0, tiled=True)  33.8 us
    pallas_call x1, Pallas kernels, seq_gather(): pl.pallas_call(functools.partial(gather_kernel, count), out_shape=[jax.Sh...  28.5 us
    pallas_call x1, Pallas kernels, mix_forward(): pl.pallas_call(functools.partial(forward_kernel, heads, taps), out_shape=...  21.9 us
  transfers between devices with their start and end apart: 23, of which 8 were waited for; matrix products, arithmetic and copies ran while one was open for 19% of the time, Pallas kernels for 55%

profile of v2, /device:TPU:0, one launch (start us, length us, event | category | flops | bytes accessed | tf_op | source)
XLA Modules:
  0.0 704.1 jit_solution(13199286014034100789)
XLA Ops:
  12.9 6.7 pick_columns.1
  20.4 63.2 %start_gathers.1 = (bf16[4,256,2048]{2,1,0:T(8,128)(2,1)}, bf16[8,16,256]{2,1,0:T(8,128)(2,1)}) custom-call(bf16[256,2048]{1,0:T(8,128)(2,1)} %bitcast.75, bf16[16,256]{1,0:T(8,128)(2,1)} %fusion.16.small_ref), custom_call_target="tpu_custom_call" | custom-call | bytes 83886080 | tf_op jit(solution)/shard_map/start_gathers/pallas_call | solution.py:470
  83.6 1.5 collective-permute-start.2
  85.0 2.1 collective-permute-start
  89.2 3.3 multiply_reduce_fusion
  92.7 3.1 fusion.1
  95.8 11.2 %fusion.4.proj_ref = bf16[1024,1536]{1,0:T(8,128)(2,1)S(1)} fusion(bf16[1024,2048]{1,0:T(8,128)(2,1)} %fusion.1, bf16[2048,1664]{1,0:T(8,128)(2,1)} %all-gather.5.cloned.1.call-done.refs_1_), kind=kOutput, calls=%fused_computation.14 | convolution fusion | flops 6444023808 | bytes 13631488 | tf_op jit(solution)/shard_map/dot_general | solution.py:18
  107.0 2.7 fusion.10.logit_ref
  109.8 21.9 %mix_forward.1 = (bf16[1024,512]{1,0:T(8,128)(2,1)S(1)}, bf16[1024,512]{1,0:T(8,128)(2,1)S(1)}, bf16[1024,512]{1,0:T(8,128)(2,1)S(1)}, bf16[8,4,128,128]{3,2,1,0:T(8,128)(2,1)S(1)}, bf16[8,4,128,128]{3,2,1,0:T(8,128)(2,1)S(1)}) custom-call(bf16[1024,1536]{1,0:T(8,128)(2,1)S(1)} %fusion.4.proj_ref, f32[1024,128]{1,0:T(8,128)S(1)} %fusion.10.logit_ref, ...), custom_call_target="tpu_custom_call" | custom-call | flops 4194304000 | bytes 8388608 | tf_op jit(solution)/shard_map/mix_forward/pallas_call | solution.py:260
  136.8 4.9 place.2
  141.7 77.8 %out_and_norm.1 = (bf16[4,256,2048]{2,1,0:T(8,128)(2,1)}, f32[256,2048]{1,0:T(8,128)}) custom-call(bf16[1024,512]{1,0:T(8,128)(2,1)S(1)} %copy-done.9, bf16[512,2048]{1,0:T(8,128)(2,1)} %all-gather.7.cloned.1.call-done.refs_1_, bf16[256,2048]{1,0:T(8,128)(2,1)S(1)} %bitcast.76, f32[1,2048]{1,0:T(1,128)S(1)} %bitcast.85), custom_call_target="tpu_custom_call" | custom-call | flops 2147483648 | bytes 167772160 | tf_op jit(solution)/shard_map/out_and_norm/pallas_call | solution.py:637
  219.5 5.7 all-gather.9.cloned.1.call-done.refs_2_
  225.1 17.2 %fusion.18 = f32[1024,2816]{1,0:T(8,128)S(1)} fusion(bf16[1024,2048]{1,0:T(8,128)(2,1)} %bitcast.97, bf16[2048,2816]{1,0:T(8,128)(2,1)} %all-gather.9.cloned.1.call-done.refs_2_), kind=kOutput, calls=%fused_computation.59 | convolution fusion | flops 11811160064 | bytes 27262976 | tf_op jit(solution)/shard_map/dot_general | solution.py:18
  242.3 1.8 multiply_convert_fusion.2
  244.2 3.6 copy-done.23
  247.7 1.6 copy-done.28
  249.3 8.3 %convolution_convert_fusion.3 = bf16[1408,2048]{1,0:T(8,128)(2,1)} fusion(bf16[1024,1408]{1,0:T(8,128)(2,1)S(1)} %multiply_convert_fusion.2, bf16[1024,2048]{1,0:T(8,128)(2,1)S(1)} %bitcast.90), kind=kOutput, calls=%fused_computation.7 | convolution fusion | flops 5908463616 | bytes 12845056 | tf_op jit(solution)/shard_map/dot_general | solution.py:18
  257.7 28.2 %all-gather.11.cloned.1.call-done = bf16[1408,2048]{1,0:T(8,128)(2,1)} async-done(((bf16[176,2048]{1,0:T(8,128)(2,1)}), bf16[1408,2048]{1,0:T(8,128)(2,1)}) %all-gather.11.cloned.1.call-update) | async-done | bytes 5767184 | tf_op jit(solution)/shard_map/all_gather | solution.py:965
  285.9 9.5 %convolution_convert_fusion.4 = bf16[1024,2048]{1,0:T(8,128)(2,1)S(1)} fusion(bf16[1024,1408]{1,0:T(8,128)(2,1)} %copy-done.28, bf16[1408,2048]{1,0:T(8,128)(2,1)} %all-gather.11.cloned.1.call-done), kind=kOutput, calls=%fused_computation.15 | convolution fusion | flops 5907677184 | bytes 12845056 | tf_op jit(solution)/shard_map/dot_general | solution.py:18
  295.5 1.8 dynamic-slice_bitcast_fusion
  297.2 1.5 collective-permute-start.5
  298.7 1.5 collective-permute-start.4
  300.2 14.4 %multiply_convert_fusion = (bf16[1024,1408]{1,0:T(8,128)(2,1)}, bf16[1024,1408]{1,0:T(8,128)(2,1)}) fusion(f32[1024,2816]{1,0:T(8,128)} %copy-done.23, bf16[1024,2048]{1,0:T(8,128)(2,1)S(1)} %bitcast.91, bf16[1408,2048]{1,0:T(8,128)(2,1)} %all-gather.11.cloned.1.call-done), kind=kOutput, calls=%fused_computation.10 | convolution fusion | flops 5924323328 | bytes 27262976 | tf_op jit(solution)/shard_map/dot_general | solution.py:18
  314.6 8.0 %collective-permute-done.5 = bf16[256,2048]{1,0:T(8,128)(2,1)S(1)} collective-permute-done((bf16[256,2048]{1,0:T(8,128)(2,1)S(1)}, bf16[256,2048]{1,0:T(8,128)(2,1)S(1)}, u32[]{:S(2)}, u32[]{:S(2)}) %collective-permute-start.5) | collective-permute-done | bytes 1048608 | tf_op jit(solution)/shard_map/ppermute | solution.py:711
  323.7 10.8 %convolution_convert_fusion.2 = bf16[2048,1408]{1,0:T(8,128)(2,1)} fusion(bf16[1024,2048]{1,0:T(8,128)(2,1)S(1)} %bitcast.99, bf16[1024,1408]{1,0:T(8,128)(2,1)} %get-tuple-element.99.refs_0_), kind=kOutput, calls=%fused_computation.6 | convolution fusion | flops 5908463616 | bytes 12845056 | tf_op jit(solution)/shard_map/dot_general | solution.py:18
  335.7 1.6 collective-permute-start.6
  337.3 23.6 %collective-permute-done.6 = bf16[256,2048]{1,0:T(8,128)(2,1)S(1)} collective-permute-done((bf16[256,2048]{1,0:T(8,128)(2,1)S(1)}, bf16[256,2048]{1,0:T(8,128)(2,1)S(1)}, u32[]{:S(2)}, u32[]{:S(2)}) %collective-permute-start.6) | collective-permute-done | bytes 1048608 | tf_op jit(solution)/shard_map/ppermute | solution.py:711
  361.0 11.4 %convolution_convert_fusion.1 = bf16[2048,1408]{1,0:T(8,128)(2,1)} fusion(bf16[1024,2048]{1,0:T(8,128)(2,1)} %bitcast.98, bf16[1024,1408]{1,0:T(8,128)(2,1)} %get-tuple-element.100.refs_1_), kind=kOutput, calls=%fused_computation.5 | convolution fusion | flops 5908463616 | bytes 12845056 | tf_op jit(solution)/shard_map/dot_general | solution.py:18
  373.7 83.0 %branch_grad.1 = (bf16[4,256,2048]{2,1,0:T(8,128)(2,1)}, f32[256,2048]{1,0:T(8,128)S(1)}) custom-call(bf16[1024,1408]{1,0:T(8,128)(2,1)} %get-tuple-element.99.refs_0_, bf16[1024,1408]{1,0:T(8,128)(2,1)} %get-tuple-element.100.refs_1_, bf16[2048,2816]{1,0:T(8,128)(2,1)} %all-gather.9.cloned.1.call-done.refs_2_, f32[256,2048]{1,0:T(8,128)} %get-tuple-element.77.refs_3_, ...), custom_call_target="tpu_custom_call" | custom-call | flops 11811160064 | bytes 167772160 | tf_op jit(solution)/shard_map/branch_grad/pallas_call | solution.py:637
  456.7 7.0 convolution_convert_fusion.5
  463.8 1.5 collective-permute-start.9
  470.1 5.3 fusion.19.grad_ref
  475.4 18.7 %mix_backward.1 = (bf16[1024,1664]{1,0:T(8,128)(2,1)S(1)}, f32[12,512]{1,0:T(8,128)S(1)}, f32[1,128]{1,0:T(1,128)S(1)}) custom-call(bf16[1024,1536]{1,0:T(8,128)(2,1)S(1)} %copy-done.12, f32[1024,128]{1,0:T(8,128)S(1)} %fusion.10.logit_ref, f32[12,512]{1,0:T(8,128)S(1)} %constant_dynamic-slice_fusion.2.table_ref, ...), custom_call_target="tpu_custom_call" | custom-call | flops 5242880000 | bytes 13631488 | tf_op jit(solution)/shard_map/mix_backward/pallas_call | solution.py:286
  494.2 1.7 copy-done.10
  496.9 2.7 collective-permute-done.8.refs_2_
  499.7 12.5 %convolution_convert_fusion = bf16[2048,1664]{1,0:T(8,128)(2,1)} fusion(bf16[1024,2048]{1,0:T(8,128)(2,1)} %fusion.1, bf16[1024,1664]{1,0:T(8,128)(2,1)} %copy-done.10), kind=kOutput, calls=%fused_computation.4 | convolution fusion | flops 6982729728 | bytes 14417920 | tf_op jit(solution)/shard_map/dot_general | solution.py:18
  512.2 3.4 dynamic_update_slice.3
  515.6 10.4 %collective-permute-done.11.refs_2_ = bf16[256,1408]{1,0:T(8,128)(2,1)} collective-permute-done((bf16[256,1408]{1,0:T(8,128)(2,1)}, bf16[256,1408]{1,0:T(8,128)(2,1)}, u32[]{:S(2)}, u32[]{:S(2)}) %collective-permute-start.11) | collective-permute-done | bytes 720928 | tf_op jit(solution)/shard_map/ppermute | solution.py:711
  526.8 4.0 fusion.8
  530.8 1.6 collective-permute-start.13
  533.7 51.0 %input_grad.1 = f32[256,2048]{1,0:T(8,128)S(1)} custom-call(bf16[1024,1664]{1,0:T(8,128)(2,1)} %copy-done.10, bf16[2048,1664]{1,0:T(8,128)(2,1)} %all-gather.5.cloned.1.call-done.refs_1_, bf16[256,2048]{1,0:T(8,128)(2,1)S(1)} %bitcast.77, f32[256,2048]{1,0:T(8,128)} %copy-done.13, f32[1,2048]{1,0:T(1,128)S(1)} %bitcast.84), custom_call_target="tpu_custom_call" | custom-call | flops 6979321856 | bytes 83886080 | tf_op jit(solution)/shard_map/input_grad/pallas_call | solution.py:637
  584.7 5.7 place.3
  591.1 44.3 %gather_total.1 = (bf16[4,256,1408]{2,1,0:T(8,128)(2,1)}, bf16[4,64,2048]{2,1,0:T(8,128)(2,1)}, f32[8,128]{1,0:T(8,128)}) custom-call(bf16[256,1408]{1,0:T(8,128)(2,1)} %reduce-scatter.10.cloned.1.call-done.refs_0_, bf16[64,2048]{1,0:T(8,128)(2,1)} %copy-done.36, f32[8,128]{1,0:T(8,128)} %broadcast_in_dim.24.refs_2_), custom_call_target="tpu_custom_call" | custom-call | bytes 78643200 | tf_op jit(solution)/shard_map/gather_total/pallas_call | solution.py:807
  635.4 12.9 %spread_columns.1 = (f32[256,11264]{1,0:T(8,128)}, f32[256,128]{1,0:T(8,128)}) custom-call(bf16[256,1408]{1,0:T(8,128)(2,1)} %reduce-scatter.8.cloned.1.call-done.refs_0_, bf16[256,1408]{1,0:T(8,128)(2,1)} %collective-permute-done.10.refs_1_, bf16[256,1408]{1,0:T(8,128)(2,1)} %collective-permute-done.11.refs_2_, ...), custom_call_target="tpu_custom_call" | custom-call | tf_op jit(solution)/shard_map/spread_columns/pallas_call | solution.py:882
  651.1 1.6 bitcast_convert_fusion
  652.8 28.5 %gather_qkv.1.grad_ref = bf16[4,256,1664]{2,1,0:T(8,128)(2,1)} custom-call(bf16[256,1664]{1,0:T(8,128)(2,1)} %reduce-scatter.12.cloned.1.call-done.refs_0_), custom_call_target="tpu_custom_call" | custom-call | bytes 68157440 | tf_op jit(solution)/shard_map/gather_qkv/pallas_call | solution.py:385
  682.5 8.1 %assemble_columns.1 = (f32[256,6144]{1,0:T(8,128)}, f32[256,128]{1,0:T(8,128)}) custom-call(bf16[4,256,1664]{2,1,0:T(8,128)(2,1)} %gather_qkv.1.grad_ref, bf16[256,6144]{1,0:T(8,128)(2,1)} %weight_ref.1), custom_call_target="tpu_custom_call" | custom-call | tf_op jit(solution)/shard_map/assemble_columns/pallas_call | solution.py:912
  693.9 3.1 copy.45
  (165 shorter events, 33.3 us)
Async XLA Ops:
  7.2 79.9 %copy-start = (bf16[704,2048]{1,0:T(8,128)(2,1)S(1)}, bf16[704,2048]{1,0:T(8,128)(2,1)}, u32[]{:S(2)}) copy-start(bf16[704,2048]{1,0:T(8,128)(2,1)} %param.21) | copy-start | bytes 8650756
  7.2 88.6 %all-gather.5.cloned.1.call-start = ((), (), s32[]{:S(2)}) async-start(), calls=%async_computation.5 | async-start | bytes 7667712 | tf_op jit(solution)/shard_map/all_gather | solution.py:965
  10.4 131.2 %all-gather.7.cloned.1.call-start = ((), (), s32[]{:S(2)}) async-start(), calls=%async_computation.6 | async-start | bytes 2359296 | tf_op jit(solution)/shard_map/all_gather | solution.py:965
  11.4 0.7 collective-permute-start.3
  12.9 6.9 copy-start.41
  12.9 6.9 copy-start.39
  12.9 6.9 copy-start.38
  12.9 212.2 %all-gather.9.cloned.1.call-start = ((), (), s32[]{:S(2)}) async-start(), calls=%async_computation.7 | async-start | bytes 12976128 | tf_op jit(solution)/shard_map/all_gather | solution.py:965
  19.7 69.5 %copy-start.43 = (bf16[128]{0:T(256)(128)(2,1)S(1)}, bf16[128]{0:T(256)(128)(2,1)}, u32[]{:S(2)}) copy-start(bf16[128]{0:T(256)(128)(2,1)} %param.17) | copy-start | bytes 772
  19.7 266.2 %all-gather.11.cloned.1.call-start = ((), (), s32[]{:S(2)}) async-start(), calls=%async_computation.8 | async-start | bytes 6488064 | tf_op jit(solution)/shard_map/all_gather | solution.py:965
  83.6 53.2 %collective-permute-start.2 = (bf16[256,2048]{1,0:T(8,128)(2,1)}, bf16[256,2048]{1,0:T(8,128)(2,1)}, u32[]{:S(2)}, u32[]{:S(2)}) collective-permute-start(bf16[256,2048]{1,0:T(8,128)(2,1)} %bitcast.78), channel_id=1, source_target_pairs={{0,3},{1,2},{2,1},{3,0},{4,7},{5,6},{6,5},{7,4},{8,11},{9,10},{10,... | collective-permute-start | bytes 3145736 | tf_op jit(solution)/shard_map/ppermute | solution.py:711
  85.0 51.7 %collective-permute-start.1 = (bf16[256,2048]{1,0:T(8,128)(2,1)}, bf16[256,2048]{1,0:T(8,128)(2,1)}, u32[]{:S(2)}, u32[]{:S(2)}) collective-permute-start(bf16[256,2048]{1,0:T(8,128)(2,1)} %bitcast.79), channel_id=1, source_target_pairs={{0,2},{1,3},{2,0},{3,1},{4,6},{5,7},{6,4},{7,5},{8,10},{9,11},{10,... | collective-permute-start | bytes 3145736 | tf_op jit(solution)/shard_map/ppermute | solution.py:711
  85.0 51.7 %collective-permute-start = (bf16[256,2048]{1,0:T(8,128)(2,1)}, bf16[256,2048]{1,0:T(8,128)(2,1)}, u32[]{:S(2)}, u32[]{:S(2)}) collective-permute-start(bf16[256,2048]{1,0:T(8,128)(2,1)} %bitcast.80), channel_id=1, source_target_pairs={{0,1},{1,0},{2,3},{3,2},{4,5},{5,4},{6,7},{7,6},{8,9},{9,8},{10,11... | collective-permute-start | bytes 3145736 | tf_op jit(solution)/shard_map/ppermute | solution.py:711
  88.1 368.6 %reduce-scatter.6.cloned.1.call-start = ((), (), s32[]{:S(2)}) async-start(), calls=%async_computation.9 | async-start | bytes 6488064 | tf_op jit(solution)/shard_map/reduce_scatter | solution.py:926
  95.8 11.3 %copy-start.25 = (bf16[1024,2048]{1,0:T(8,128)(2,1)S(1)}, bf16[1024,2048]{1,0:T(8,128)(2,1)}, u32[]{:S(2)}) copy-start(bf16[1024,2048]{1,0:T(8,128)(2,1)} %fusion.1) | copy-start | bytes 12582916
  107.0 24.6 %copy-start.11 = (bf16[1024,1536]{1,0:T(8,128)(2,1)}, bf16[1024,1536]{1,0:T(8,128)(2,1)S(1)}, u32[]{:S(2)}) copy-start(bf16[1024,1536]{1,0:T(8,128)(2,1)S(1)} %fusion.4.proj_ref) | copy-start | bytes 9437188
  242.3 7.0 copy-start.26
  257.7 199.1 %reduce-scatter.8.cloned.1.call-start = ((), (), s32[]{:S(2)}) async-start(), calls=%async_computation.10 | async-start | bytes 6488064 | tf_op jit(solution)/shard_map/reduce_scatter | solution.py:926
  297.2 25.3 %collective-permute-start.5 = (bf16[256,2048]{1,0:T(8,128)(2,1)S(1)}, bf16[256,2048]{1,0:T(8,128)(2,1)S(1)}, u32[]{:S(2)}, u32[]{:S(2)}) collective-permute-start(bf16[256,2048]{1,0:T(8,128)(2,1)S(1)} %get-tuple-element.170), channel_id=1, source_target_pairs={{0,2},{1,3},{2,0},{3,1},{4,6},{5,7},{6,4},{7,5},{8,10},{9,11},{10,... | collective-permute-start | bytes 3145736 | tf_op jit(solution)/shard_map/ppermute | solution.py:711
  298.7 25.0 %copy-start.44 = (bf16[4,256,2048]{2,1,0:T(8,128)(2,1)S(1)}, bf16[4,256,2048]{2,1,0:T(8,128)(2,1)}, u32[]{:S(2)}) copy-start(bf16[4,256,2048]{2,1,0:T(8,128)(2,1)} %get-tuple-element.82) | copy-start | bytes 12582916
  298.7 25.0 %collective-permute-start.4 = (bf16[256,2048]{1,0:T(8,128)(2,1)S(1)}, bf16[256,2048]{1,0:T(8,128)(2,1)S(1)}, u32[]{:S(2)}, u32[]{:S(2)}) collective-permute-start(bf16[256,2048]{1,0:T(8,128)(2,1)S(1)} %get-tuple-element.171), channel_id=1, source_target_pairs={{0,1},{1,0},{2,3},{3,2},{4,5},{5,4},{6,7},{7,6},{8,9},{9,8},{10,11... | collective-permute-start | bytes 3145736 | tf_op jit(solution)/shard_map/ppermute | solution.py:711
  322.5 12.0 %copy-start.29 = (bf16[256,2048]{1,0:T(8,128)(2,1)}, bf16[256,2048]{1,0:T(8,128)(2,1)S(1)}, u32[]{:S(2)}) copy-start(bf16[256,2048]{1,0:T(8,128)(2,1)S(1)} %collective-permute-done.5) | copy-start | bytes 3145732
  323.7 10.8 %copy-start.31 = (bf16[256,2048]{1,0:T(8,128)(2,1)}, bf16[256,2048]{1,0:T(8,128)(2,1)S(1)}, u32[]{:S(2)}) copy-start(bf16[256,2048]{1,0:T(8,128)(2,1)S(1)} %collective-permute-done.4) | copy-start | bytes 3145732
  334.5 162.4 %reduce-scatter.10.cloned.1.call-start = ((), (), s32[]{:S(2)}) async-start(), calls=%async_computation.11 | async-start | bytes 6488064 | tf_op jit(solution)/shard_map/reduce_scatter | solution.py:926
  335.7 25.2 %collective-permute-start.6 = (bf16[256,2048]{1,0:T(8,128)(2,1)S(1)}, bf16[256,2048]{1,0:T(8,128)(2,1)S(1)}, u32[]{:S(2)}, u32[]{:S(2)}) collective-permute-start(bf16[256,2048]{1,0:T(8,128)(2,1)S(1)} %copy-done.33), channel_id=1, source_target_pairs={{0,3},{1,2},{2,1},{3,0},{4,7},{5,6},{6,5},{7,4},{8,11},{9,10},{10,... | collective-permute-start | bytes 3145736 | tf_op jit(solution)/shard_map/ppermute | solution.py:711
  361.0 11.4 %copy-start.32 = (bf16[256,2048]{1,0:T(8,128)(2,1)}, bf16[256,2048]{1,0:T(8,128)(2,1)S(1)}, u32[]{:S(2)}) copy-start(bf16[256,2048]{1,0:T(8,128)(2,1)S(1)} %collective-permute-done.6) | copy-start | bytes 3145732
  372.3 158.5 %reduce-scatter.14.cloned.1.call-start = ((), (), s32[]{:S(2)}) async-start(), calls=%async_computation.13 | async-start | bytes 2359296 | tf_op jit(solution)/shard_map/reduce_scatter | solution.py:926
  456.7 7.1 %copy-start.13 = (f32[256,2048]{1,0:T(8,128)}, f32[256,2048]{1,0:T(8,128)S(1)}, u32[]{:S(2)}) copy-start(f32[256,2048]{1,0:T(8,128)S(1)} %get-tuple-element.111.refs_3_) | copy-start | bytes 6291460
  463.7 189.0 %reduce-scatter.12.cloned.1.call-start = ((), (), s32[]{:S(2)}) async-start(), calls=%async_computation.12 | async-start | bytes 7667712 | tf_op jit(solution)/shard_map/reduce_scatter | solution.py:926
  463.8 11.6 %copy-start.12 = (bf16[1024,1536]{1,0:T(8,128)(2,1)S(1)}, bf16[1024,1536]{1,0:T(8,128)(2,1)}, u32[]{:S(2)}) copy-start(bf16[1024,1536]{1,0:T(8,128)(2,1)} %copy-done.11) | copy-start | bytes 9437188
  463.8 11.6 %copy-start.15 = (bf16[1024,512]{1,0:T(8,128)(2,1)S(1)}, bf16[1024,512]{1,0:T(8,128)(2,1)}, u32[]{:S(2)}) copy-start(bf16[1024,512]{1,0:T(8,128)(2,1)} %copy-done.14) | copy-start | bytes 3145732
  463.8 11.6 %copy-start.17 = (bf16[1024,512]{1,0:T(8,128)(2,1)S(1)}, bf16[1024,512]{1,0:T(8,128)(2,1)}, u32[]{:S(2)}) copy-start(bf16[1024,512]{1,0:T(8,128)(2,1)} %copy-done.16) | copy-start | bytes 3145732
  463.8 11.6 %copy-start.19 = (bf16[8,4,128,128]{3,2,1,0:T(8,128)(2,1)S(1)}, bf16[8,4,128,128]{3,2,1,0:T(8,128)(2,1)}, u32[]{:S(2)}) copy-start(bf16[8,4,128,128]{3,2,1,0:T(8,128)(2,1)} %copy-done.18) | copy-start | bytes 3145732
  463.8 11.6 %copy-start.21 = (bf16[8,4,128,128]{3,2,1,0:T(8,128)(2,1)S(1)}, bf16[8,4,128,128]{3,2,1,0:T(8,128)(2,1)}, u32[]{:S(2)}) copy-start(bf16[8,4,128,128]{3,2,1,0:T(8,128)(2,1)} %copy-done.20) | copy-start | bytes 3145732
  463.8 32.3 %collective-permute-start.9 = (bf16[176,2048]{1,0:T(8,128)(2,1)}, bf16[176,2048]{1,0:T(8,128)(2,1)}, u32[]{:S(2)}, u32[]{:S(2)}) collective-permute-start(bf16[176,2048]{1,0:T(8,128)(2,1)} %reduce-scatter.6.cloned.1.call-done.refs_0_), channel_id=1, source_target_pairs={{0,3},{1,2},{2,1},{3,0},{4,7},{5,6},{6,5},{7,4},{8,11},{9,10},{10,... | collective-permute-start | bytes 2162696 | tf_op jit(solution)/shard_map/ppermute | solution.py:711
  465.3 34.4 %collective-permute-start.8 = (bf16[176,2048]{1,0:T(8,128)(2,1)}, bf16[176,2048]{1,0:T(8,128)(2,1)}, u32[]{:S(2)}, u32[]{:S(2)}) collective-permute-start(bf16[176,2048]{1,0:T(8,128)(2,1)} %reduce-scatter.6.cloned.1.call-done.refs_0_), channel_id=1, source_target_pairs={{0,2},{1,3},{2,0},{3,1},{4,6},{5,7},{6,4},{7,5},{8,10},{9,11},{10,... | collective-permute-start | bytes 2162696 | tf_op jit(solution)/shard_map/ppermute | solution.py:711
  466.6 33.1 %collective-permute-start.7 = (bf16[176,2048]{1,0:T(8,128)(2,1)}, bf16[176,2048]{1,0:T(8,128)(2,1)}, u32[]{:S(2)}, u32[]{:S(2)}) collective-permute-start(bf16[176,2048]{1,0:T(8,128)(2,1)} %reduce-scatter.6.cloned.1.call-done.refs_0_), channel_id=1, source_target_pairs={{0,1},{1,0},{2,3},{3,2},{4,5},{5,4},{6,7},{7,6},{8,9},{9,8},{10,11... | collective-permute-start | bytes 2162696 | tf_op jit(solution)/shard_map/ppermute | solution.py:711
  467.4 48.2 %collective-permute-start.12 = (bf16[256,1408]{1,0:T(8,128)(2,1)}, bf16[256,1408]{1,0:T(8,128)(2,1)}, u32[]{:S(2)}, u32[]{:S(2)}) collective-permute-start(bf16[256,1408]{1,0:T(8,128)(2,1)} %reduce-scatter.8.cloned.1.call-done.refs_0_), channel_id=1, source_target_pairs={{0,3},{1,2},{2,1},{3,0},{4,7},{5,6},{6,5},{7,4},{8,11},{9,10},{10,... | collective-permute-start | bytes 2162696 | tf_op jit(solution)/shard_map/ppermute | solution.py:711
  468.8 57.2 %collective-permute-start.11 = (bf16[256,1408]{1,0:T(8,128)(2,1)}, bf16[256,1408]{1,0:T(8,128)(2,1)}, u32[]{:S(2)}, u32[]{:S(2)}) collective-permute-start(bf16[256,1408]{1,0:T(8,128)(2,1)} %reduce-scatter.8.cloned.1.call-done.refs_0_), channel_id=1, source_target_pairs={{0,2},{1,3},{2,0},{3,1},{4,6},{5,7},{6,4},{7,5},{8,10},{9,11},{10,... | collective-permute-start | bytes 2162696 | tf_op jit(solution)/shard_map/ppermute | solution.py:711
  496.1 30.7 %collective-permute-start.10 = (bf16[256,1408]{1,0:T(8,128)(2,1)}, bf16[256,1408]{1,0:T(8,128)(2,1)}, u32[]{:S(2)}, u32[]{:S(2)}) collective-permute-start(bf16[256,1408]{1,0:T(8,128)(2,1)} %reduce-scatter.8.cloned.1.call-done.refs_0_), channel_id=1, source_target_pairs={{0,1},{1,0},{2,3},{3,2},{4,5},{5,4},{6,7},{7,6},{8,9},{9,8},{10,11... | collective-permute-start | bytes 2162696 | tf_op jit(solution)/shard_map/ppermute | solution.py:711
  512.2 14.6 %copy-start.24 = (bf16[256,2048]{1,0:T(8,128)(2,1)S(1)}, bf16[256,2048]{1,0:T(8,128)(2,1)}, u32[]{:S(2)}) copy-start(bf16[256,2048]{1,0:T(8,128)(2,1)} %get-tuple-element.91) | copy-start | bytes 3145732
  512.2 14.6 %copy-start.30 = (bf16[256,2048]{1,0:T(8,128)(2,1)S(1)}, bf16[256,2048]{1,0:T(8,128)(2,1)}, u32[]{:S(2)}) copy-start(bf16[256,2048]{1,0:T(8,128)(2,1)} %copy-done.29) | copy-start | bytes 3145732
  530.8 59.6 %collective-permute-start.13 = (bf16[64,2048]{1,0:T(8,128)(2,1)}, bf16[64,2048]{1,0:T(8,128)(2,1)S(1)}, u32[]{:S(2)}, u32[]{:S(2)}) collective-permute-start(bf16[64,2048]{1,0:T(8,128)(2,1)} %reduce-scatter.14.cloned.1.call-done), channel_id=1, source_target_pairs={{0,0},{4,1},{8,2},{12,3},{16,4},{20,5},{24,6},{28,7},{1,8},{5,9},{... | collective-permute-start | bytes 786440 | tf_op jit(solution)/shard_map/ppermute | solution.py:1058
  635.4 14.0 %copy-start.40 = (bf16[256]{0:T(256)(128)(2,1)S(1)}, bf16[256]{0:T(256)(128)(2,1)}, u32[]{:S(2)}) copy-start(bf16[256]{0:T(256)(128)(2,1)} %param.19) | copy-start | bytes 1540
  635.4 15.7 %copy-start.34 = (bf16[4,64,2048]{2,1,0:T(8,128)(2,1)S(1)}, bf16[4,64,2048]{2,1,0:T(8,128)(2,1)}, u32[]{:S(2)}) copy-start(bf16[4,64,2048]{2,1,0:T(8,128)(2,1)} %get-tuple-element.119) | copy-start | bytes 3145732
  682.5 10.2 %copy-start.37 = (bf16[256,16]{0,1:T(8,128)(2,1)S(1)}, bf16[256,16]{0,1:T(8,128)(2,1)}, u32[]{:S(2)}) copy-start(bf16[256,16]{0,1:T(8,128)(2,1)} %param.15) | copy-start | bytes 24580
  682.5 10.8 %copy-start.42 = (bf16[256]{0:T(256)(128)(2,1)S(1)}, bf16[256]{0:T(256)(128)(2,1)}, u32[]{:S(2)}) copy-start(bf16[256]{0:T(256)(128)(2,1)} %param.13) | copy-start | bytes 1540
  682.5 14.5 %copy-start.1 = (bf16[704,2048]{1,0:T(8,128)(2,1)S(1)}, bf16[704,2048]{1,0:T(8,128)(2,1)}, u32[]{:S(2)}) copy-start(bf16[704,2048]{1,0:T(8,128)(2,1)} %param.21) | copy-start | bytes 8650756
  (20 other events, 55.9 us)
Sparse Core Ops, SparseCore 0:
  10.5 74.1 all-gather.4
  86.9 28.3 all-gather.6
  117.5 107.6 all-gather.8
  227.2 58.6 all-gather.10
  288.0 63.5 reduce-scatter.5
  354.4 63.2 reduce-scatter.7
  420.5 63.2 reduce-scatter.9
  486.6 33.9 reduce-scatter.13
  526.9 85.8 reduce-scatter.11

commit v3 on v2

v3 whole, which is shorter than its diff:
```python
import functools

import jax
import jax.numpy as jnp
from jax import lax
from jax.experimental import pallas as pl
from jax.experimental.pallas import tpu as pltpu
from jax.sharding import PartitionSpec as P

H = 16
DK = 128
EPS = 1e-06
CHUNK = 128
HEAD_ROOM = 8


def dotf(left, right, dims):
    return lax.dot_general(left, right, (dims, ((), ())), preferred_element_type=jnp.float32)


NN = ((1,), (0,))
NT = ((1,), (1,))
TN = ((0,), (0,))


def low(value):
    return value.astype(jnp.bfloat16)


def square_iota(axis):
    return lax.broadcasted_iota(jnp.int32, (CHUNK, CHUNK), axis)


def sigmoid(value):
    return 1.0 / (1.0 + jnp.exp(-value))


def conv_chunk(window, taps, count):
    mixed = window[HEAD_ROOM:] * taps[count - 1]
    for back in range(1, count):
        mixed = mixed + pltpu.roll(window, back, 0)[HEAD_ROOM:] * taps[count - 1 - back]
    return mixed


def window_of(ahead_ref, proj_ref, chunk, column):
    lanes = pl.ds(column, DK)
    before = ahead_ref[:, lanes].astype(jnp.float32)[8:]
    before = jnp.where(chunk > 0, before, 0.0)
    return jnp.concatenate([before, proj_ref[:, lanes].astype(jnp.float32)], axis=0)


def head_inputs(ahead_ref, proj_ref, table_ref, chunk, head, heads, taps):
    wide = heads * DK
    found = []
    for part in range(3):
        window = window_of(ahead_ref, proj_ref, chunk, part * wide + head * DK)
        weights = [
            table_ref[pl.ds(part * taps + tap, 1), pl.ds(head * DK, DK)] for tap in range(taps)
        ]
        mixed = conv_chunk(window, weights, taps)
        gate = sigmoid(mixed)
        found.append((window, weights, mixed, gate, mixed * gate))
    active_key = found[1][4]
    scale = lax.rsqrt(jnp.sum(active_key * active_key, axis=-1, keepdims=True) + EPS)
    key = active_key * scale
    return found, found[0][4] * DK**-0.5, key, scale, found[2][4]


def inverses_of(stricts):
    row, column = square_iota(0), square_iota(1)
    eye = (row == column).astype(jnp.float32)
    solved = [eye - jnp.where(row // 2 == column // 2, strict, 0.0) for strict in stricts]
    half = 2
    while half < CHUNK:
        below = (row // (2 * half) == column // (2 * half)) & (row // half != column // half)
        off = [low(jnp.where(below, strict, 0.0)) for strict in stricts]
        known = [low(item) for item in solved]
        first = [low(dotf(k, o, NN)) for k, o in zip(known, off)]
        second = [dotf(p, k, NN) for p, k in zip(first, known)]
        solved = [item - change for item, change in zip(solved, second)]
        half *= 2
    return [low(item) for item in solved]


def forward_kernel(
    heads, taps, ahead_ref, proj_ref, logit_ref, table_ref, gain_ref,
    normed_ref, raw_ref, fresh_ref, solve_ref, state_ref, carry,
):
    every = range(heads)
    chunk = pl.program_id(0)

    @pl.when(chunk == 0)
    def _():
        carry[...] = jnp.zeros_like(carry)

    row, column = square_iota(0), square_iota(1)
    beta_all = low(sigmoid(logit_ref[...])).astype(jnp.float32)
    beta = [beta_all[:, h : h + 1] for h in every]
    ready = [head_inputs(ahead_ref, proj_ref, table_ref, chunk, h, heads, taps) for h in every]
    query = [low(item[1]) for item in ready]
    key = [low(item[2]) for item in ready]
    value = [low(item[4]) for item in ready]
    gram = [dotf(key[h], key[h], NT) for h in every]
    score = [dotf(query[h], key[h], NT) for h in every]
    strict = [jnp.where(row > column, gram[h] * beta[h], 0.0) for h in every]
    within = [low(jnp.where(row >= column, score[h], 0.0)) for h in every]
    solved = inverses_of(strict)
    state = [carry[h] for h in every]
    state_low = [low(item) for item in state]
    recalled = [dotf(key[h], state_low[h], NN) for h in every]
    rest = [low(beta[h] * (value[h].astype(jnp.float32) - recalled[h])) for h in every]
    fresh = [low(dotf(solved[h], rest[h], NN)) for h in every]
    grown = [dotf(key[h], fresh[h], TN) for h in every]
    for h in every:
        carry[h] = state[h] + grown[h]
    past = [dotf(query[h], state_low[h], NN) for h in every]
    inner = [dotf(within[h], fresh[h], NN) for h in every]
    for h in every:
        lanes = pl.ds(h * DK, DK)
        raw = low(past[h] + inner[h])
        wide_raw = raw.astype(jnp.float32)
        normed = wide_raw * lax.rsqrt(
            jnp.mean(wide_raw * wide_raw, axis=-1, keepdims=True) + EPS
        )
        normed_ref[:, lanes] = low(normed * gain_ref[...])
        raw_ref[:, lanes] = raw
        fresh_ref[:, lanes] = fresh[h]
        solve_ref[0, h] = solved[h]
        state_ref[0, h] = state_low[h]


def backward_kernel(
    heads, taps, ahead_ref, proj_ref, logit_ref, table_ref, gain_ref, raw_ref, fresh_ref, solve_ref,
    state_ref, grad_ref, gproj_ref, gtable_ref, ggain_ref, carry, after,
):
    wide = heads * DK
    every = range(heads)
    chunk = pl.num_programs(0) - 1 - pl.program_id(0)

    @pl.when(pl.program_id(0) == 0)
    def _():
        carry[...] = jnp.zeros_like(carry)
        after[...] = jnp.zeros_like(after)
        gtable_ref[...] = jnp.zeros_like(gtable_ref)
        ggain_ref[...] = jnp.zeros_like(ggain_ref)

    row, column = square_iota(0), square_iota(1)
    beta_wide = sigmoid(logit_ref[...])
    beta_all = low(beta_wide).astype(jnp.float32)
    beta = [beta_all[:, h : h + 1] for h in every]
    lane = lax.broadcasted_iota(jnp.int32, (CHUNK, DK), 1)
    ready = [head_inputs(ahead_ref, proj_ref, table_ref, chunk, h, heads, taps) for h in every]
    query = [low(item[1]) for item in ready]
    key = [low(item[2]) for item in ready]
    value = [low(item[4]) for item in ready]
    grad_out = []
    for h in every:
        lanes = pl.ds(h * DK, DK)
        raw = raw_ref[:, lanes].astype(jnp.float32)
        grad_normed = grad_ref[:, lanes].astype(jnp.float32)
        r = lax.rsqrt(jnp.mean(raw * raw, axis=-1, keepdims=True) + EPS)
        scaled = grad_normed * gain_ref[...]
        mean = jnp.mean(scaled * raw, axis=-1, keepdims=True)
        grad_out.append(low(r * (scaled - raw * (r * r) * mean)))
        ggain_ref[...] += jnp.sum(grad_normed * raw * r, axis=0, keepdims=True)
    state = [state_ref[0, h] for h in every]
    solved = [solve_ref[0, h] for h in every]
    fresh = [fresh_ref[:, pl.ds(h * DK, DK)] for h in every]
    later = [carry[h] for h in every]
    later_low = [low(item) for item in later]
    score = [dotf(query[h], key[h], NT) for h in every]
    onward = [dotf(key[h], later_low[h], NN) for h in every]
    within = [low(jnp.where(row >= column, item, 0.0)) for item in score]
    grad_fresh = [low(dotf(within[h], grad_out[h], TN) + onward[h]) for h in every]
    grad_solved = [dotf(solved[h], grad_fresh[h], TN) for h in every]
    grad_value = [beta[h] * grad_solved[h] for h in every]
    grad_rest = [low(item) for item in grad_value]
    asked = [dotf(query[h], grad_out[h], TN) for h in every]
    taken = [dotf(key[h], grad_rest[h], TN) for h in every]
    for h in every:
        carry[h] = later[h] + asked[h] - taken[h]
    gram = [dotf(key[h], key[h], NT) for h in every]
    recalled = [dotf(key[h], state[h], NN) for h in every]
    product = [dotf(grad_out[h], fresh[h], NT) for h in every]
    cross = [dotf(low(grad_solved[h]), fresh[h], NT) for h in every]
    grad_within = [low(jnp.where(row >= column, item, 0.0)) for item in product]
    grad_strict = [jnp.where(row > column, -item, 0.0) for item in cross]
    mixing = [low(beta[h] * grad_strict[h]) for h in every]
    grad_query = [
        dotf(grad_out[h], state[h], NT) + dotf(grad_within[h], key[h], NN) for h in every
    ]
    grad_key = [
        dotf(grad_within[h], query[h], TN)
        + dotf(fresh[h], later_low[h], NT)
        - dotf(grad_rest[h], state[h], NT)
        + dotf(mixing[h], key[h], NN)
        + dotf(mixing[h], key[h], TN)
        for h in every
    ]
    glogit = jnp.zeros((CHUNK, DK), jnp.float32)
    for h in every:
        rest = value[h].astype(jnp.float32) - recalled[h]
        grad_beta = jnp.sum(grad_solved[h] * rest, axis=-1, keepdims=True) + jnp.sum(
            grad_strict[h] * gram[h], axis=-1, keepdims=True
        )
        bw = beta_wide[:, h : h + 1]
        grad_beta = low(grad_beta).astype(jnp.float32) * bw * (1.0 - bw)
        glogit = glogit + jnp.where(lane == h, grad_beta, 0.0)
    gproj_ref[:, pl.ds(3 * wide, DK)] = low(glogit)
    for h in every:
        found, _, key_wide, scale, _ = ready[h]
        lanes = pl.ds(h * DK, DK)
        back_query = low(grad_query[h]).astype(jnp.float32) * DK**-0.5
        back_key = low(grad_key[h]).astype(jnp.float32)
        back_key = scale * (
            back_key - key_wide * jnp.sum(back_key * key_wide, axis=-1, keepdims=True)
        )
        back_value = low(grad_value[h]).astype(jnp.float32)
        for part, grad_active in enumerate((back_query, back_key, back_value)):
            window, weights, mixed, gate, _ = found[part]
            grad_conv = grad_active * (gate * (1.0 + mixed * (1.0 - gate)))
            columns = pl.ds(part * wide + h * DK, DK)
            tail = jnp.concatenate([grad_conv, after[:, columns]], axis=0)
            size = CHUNK + HEAD_ROOM
            total = grad_conv * weights[taps - 1]
            for back in range(1, taps):
                ahead = pltpu.roll(tail, size - back, 0)[:CHUNK]
                total = total + ahead * weights[taps - 1 - back]
            gproj_ref[:, columns] = low(total)
            after[:, columns] = grad_conv[:HEAD_ROOM]
            for back in range(taps):
                shifted = pltpu.roll(window, back, 0)[HEAD_ROOM:] if back else window[HEAD_ROOM:]
                spot = pl.ds(part * taps + taps - 1 - back, 1)
                gtable_ref[spot, lanes] += jnp.sum(grad_conv * shifted, axis=0, keepdims=True)


def in_vmem(count):
    return [pl.BlockSpec(memory_space=pltpu.VMEM)] * count


def mix_specs(heads, wide, turn):
    ratio = CHUNK // 16
    proj = [
        pl.BlockSpec((16, 3 * wide), lambda i: (jnp.maximum(turn(i) * ratio - 1, 0), 0)),
        pl.BlockSpec((CHUNK, 3 * wide), lambda i: (turn(i), 0)),
        pl.BlockSpec((CHUNK, DK), lambda i: (turn(i), 0)),
    ]
    rows = pl.BlockSpec((CHUNK, wide), lambda i: (turn(i), 0))
    square = [
        pl.BlockSpec((1, heads, size, size), lambda i: (turn(i), 0, 0, 0)) for size in (CHUNK, DK)
    ]
    return proj, rows, square


def whole_of(shape):
    return pl.BlockSpec(shape, lambda i: (0,) * len(shape))


def mix_forward(proj, logits, table, gain):
    length = proj.shape[0]
    heads = table.shape[1] // DK
    taps = table.shape[0] // 3
    count = length // CHUNK
    wide = heads * DK
    shape = jax.ShapeDtypeStruct
    specs, rows, square = mix_specs(heads, wide, lambda i: i)
    return pl.pallas_call(
        functools.partial(forward_kernel, heads, taps),
        grid=(count,),
        out_shape=(
            shape((length, wide), jnp.bfloat16),
            shape((length, wide), jnp.bfloat16),
            shape((length, wide), jnp.bfloat16),
            shape((count, heads, CHUNK, CHUNK), jnp.bfloat16),
            shape((count, heads, DK, DK), jnp.bfloat16),
        ),
        in_specs=specs + [whole_of(table.shape), whole_of(gain.shape)],
        out_specs=(rows, rows, rows, *square),
        scratch_shapes=[pltpu.VMEM((heads, DK, DK), jnp.float32)],
        compiler_params=pltpu.CompilerParams(vmem_limit_bytes=32 * 2**20),
        cost_estimate=pl.CostEstimate(
            flops=length * heads * DK * 40000,
            bytes_accessed=16 * length * wide,
            transcendentals=3 * length * wide,
        ),
        name="mix_forward",
    )(proj, proj, logits, table, gain)


def mix_backward(proj, logits, table, gain, raw, fresh, solved, states, grad):
    length = proj.shape[0]
    heads = table.shape[1] // DK
    taps = table.shape[0] // 3
    count = length // CHUNK
    wide = heads * DK
    shape = jax.ShapeDtypeStruct

    def turn(i):
        return count - 1 - i

    specs, rows, square = mix_specs(heads, wide, turn)
    return pl.pallas_call(
        functools.partial(backward_kernel, heads, taps),
        grid=(count,),
        out_shape=(
            shape((length, 3 * wide + DK), jnp.bfloat16),
            shape((3 * taps, wide), jnp.float32),
            shape((1, DK), jnp.float32),
        ),
        in_specs=specs
        + [whole_of(table.shape), whole_of(gain.shape), rows, rows, *square, rows],
        out_specs=(
            pl.BlockSpec((CHUNK, 3 * wide + DK), lambda i: (turn(i), 0)),
            whole_of((3 * taps, wide)),
            whole_of((1, DK)),
        ),
        scratch_shapes=[
            pltpu.VMEM((heads, DK, DK), jnp.float32),
            pltpu.VMEM((HEAD_ROOM, 3 * wide), jnp.float32),
        ],
        compiler_params=pltpu.CompilerParams(vmem_limit_bytes=32 * 2**20),
        cost_estimate=pl.CostEstimate(
            flops=length * heads * DK * 40000,
            bytes_accessed=26 * length * wide,
            transcendentals=3 * length * wide,
        ),
        name="mix_backward",
    )(proj, proj, logits, table, gain, raw, fresh, solved, states, grad)


def neighbours():
    me = lax.axis_index("seq")
    return me, me + 1 - 2 * (me % 2), me + 2 - 4 * (me // 2), 3 - me


def greet(across, along):
    barrier = pltpu.get_barrier_semaphore()
    for other in (across, along):
        pl.semaphore_signal(
            barrier, inc=1, device_id={"seq": other}, device_id_type=pl.DeviceIdType.MESH
        )
    pl.semaphore_wait(barrier, 2)


def remote(source, target, send, arrive, slot, other):
    return pltpu.make_async_remote_copy(
        src_ref=source,
        dst_ref=target,
        send_sem=send.at[slot],
        recv_sem=arrive.at[slot],
        device_id={"seq": other},
        device_id_type=pl.DeviceIdType.MESH,
    )


def half_of(rows):
    return (rows // 2 + 15) // 16 * 16


def gather_copies(source, target, near, send, arrive, keep):
    me, across, along, _ = near
    return (
        pltpu.make_async_copy(source, target.at[me], keep),
        remote(source, target.at[me], send, arrive, 0, across),
        remote(source, target.at[me], send, arrive, 1, along),
    )


def gather_start(source, target, near, send, arrive, keep):
    started = gather_copies(source, target, near, send, arrive, keep)
    for copy in started:
        copy.start()
    return started


def gather_finish(started, target, near, send, arrive):
    _, across, along, _ = near
    own, first, second = started
    rows = target.shape[1]
    split = half_of(rows)
    head, rest = pl.ds(0, split), pl.ds(split, rows - split)
    first.wait_recv()
    third = remote(target.at[across, head], target.at[across, head], send, arrive, 2, along)
    third.start()
    second.wait_recv()
    fourth = remote(target.at[along, rest], target.at[along, rest], send, arrive, 3, across)
    fourth.start()
    third.wait_recv()
    fourth.wait_recv()
    for copy in (first, second, third, fourth):
        copy.wait_send()
    own.wait()


def gather_kernel(count, inputs, outputs, body, *refs):
    sources, operands = refs[:count], refs[count : count + inputs]
    targets = refs[count + inputs : 2 * count + inputs]
    results = refs[2 * count + inputs : 2 * count + inputs + outputs]
    send, arrive, keep = refs[2 * count + inputs + outputs :]
    near = neighbours()

    def copies(i):
        return gather_copies(sources[i], targets[i], near, send.at[i], arrive.at[i], keep.at[i])

    @pl.when(pl.program_id(0) == 0)
    def _():
        greet(near[1], near[2])
        for i in range(count):
            for copy in copies(i):
                copy.start()

    body(*operands, *results)

    @pl.when(pl.program_id(0) == pl.num_programs(0) - 1)
    def _():
        for i in range(count):
            gather_finish(copies(i), targets[i], near, send.at[i], arrive.at[i])


def nothing(*refs):
    del refs


def beside_gather(number, blocks, work=(nothing, "gather", (1,), [], [], [], [])):
    side, count = lax.axis_size("seq"), len(blocks)
    body, name, grid, out_shape, in_specs, out_specs, operands = work
    if side != 4 and not operands:
        return [lax.all_gather(block, "seq", axis=0) for block in blocks], []
    if side != 4:
        results = pl.pallas_call(
            body, grid=grid, out_shape=out_shape, in_specs=in_specs, out_specs=out_specs, name=name
        )(*operands)
        return [lax.all_gather(block, "seq", axis=0) for block in blocks], results
    anywhere = [pl.BlockSpec(memory_space=pl.ANY)] * count
    moved = sum(block.size for block in blocks)
    results = pl.pallas_call(
        functools.partial(gather_kernel, count, len(operands), len(out_shape), body),
        grid=grid,
        out_shape=[
            jax.ShapeDtypeStruct((side,) + block.shape, block.dtype) for block in blocks
        ]
        + out_shape,
        in_specs=anywhere + in_specs,
        out_specs=anywhere + out_specs,
        scratch_shapes=[
            pltpu.SemaphoreType.DMA((count, 4)),
            pltpu.SemaphoreType.DMA((count, 4)),
            pltpu.SemaphoreType.DMA((count,)),
        ],
        compiler_params=pltpu.CompilerParams(
            collective_id=number, has_side_effects=True, vmem_limit_bytes=40 * 2**20
        ),
        cost_estimate=pl.CostEstimate(flops=0, bytes_accessed=160 * moved, transcendentals=0),
        name=name,
    )(*blocks, *operands)
    return results[:count], results[count:]


def signal_all(peers):
    barrier = pltpu.get_barrier_semaphore()
    for peer in peers:
        pl.semaphore_signal(barrier, inc=1, device_id=peer, device_id_type=pl.DeviceIdType.MESH)
    pl.semaphore_wait(barrier, len(peers))


def send_share(row, first, where, mine, boxes, send, arrive):
    axis, spot, size = where
    copies = []
    for step in range(1, size):
        copies.append(
            pltpu.make_async_remote_copy(
                src_ref=mine.at[row],
                dst_ref=boxes.at[row, spot],
                send_sem=send.at[first + step - 1],
                recv_sem=arrive.at[first + step - 1],
                device_id={axis: (spot + step) % size},
                device_id_type=pl.DeviceIdType.MESH,
            )
        )
        copies[-1].start()
    boxes[row, spot] = mine[row]
    return copies


def add_shares(row, size, copies, boxes):
    for copy in copies:
        copy.wait()
    total = boxes[row, 0]
    for index in range(1, size):
        total = total + boxes[row, index]
    return total


def start_kernel(
    source_ref, small_ref, sources, smalls,
    send, arrive, keep, send_z, arrive_z, keep_z,
):
    near = neighbours()
    _, across, along, _ = near
    here, count = lax.axis_index("fsdp"), lax.axis_size("fsdp")
    sibling = here + 1 - 2 * (here % 2)
    others = [(here + 2 * step) % count for step in range(1, count // 2)]
    barrier = pltpu.get_barrier_semaphore()
    peers = [{"seq": across}, {"seq": along}, {"fsdp": sibling}]
    peers += [{"fsdp": other} for other in others]
    for peer in peers:
        pl.semaphore_signal(barrier, inc=1, device_id=peer, device_id_type=pl.DeviceIdType.MESH)
    pl.semaphore_wait(barrier, len(peers))

    def send_to(source, target, row, slot, other):
        return pltpu.make_async_remote_copy(
            src_ref=source,
            dst_ref=target,
            send_sem=send_z.at[row, slot],
            recv_sem=arrive_z.at[row, slot],
            device_id={"fsdp": other},
            device_id_type=pl.DeviceIdType.MESH,
        )

    flow = [(small_ref, smalls)]
    first = []
    for row, (source, target) in enumerate(flow):
        own = pltpu.make_async_copy(source, target.at[here], keep_z.at[row])
        own.start()
        copies = [send_to(source, target.at[here], row, 0, sibling)]
        copies += [
            send_to(source, target.at[here], row, 1 + i, other) for i, other in enumerate(others)
        ]
        for copy in copies:
            copy.start()
        first.append((own, copies))
    started = [
        gather_start(block, target, near, send.at[i], arrive.at[i], keep.at[i])
        for i, (block, target) in enumerate([(source_ref, sources)])
    ]
    gather_finish(started[0], sources, near, send.at[0], arrive.at[0])
    for row, (source, target) in enumerate(flow):
        own, copies = first[row]
        passed = []
        for i in range(len(others)):
            copies[1 + i].wait_recv()
            origin = target.at[(here + count - 2 * (i + 1)) % count]
            passed.append(send_to(origin, origin, row, 1 + len(others) + i, sibling))
            passed[-1].start()
        copies[0].wait_recv()
        for copy in passed:
            copy.wait_recv()
        for copy in copies + passed:
            copy.wait_send()
        own.wait()


def start_gathers(source, small):
    side, count = lax.axis_size("seq"), lax.axis_size("fsdp")
    if side != 4:
        return (
            lax.all_gather(source, "seq", axis=0),
            lax.all_gather(small, "fsdp", axis=0),
        )
    slots = count - 1
    return pl.pallas_call(
        start_kernel,
        out_shape=[
            jax.ShapeDtypeStruct((many,) + block.shape, block.dtype)
            for block, many in ((source, side), (small, count))
        ],
        in_specs=[pl.BlockSpec(memory_space=pl.ANY)] * 2,
        out_specs=[pl.BlockSpec(memory_space=pl.ANY)] * 2,
        scratch_shapes=[
            pltpu.SemaphoreType.DMA((2, 4)),
            pltpu.SemaphoreType.DMA((2, 4)),
            pltpu.SemaphoreType.DMA((2,)),
            pltpu.SemaphoreType.DMA((2, slots)),
            pltpu.SemaphoreType.DMA((2, slots)),
            pltpu.SemaphoreType.DMA((2,)),
        ],
        compiler_params=pltpu.CompilerParams(collective_id=1, has_side_effects=True),
        cost_estimate=pl.CostEstimate(
            flops=0, bytes_accessed=160 * source.size, transcendentals=0
        ),
        name="start_gathers",
    )(source, small)


TILE = 256
STEP = 16


def reduce_rows_kernel(flip, gathers, totals, fills, epilogue, lefts, in_count, out_count, *refs):
    left_refs, right_ref, extra = refs[:lefts], refs[lefts], refs[lefts + 1 : in_count]
    outs = refs[in_count : in_count + out_count]
    far, wide_x, wide_y, own, get_a, get_b, get_x, get_y, send, arrive = refs[
        in_count + out_count : in_count + out_count + 10
    ]
    rest_refs = refs[in_count + out_count + 10 :]
    near = neighbours()
    me, across, along, opposite = near
    if totals:
        mine, boxes, send_t, arrive_t = rest_refs
        spots = [(axis, lax.axis_index(axis), lax.axis_size(axis)) for axis in ("seq", "fsdp")]
        signal_all(
            [{axis: (spot + step) % size} for axis, spot, size in spots for step in range(1, size)]
        )
        mine[0] = extra[-1][...]
        shares = send_share(0, 0, spots[0], mine, boxes, send_t, arrive_t)
    else:
        greet(across, along)
    rows, width = own.shape
    split = half_of(rows)
    head, rest = pl.ds(0, split), pl.ds(split, rows - split)

    def part(block, store):
        here = pl.ds(pl.multiple_of(block * rows, rows), rows)

        @pl.loop(0, width // TILE)
        def _(tile):
            columns = pl.ds(pl.multiple_of(tile * TILE, TILE), TILE)
            value, base = 0.0, 0
            for left_ref in left_refs:
                depth = pl.ds(base, left_ref.shape[1])
                if flip:
                    value = value + dotf(left_ref[here, :], right_ref[columns, depth], NT)
                else:
                    value = value + dotf(left_ref[here, :], right_ref[depth, columns], NN)
                base += left_ref.shape[1]
            store[:, columns] = value.astype(store.dtype)

    def term(rows_ref, grads_ref, store):
        @pl.loop(0, rows_ref.shape[1] // TILE)
        def _(tile):
            columns = pl.ds(pl.multiple_of(tile * TILE, TILE), TILE)
            store[columns, :] = low(dotf(rows_ref[:, columns], grads_ref[...], TN))

    def add_into(store, base, source):
        @pl.loop(0, source.shape[0] // STEP)
        def _(index):
            start = pl.multiple_of(index * STEP, STEP)
            there = pl.ds(pl.multiple_of(base + start, STEP), STEP)
            total = store[there, :].astype(jnp.float32) + source[pl.ds(start, STEP), :].astype(
                jnp.float32
            )
            store[there, :] = low(total)

    part(opposite, far)
    if totals:
        mine[1] = add_shares(0, spots[0][2], shares, boxes)
        shares = send_share(1, spots[0][2] - 1, spots[1], mine, boxes, send_t, arrive_t)
    copies = [
        remote(far.at[head], get_a, send, arrive, 0, across),
        remote(far.at[rest], get_b, send, arrive, 1, along),
    ]
    copies[0].start()
    copies[1].start()
    part(across, wide_x)
    copies.append(remote(wide_x.at[head], get_x.at[head], send, arrive, 2, across))
    copies[2].start()
    part(along, wide_y)
    if fills:
        copies.append(remote(wide_y.at[rest], get_y.at[rest], send, arrive, 3, along))
        copies[3].start()
        term(extra[1], extra[2], outs[1])
    else:
        copies.append(remote(wide_y.at[rest], get_y.at[rest], send, arrive, 3, along))
        copies[3].start()
    copies[0].wait_recv()
    add_into(wide_y, 0, get_a)
    copies.append(remote(wide_y.at[head], get_y.at[head], send, arrive, 4, along))
    copies[4].start()
    copies[1].wait_recv()
    add_into(wide_x, split, get_b)
    copies.append(remote(wide_x.at[rest], get_x.at[rest], send, arrive, 5, across))
    copies[5].start()
    if fills:
        term(extra[1], extra[3], outs[2])
    part(me, own)
    for copy in copies[2:]:
        copy.wait_recv()
    epilogue_prepare = rest_refs[0] if gathers else None

    @pl.loop(0, rows // STEP)
    def _(index):
        here = pl.ds(pl.multiple_of(index * STEP, STEP), STEP)
        total = (
            own[here, :] + get_x[here, :].astype(jnp.float32) + get_y[here, :].astype(jnp.float32)
        )
        epilogue(index, here, total, extra, outs, epilogue_prepare)

    for copy in copies:
        copy.wait_send()
    if totals:
        outs[-1][...] = add_shares(1, spots[1][2], shares, boxes)
    if gathers:
        block, send_2, arrive_2, keep = rest_refs
        target = outs[0]
        started = gather_start(block, target, near, send_2, arrive_2, keep.at[0])
        gather_finish(started, target, near, send_2, arrive_2)


def rms_back(grad, values, gain):
    r = lax.rsqrt(jnp.mean(values * values, axis=-1, keepdims=True) + EPS)
    scaled = grad * gain
    change = r * (scaled - values * (r * r) * jnp.mean(scaled * values, axis=-1, keepdims=True))
    return change


def middle_epilogue(index, here, total, extra, outs, block):
    source_ref, gain_ref = extra
    middle = source_ref[here, :].astype(jnp.float32) + total
    outs[1][here, :] = middle
    r = lax.rsqrt(jnp.mean(middle * middle, axis=-1, keepdims=True) + EPS)
    block[here, :] = low(middle * r * gain_ref[...])


def output_epilogue(index, here, total, extra, outs, block):
    outs[0][here, :] = low(extra[0][here, :] + total)


def branch_epilogue(index, here, total, extra, outs, block):
    middle_ref, upstream_ref, gain_ref = extra
    change = rms_back(total, middle_ref[here, :], gain_ref[...])
    grad = upstream_ref[here, :].astype(jnp.float32) + change
    outs[1][here, :] = grad
    block[here, :] = low(grad)


def input_epilogue(index, here, total, extra, outs, block):
    source_ref, carried_ref, gain_ref, _ = extra
    change = rms_back(total, source_ref[here, :].astype(jnp.float32), gain_ref[...])
    outs[0][here, :] = carried_ref[here, :] + change


def fused_reduce(name, number, flip, mode, epilogue, outs, lefts, right, *extra):
    gathers, totals = mode == "gather", mode == "total"
    side = lax.axis_size("seq")
    length = lefts[0].shape[0]
    rows = length // side
    width = right.shape[0] if flip else right.shape[1]
    split = half_of(rows)
    scratch = [
        pltpu.VMEM((rows, width), jnp.bfloat16),
        pltpu.VMEM((rows, width), jnp.bfloat16),
        pltpu.VMEM((rows, width), jnp.bfloat16),
        pltpu.VMEM((rows, width), jnp.float32),
        pltpu.VMEM((split, width), jnp.bfloat16),
        pltpu.VMEM((rows - split, width), jnp.bfloat16),
        pltpu.VMEM((rows, width), jnp.bfloat16),
        pltpu.VMEM((rows, width), jnp.bfloat16),
        pltpu.SemaphoreType.DMA((6,)),
        pltpu.SemaphoreType.DMA((6,)),
    ]
    out_specs = in_vmem(len(outs))
    if totals:
        shape, f_count = extra[-1].shape, lax.axis_size("fsdp")
        peers = side + f_count - 2
        scratch += [
            pltpu.VMEM((2,) + shape, jnp.float32),
            pltpu.VMEM((2, max(side, f_count)) + shape, jnp.float32),
            pltpu.SemaphoreType.DMA((peers,)),
            pltpu.SemaphoreType.DMA((peers,)),
        ]
    if gathers:
        scratch += [
            pltpu.VMEM((rows, width), jnp.bfloat16),
            pltpu.SemaphoreType.DMA((4,)),
            pltpu.SemaphoreType.DMA((4,)),
            pltpu.SemaphoreType.DMA((1,)),
        ]
        out_specs[0] = pl.BlockSpec(memory_space=pl.ANY)
    return pl.pallas_call(
        functools.partial(
            reduce_rows_kernel,
            flip,
            gathers,
            totals,
            mode == "fill",
            epilogue,
            len(lefts),
            len(lefts) + 1 + len(extra),
            len(outs),
        ),
        out_shape=outs,
        in_specs=in_vmem(len(lefts) + 1 + len(extra)),
        out_specs=out_specs,
        scratch_shapes=scratch,
        compiler_params=pltpu.CompilerParams(
            collective_id=number, has_side_effects=True, vmem_limit_bytes=56 * 2**20
        ),
        cost_estimate=pl.CostEstimate(
            flops=2 * sum(left.size for left in lefts) * width,
            bytes_accessed=(320 if gathers else 160) * rows * width,
            transcendentals=0,
        ),
        name=name,
    )(*lefts, right, *extra)


def seq_sum(partial, side):
    block = low(partial).reshape(side, -1, partial.shape[-1])
    return lax.psum_scatter(block, "seq", scatter_dimension=0).astype(jnp.float32)


def out_and_norm(attn_in, weight, source, gain):
    side = lax.axis_size("seq")
    rows, width = source.shape
    if side != 4:
        middle = source.astype(jnp.float32) + seq_sum(dotf(attn_in, weight, NN), side)
        r = lax.rsqrt(jnp.mean(middle * middle, axis=-1, keepdims=True) + EPS)
        return lax.all_gather(low(middle * r * gain), "seq", axis=0), middle
    outs = (
        jax.ShapeDtypeStruct((side, rows, width), jnp.bfloat16),
        jax.ShapeDtypeStruct((rows, width), jnp.float32),
    )
    return fused_reduce(
        "out_and_norm", 2, False, "gather", middle_epilogue, outs, [attn_in], weight, source, gain
    )


def place_kernel(side, *refs):
    target_ref = refs[side]
    me = lax.axis_index("seq")
    for spot in range(side):

        @pl.when(me == spot)
        def _():
            for index in range(side):
                target_ref[index] = refs[index ^ spot][...].astype(target_ref.dtype)


def place_work(blocks, kind):
    side = len(blocks)
    rows, width = blocks[0].shape
    tile = 512
    return (
        functools.partial(place_kernel, side),
        "place",
        (width // tile,),
        [jax.ShapeDtypeStruct((side, rows, width), kind)],
        [pl.BlockSpec((rows, tile), lambda i: (0, i))] * side,
        [pl.BlockSpec((side, rows, tile), lambda i: (0, 0, i))],
        blocks,
    )


def place(blocks, kind):
    body, name, grid, out_shape, in_specs, out_specs, operands = place_work(blocks, kind)
    return pl.pallas_call(
        body, grid=grid, out_shape=out_shape, in_specs=in_specs, out_specs=out_specs, name=name
    )(*operands)[0]


def swap(block, step):
    pairs = [(i, i ^ step) for i in range(lax.axis_size("seq"))]
    return lax.ppermute(block, "seq", pairs)


def down_and_terms(hidden, weight, middle, ffn_in, grads):
    side = lax.axis_size("seq")
    if side != 4:
        output = low(middle + seq_sum(dotf(hidden, weight, NN), side))
        return output, *[low(dotf(ffn_in, grad, TN)) for grad in grads]
    term = jax.ShapeDtypeStruct((ffn_in.shape[1], grads[0].shape[1]), jnp.bfloat16)
    outs = (jax.ShapeDtypeStruct(middle.shape, jnp.bfloat16), term, term)
    return fused_reduce(
        "down_and_terms", 3, False, "fill", output_epilogue, outs, [hidden], weight, middle, ffn_in,
        *grads,
    )


def branch_grad(grads, weight, middle, upstream, gain):
    side = lax.axis_size("seq")
    rows, width = middle.shape
    if side != 4:
        grad = jnp.concatenate(grads, axis=1)
        change = rms_back(seq_sum(dotf(grad, weight, NT), side), middle, gain)
        total = upstream.astype(jnp.float32) + change
        return lax.all_gather(low(total), "seq", axis=0), total
    outs = (
        jax.ShapeDtypeStruct((side, rows, width), jnp.bfloat16),
        jax.ShapeDtypeStruct((rows, width), jnp.float32),
    )
    return fused_reduce(
        "branch_grad", 4, True, "gather", branch_epilogue, outs, grads, weight, middle, upstream, gain
    )


def input_grad(grad, weight, source, carried, gain, value):
    side = lax.axis_size("seq")
    if side != 4:
        partial = dotf(grad, weight[:, : grad.shape[1]], NT)
        change = rms_back(seq_sum(partial, side), source.astype(jnp.float32), gain)
        return carried + change, lax.psum(value, ("fsdp", "seq"))
    outs = (
        jax.ShapeDtypeStruct(carried.shape, jnp.float32),
        jax.ShapeDtypeStruct(value.shape, jnp.float32),
    )
    return fused_reduce(
        "input_grad", 5, True, "total", input_epilogue, outs, [grad], weight, source, carried, gain,
        value,
    )


def pick_kernel(side, share, source_ref, target_ref):
    me = lax.axis_index("seq")
    count = target_ref.shape[1] // share
    for index in range(side):

        @pl.when(me == index)
        def _():
            pieces = [
                source_ref[:, pl.ds((k * side + index) * share, share)].astype(jnp.float32)
                for k in range(count)
            ]
            target_ref[...] = low(jnp.concatenate(pieces, axis=1))


def pick_columns(weight, share):
    side = lax.axis_size("seq")
    rows, width = weight.shape
    tile = 32
    return pl.pallas_call(
        functools.partial(pick_kernel, side, share),
        grid=(rows // tile,),
        out_shape=jax.ShapeDtypeStruct((rows, width // side), weight.dtype),
        in_specs=[pl.BlockSpec((tile, width), lambda i: (i, 0))],
        out_specs=pl.BlockSpec((tile, width // side), lambda i: (i, 0)),
        name="pick_columns",
    )(weight)


def spread_kernel(side, share, *refs):
    gate_refs, (up_ref, weight_ref, target_ref, total_ref) = refs[:side], refs[side:]
    count = up_ref.shape[2] // share
    me = lax.axis_index("seq")
    half = target_ref.shape[1] // 2

    def place(pieces, base):
        grad = jnp.concatenate([piece.astype(jnp.float32) for piece in pieces], axis=1)
        target_ref[:, pl.ds(base, half)] = low(grad)
        weight = weight_ref[:, pl.ds(base, half)].astype(jnp.float32)
        return jnp.sum(grad * weight, axis=1, keepdims=True)

    spans = [(pl.ds(k * share, share), index) for k in range(count) for index in range(side)]
    total = place([up_ref[index, :, span] for span, index in spans], half)
    for spot in range(side):

        @pl.when(me == spot)
        def _():
            whole = total + place([gate_refs[index ^ spot][:, span] for span, index in spans], 0)
            total_ref[...] = jnp.broadcast_to(whole, total_ref.shape)


def spread_work(gates, up, weight, share):
    side, rows, width = up.shape
    tile = 32
    by_row = pl.BlockSpec((tile, 2 * width * side), lambda i: (i, 0))
    return (
        functools.partial(spread_kernel, side, share),
        "spread",
        (rows // tile,),
        [
            jax.ShapeDtypeStruct((rows, 2 * width * side), jnp.bfloat16),
            jax.ShapeDtypeStruct((rows, DK), jnp.float32),
        ],
        [pl.BlockSpec((tile, width), lambda i: (i, 0))] * side
        + [pl.BlockSpec((side, tile, width), lambda i: (0, i, 0)), by_row],
        [by_row, pl.BlockSpec((tile, DK), lambda i: (i, 0))],
        [*gates, up, weight],
    )


def assemble_kernel(
    side, wide, taps, grad_ref, weight_ref, beta_ref, target_ref, total_ref, rest_ref
):
    heads = wide // DK
    total = 0.0
    for part in range(3):
        for index in range(side):
            columns = pl.ds((part * side + index) * wide, wide)
            grad = grad_ref[index, :, pl.ds(part * wide, wide)].astype(jnp.float32)
            target_ref[:, columns] = grad
            weight = weight_ref[:, columns].astype(jnp.float32)
            total = total + jnp.sum(grad * weight, axis=1, keepdims=True)
    lane = lax.broadcasted_iota(jnp.int32, beta_ref.shape, 1)
    beta, conv = 0.0, 0.0
    for index in range(side):
        rest = grad_ref[index, :, pl.ds(3 * wide, DK)].astype(jnp.float32)
        mine = jnp.where(lane < heads, rest, 0.0)
        beta = beta + (pltpu.roll(mine, index * heads, 1) if index else mine)
        conv = conv + rest
    conv = jnp.where((lane >= heads) & (lane < heads + 3 * taps), conv, 0.0)
    if side > 1:
        conv = pltpu.roll(conv, H - heads, 1)
    total = total + jnp.sum(beta * beta_ref[...].astype(jnp.float32), axis=1, keepdims=True)
    total_ref[...] = jnp.broadcast_to(total, total_ref.shape)
    rest_ref[...] = (beta + conv).T


def assemble_columns(grad, weight, beta, wide, taps):
    side, rows, depth = grad.shape
    tile = min(rows, DK)
    by_row = pl.BlockSpec((tile, weight.shape[1]), lambda i: (i, 0))
    narrow = pl.BlockSpec((tile, DK), lambda i: (i, 0))
    return pl.pallas_call(
        functools.partial(assemble_kernel, side, wide, taps),
        grid=(rows // tile,),
        out_shape=(
            jax.ShapeDtypeStruct(weight.shape, jnp.float32),
            jax.ShapeDtypeStruct((rows, DK), jnp.float32),
            jax.ShapeDtypeStruct((DK, rows), jnp.float32),
        ),
        in_specs=[pl.BlockSpec((side, tile, depth), lambda i: (0, i, 0)), by_row, narrow],
        out_specs=(by_row, narrow, pl.BlockSpec((DK, tile), lambda i: (0, i))),
        compiler_params=pltpu.CompilerParams(vmem_limit_bytes=40 * 2**20),
        name="assemble_columns",
    )(grad, weight, beta)


def fsdp_sum(term):
    return lax.psum_scatter(low(term), "fsdp", scatter_dimension=0, tiled=True)


def per_device(
    inputs,
    cotangent,
    norm1_gain,
    w_qkv,
    w_beta,
    conv_weight,
    out_gain,
    w_out,
    norm2_gain,
    w_gate_up,
    w_down,
):
    side = lax.axis_size("seq")
    s = lax.axis_index("seq")
    shape = inputs.shape
    width = shape[2]
    source = inputs.reshape(-1, width)
    upstream = cotangent.reshape(-1, width)
    length = source.shape[0] * side
    heads = H // side
    wide = heads * DK
    rows = w_qkv.shape[0]
    share = w_down.shape[0] // side
    taps = conv_weight.shape[1] // 3

    f_count = lax.axis_size("fsdp")
    depth = 3 * wide + DK
    homes = [
        (f * side + i, (side * (f % 2) + i) * side + f // 2)
        for f in range(f_count)
        for i in range(side)
    ]
    strip = rows // side

    def everywhere(block):
        return lax.all_gather(block, "fsdp", axis=0, tiled=True)

    parts = [
        lax.dynamic_slice_in_dim(w_qkv, part * width + s * wide, wide, 1) for part in range(3)
    ]
    beta_part = lax.dynamic_slice_in_dim(w_beta, s * heads, heads, 1)
    parts.append(jnp.pad(beta_part, ((0, 0), (0, DK - heads))))
    qkv_part = everywhere(jnp.concatenate(parts, axis=1))
    small = jnp.concatenate([norm1_gain[None], norm2_gain[None], conv_weight.T], axis=0)
    small = jnp.pad(small, ((0, 16 - small.shape[0]), (0, 0)))
    piece = lax.dynamic_slice_in_dim(w_out, s * strip, strip, 0)
    piece = lax.ppermute(piece, ("fsdp", "seq"), homes)
    source_all, small = start_gathers(source, small)
    sent, source_all = lax.optimization_barrier((upstream, source_all))
    out_part = everywhere(piece)
    upstreams = [upstream] + [swap(sent, step) for step in range(1, side)]
    small = small.transpose(1, 0, 2).reshape(small.shape[1], width).astype(jnp.float32)
    gain_first = small[0:1]
    gain_second = small[1:2]
    table = lax.dynamic_slice_in_dim(small[2 : 2 + 3 * taps], s * wide, wide, 1)
    gain_heads = out_gain.astype(jnp.float32)[None]
    source_all = source_all.reshape(length, width).astype(jnp.float32)

    picked = pick_columns(w_gate_up, share)
    gate_up_part = everywhere(picked)
    down_part = everywhere(lax.dynamic_slice_in_dim(w_down, s * share, share, 0))

    normed_first = low(
        source_all
        * lax.rsqrt(jnp.mean(source_all * source_all, axis=-1, keepdims=True) + EPS)
        * gain_first
    )
    projected = low(dotf(normed_first, qkv_part[:, : 3 * wide], NN))
    beta_logits = dotf(normed_first, qkv_part[:, 3 * wide : depth], NN)
    attn_in, *kept = mix_forward(projected, beta_logits, table, gain_heads)
    attn_in, *upstreams = lax.optimization_barrier((attn_in, *upstreams))
    upstream_all = place(upstreams, jnp.bfloat16).reshape(length, width)
    ffn_in, middle = out_and_norm(attn_in, out_part, source, gain_second)
    ffn_in = ffn_in.reshape(length, width)
    gate_up = dotf(ffn_in, gate_up_part, NN)
    hidden_width = gate_up.shape[1] // 2
    gate = gate_up[:, :hidden_width]
    upward = gate_up[:, hidden_width:]
    sigma = jax.nn.sigmoid(gate)
    hidden = low(gate * sigma * upward)

    down_term = low(dotf(hidden, upstream_all, TN))
    grad_down = fsdp_sum(down_term)
    upstream_all, _ = lax.optimization_barrier((upstream_all, down_term))
    grad_hidden = dotf(upstream_all, down_part, NT)
    grad_gate = low(grad_hidden * upward * sigma * (1.0 + gate * (1.0 - sigma)))
    grad_up = low(grad_hidden * gate * sigma)
    output, gate_term, up_term = down_and_terms(
        hidden, down_part, middle, ffn_in, [grad_gate, grad_up]
    )
    gate_sum = fsdp_sum(gate_term)
    up_sum = fsdp_sum(up_term)
    grad_gate, grad_up, grad_down = lax.optimization_barrier((grad_gate, grad_up, grad_down))
    grad_branch, grad_middle = branch_grad(
        [grad_gate, grad_up], gate_up_part, middle, upstream, gain_second
    )
    grad_branch, grad_down, gate_sum = lax.optimization_barrier(
        (grad_branch, grad_down, gate_sum)
    )
    grad_branch = grad_branch.reshape(length, width)
    downs = [grad_down] + [swap(grad_down, step) for step in range(1, side)]
    gates = [gate_sum] + [swap(gate_sum, step) for step in range(1, side)]

    out_term = low(dotf(attn_in, grad_branch, TN))
    grad_attn_in, _ = lax.optimization_barrier((dotf(grad_branch, out_part, NT), out_term))
    grad_proj, grad_table, grad_gain_heads = mix_backward(
        projected, beta_logits, table, gain_heads, *kept, grad_attn_in
    )
    grad_proj, up_sum, *downs = lax.optimization_barrier((grad_proj, up_sum, *downs))
    grad_qkv = low(dotf(normed_first, grad_proj, TN))
    grad_qkv = lax.dynamic_update_slice(
        grad_qkv, low(grad_table.T), (s * wide, 3 * wide + heads)
    )
    grad_down = place(downs, jnp.float32)
    grad_proj, grad_qkv, out_term, grad_down, *gates = lax.optimization_barrier(
        (grad_proj, grad_qkv, out_term, grad_down, *gates)
    )
    grad_qkv = fsdp_sum(grad_qkv)
    grad_input, grad_out_gain = input_grad(
        grad_proj, qkv_part, source, grad_middle, gain_first,
        jnp.broadcast_to(grad_gain_heads, (8, DK)),
    )
    up_sum, grad_input = lax.optimization_barrier((up_sum, grad_input))
    (up_sum,), _ = beside_gather(7, [up_sum])
    out_term, grad_qkv, up_sum = lax.optimization_barrier((out_term, grad_qkv, up_sum))
    out_sum = fsdp_sum(out_term)
    (grad_qkv,), (grad_w_gate_up, second_total) = beside_gather(
        9, [grad_qkv], spread_work(gates, up_sum, w_gate_up, share)
    )
    out_sum = lax.ppermute(out_sum, ("fsdp", "seq"), [(b, a) for a, b in homes])
    (grad_w_out,), _ = beside_gather(8, [out_sum])
    wide_beta = jnp.pad(w_beta, ((0, 0), (0, DK - H)))
    grad_w_qkv, first_total, rest = assemble_columns(grad_qkv, w_qkv, wide_beta, wide, taps)
    return (
        output.reshape(shape),
        grad_input.reshape(shape),
        first_total[:, 0] / norm1_gain.astype(jnp.float32),
        grad_w_qkv,
        rest[:H].T,
        rest[H : H + 3 * taps].T,
        grad_out_gain[0],
        grad_w_out.reshape(rows, width).astype(jnp.float32),
        second_total[:, 0] / norm2_gain.astype(jnp.float32),
        grad_w_gate_up.astype(jnp.float32),
        grad_down.reshape(side * share, width),
    )


def solution(mesh):
    by_row = P("fsdp", None)
    tokens = P("fsdp", "seq", None)
    specs = (tokens, tokens, P("fsdp"), by_row, by_row, by_row, P(), by_row, P("fsdp"))
    specs = specs + (by_row, by_row)
    return jax.shard_map(per_device, mesh=mesh, in_specs=specs, out_specs=specs, check_vma=False)
```

time: 709 us -> 668 us (0.942)
  waiting for transfers between devices: 80.8 us -> 37.7 us
  Pallas kernels: 427 us -> 470 us
  matrix products: 110 us -> 78.8 us
    ppermute x12 -> x9, waiting for transfers between devices: 46.8 us -> 0.9 us  [swap(): return lax.ppermute(block, 'seq', pairs)]
    pallas_call x11 -> x12, Pallas kernels: 357 us -> 400 us  [the longest x4 268 us: fused_reduce(): pl.pallas_call(functools.partial(reduce_rows_kernel, flip, gathers, total...]
    dot_general x11 -> x8, matrix products: 110 us -> 78.8 us  [dotf(): lax.dot_general(left, right, (dims, ((), ())), preferred_element_type=jnp...]
    convert_element_type x1, other arithmetic: 0.99 us -> 8.42 us  [per_device(): grad_w_gate_up.astype(jnp.float32)]
    ppermute x12 -> x9, starting transfers between devices: 15.2 us -> 10.7 us  [swap(): return lax.ppermute(block, 'seq', pairs)]
    unnamed x96 -> x82, local copies, waits for them, and re-layouts: 20.5 us -> 17.4 us
  transfers between devices with their start and end apart: 23 -> 20, of which waited for: 8 -> 4; matrix products, arithmetic and copies ran while one was open for 19% -> 16% of each run, Pallas kernels for 55% -> 68%
where the time goes in v3:
time: 668 us; the launch traced here: 664 us
  Pallas kernels  470 us (70%)
  matrix products  78.8 us (12%)
  waiting for transfers between devices  37.7 us (6%)
  local copies, waits for them, and re-layouts  28 us (4%)
  other arithmetic  21.2 us (3%)
  between operations  14.6 us (2%)
  starting transfers between devices  13.3 us (2%)
    pallas_call x4, Pallas kernels, fused_reduce(): pl.pallas_call(functools.partial(reduce_rows_kernel, flip, gathers, total...  268 us
    dot_general x8, matrix products, dotf(): lax.dot_general(left, right, (dims, ((), ())), preferred_element_type=jnp...  78.8 us
    pallas_call x3, Pallas kernels, beside_gather(): pl.pallas_call(functools.partial(gather_kernel, count, len(operands), len...  77.5 us
    pallas_call x1, Pallas kernels, start_gathers(): pl.pallas_call(start_kernel, out_shape=[jax.ShapeDtypeStruct((many,) + bl...  63.2 us
    all_gather x4, waiting for transfers between devices, everywhere(): return lax.all_gather(block, 'fsdp', axis=0, tiled=True)  33.9 us
    pallas_call x1, Pallas kernels, mix_forward(): pl.pallas_call(functools.partial(forward_kernel, heads, taps), grid=(coun...  22.1 us
    pallas_call x1, Pallas kernels, mix_backward(): pl.pallas_call(functools.partial(backward_kernel, heads, taps), grid=(cou...  18.6 us
    unnamed x82, local copies, waits for them, and re-layouts  17.4 us
  transfers between devices with their start and end apart: 20, of which 4 were waited for; matrix products, arithmetic and copies ran while one was open for 16% of the time, Pallas kernels for 68%

profile of v3, /device:TPU:0, one launch (start us, length us, event | category | flops | bytes accessed | tf_op | source)
XLA Modules:
  0.0 663.5 jit_solution(5609544004261139621)
XLA Ops:
  8.3 1.2 constant_dynamic-slice_fusion.6
  13.0 6.7 %pick_columns.1 = bf16[256,2816]{1,0:T(8,128)(2,1)} custom-call(bf16[256,11264]{1,0:T(8,128)(2,1)} %refs_6_.1), custom_call_target="tpu_custom_call" | custom-call | tf_op jit(solution)/shard_map/pick_columns/pallas_call | solution.py:920
  20.5 63.2 %start_gathers.1 = (bf16[4,256,2048]{2,1,0:T(8,128)(2,1)}, bf16[8,16,256]{2,1,0:T(8,128)(2,1)}) custom-call(bf16[256,2048]{1,0:T(8,128)(2,1)} %bitcast.59, bf16[16,256]{1,0:T(8,128)(2,1)} %fusion.15.small_ref), custom_call_target="tpu_custom_call" | custom-call | bytes 83886080 | tf_op jit(solution)/shard_map/start_gathers/pallas_call | solution.py:561
  83.6 1.5 collective-permute-start.2
  85.1 2.1 collective-permute-start
  89.9 3.1 multiply_reduce_fusion
  93.1 3.0 fusion.1
  96.2 11.0 %fusion.4.ahead_ref.proj_ref = bf16[1024,1536]{1,0:T(8,128)(2,1)S(1)} fusion(bf16[1024,2048]{1,0:T(8,128)(2,1)} %fusion.1, bf16[2048,1664]{1,0:T(8,128)(2,1)} %all-gather.5.cloned.1.call-done.refs_1_), kind=kOutput, calls=%fused_computation.12 | convolution fusion | flops 6444023808 | bytes 13631488 | tf_op jit(solution)/shard_map/dot_general | solution.py:18
  107.2 2.7 fusion.9.logit_ref
  109.9 22.1 %mix_forward.1 = (bf16[1024,512]{1,0:T(8,128)(2,1)S(1)}, bf16[1024,512]{1,0:T(8,128)(2,1)S(1)}, bf16[1024,512]{1,0:T(8,128)(2,1)S(1)}, bf16[8,4,128,128]{3,2,1,0:T(8,128)(2,1)S(1)}, bf16[8,4,128,128]{3,2,1,0:T(8,128)(2,1)S(1)}) custom-call(bf16[1024,1536]{1,0:T(8,128)(2,1)S(1)} %fusion.4.ahead_ref.proj_ref, bf16[1024,1536]{1,0:T(8,128)(2,1)S(1)} %fusion.4.ahead_ref.proj_ref, ...), custom_call_target="tpu_custom_call" | custom-call | flops 20971520000 | bytes 8388608 | tf_op jit(solution)/shard_map/mix_forward/pallas_call | solution.py:267
  134.1 1.1 copy-done.19
  135.1 5.5 place.2
  140.7 78.4 %out_and_norm.1 = (bf16[4,256,2048]{2,1,0:T(8,128)(2,1)}, f32[256,2048]{1,0:T(8,128)}) custom-call(bf16[1024,512]{1,0:T(8,128)(2,1)} %copy-done.8, bf16[512,2048]{1,0:T(8,128)(2,1)} %all-gather.7.cloned.1.call-done.refs_1_, bf16[256,2048]{1,0:T(8,128)(2,1)} %bitcast.60, f32[1,2048]{1,0:T(1,128)} %bitcast.75), custom_call_target="tpu_custom_call" | custom-call | flops 2147483648 | bytes 167772160 | tf_op jit(solution)/shard_map/out_and_norm/pallas_call | solution.py:769
  219.1 6.1 all-gather.9.cloned.1.call-done.refs_2_
  225.2 17.2 %fusion.17 = f32[1024,2816]{1,0:T(8,128)S(1)} fusion(bf16[1024,2048]{1,0:T(8,128)(2,1)} %bitcast.79, bf16[2048,2816]{1,0:T(8,128)(2,1)} %all-gather.9.cloned.1.call-done.refs_2_), kind=kOutput, calls=%fused_computation.44 | convolution fusion | flops 11811160064 | bytes 27262976 | tf_op jit(solution)/shard_map/dot_general | solution.py:18
  242.4 1.8 multiply_convert_fusion.2.refs_0_
  244.3 3.5 copy-done.22
  247.8 1.5 copy-done.25
  249.3 8.3 %convolution_convert_fusion.1 = bf16[1408,2048]{1,0:T(8,128)(2,1)} fusion(bf16[1024,1408]{1,0:T(8,128)(2,1)S(1)} %multiply_convert_fusion.2.refs_0_, bf16[1024,2048]{1,0:T(8,128)(2,1)S(1)} %bitcast.57), kind=kOutput, calls=%fused_computation.5 | convolution fusion | flops 5908463616 | bytes 12845056 | tf_op jit(solution)/shard_map/dot_general | solution.py:18
  257.7 27.8 %all-gather.11.cloned.1.call-done.refs_1_ = bf16[1408,2048]{1,0:T(8,128)(2,1)} async-done(((bf16[176,2048]{1,0:T(8,128)(2,1)}), bf16[1408,2048]{1,0:T(8,128)(2,1)}) %all-gather.11.cloned.1.call-update) | async-done | bytes 5767184 | tf_op jit(solution)/shard_map/all_gather | solution.py:1058
  285.5 15.6 %multiply_convert_fusion = (bf16[1024,1408]{1,0:T(8,128)(2,1)}, bf16[1024,1408]{1,0:T(8,128)(2,1)}) fusion(f32[1024,2816]{1,0:T(8,128)} %copy-done.22, bf16[1024,2048]{1,0:T(8,128)(2,1)} %bitcast.56, bf16[1408,2048]{1,0:T(8,128)(2,1)} %all-gather.11.cloned.1.call-done.refs_1_), kind=kOutput, calls=%fused_computation.8 | convolution fusion | flops 5924323328 | bytes 27262976 | tf_op jit(solution)/shard_map/dot_general | solution.py:18
  301.1 52.9 %down_and_terms.1 = (bf16[256,2048]{1,0:T(8,128)(2,1)}, bf16[2048,1408]{1,0:T(8,128)(2,1)}, bf16[2048,1408]{1,0:T(8,128)(2,1)}) custom-call(bf16[1024,1408]{1,0:T(8,128)(2,1)} %copy-done.25, bf16[1408,2048]{1,0:T(8,128)(2,1)} %all-gather.11.cloned.1.call-done.refs_1_, f32[256,2048]{1,0:T(8,128)} %get-tuple-element.77.refs_2_.refs_3_, ...), custom_call_target="tpu_custom_call" | custom-call | flops 5905580032 | bytes 83886080 | tf_op jit(solution)/shard_map/down_and_terms/pallas_call | solution.py:769
  354.9 86.6 %branch_grad.1 = (bf16[4,256,2048]{2,1,0:T(8,128)(2,1)}, f32[256,2048]{1,0:T(8,128)}) custom-call(bf16[1024,1408]{1,0:T(8,128)(2,1)} %get-tuple-element.88.refs_4_.refs_0_, bf16[1024,1408]{1,0:T(8,128)(2,1)} %get-tuple-element.89.refs_5_.refs_1_, bf16[2048,2816]{1,0:T(8,128)(2,1)} %all-gather.9.cloned.1.call-done.refs_2_, ...), custom_call_target="tpu_custom_call" | custom-call | flops 11811160064 | bytes 167772160 | tf_op jit(solution)/shard_map/branch_grad/pallas_call | solution.py:769
  441.6 1.5 collective-permute-start.6
  443.9 1.2 collective-permute-start.4
  445.2 1.5 collective-permute-start.9
  447.4 6.0 convolution_convert_fusion.2
  453.4 5.4 fusion.18.grad_ref
  458.9 18.6 %mix_backward.1 = (bf16[1024,1664]{1,0:T(8,128)(2,1)S(1)}, f32[12,512]{1,0:T(8,128)S(1)}, f32[1,128]{1,0:T(1,128)S(1)}) custom-call(bf16[1024,1536]{1,0:T(8,128)(2,1)S(1)} %copy-done.12, bf16[1024,1536]{1,0:T(8,128)(2,1)S(1)} %copy-done.12, f32[1024,128]{1,0:T(8,128)S(1)} %fusion.9.logit_ref, f32[12,512]{1,0:T(8,128)S(1)} %constant_dynamic-slice_fusion.2.table_ref, ...), custom_call_target="tpu_custom_call" | custom-call | flops 20971520000 | bytes 13631488 | tf_op jit(solution)/shard_map/mix_backward/pallas_call | solution.py:302
  477.6 1.7 copy-done.10
  479.5 1.3 collective-permute-start.7
  480.8 2.0 reduce-scatter.10.cloned.1.call-done.refs_0_
  482.8 12.6 %convolution_convert_fusion = bf16[2048,1664]{1,0:T(8,128)(2,1)} fusion(bf16[1024,2048]{1,0:T(8,128)(2,1)} %fusion.1, bf16[1024,1664]{1,0:T(8,128)(2,1)} %copy-done.10), kind=kOutput, calls=%fused_computation.4 | convolution fusion | flops 6982729728 | bytes 14417920 | tf_op jit(solution)/shard_map/dot_general | solution.py:18
  495.4 3.2 dynamic_update_slice.3
  498.6 5.0 place.3
  505.2 50.0 %input_grad.1 = (f32[256,2048]{1,0:T(8,128)}, f32[8,128]{1,0:T(8,128)}) custom-call(bf16[1024,1664]{1,0:T(8,128)(2,1)} %copy-done.10, bf16[2048,1664]{1,0:T(8,128)(2,1)} %all-gather.5.cloned.1.call-done.refs_1_, bf16[256,2048]{1,0:T(8,128)(2,1)} %bitcast.61, f32[256,2048]{1,0:T(8,128)} %get-tuple-element.107.refs_3_, f32[1,2048]{1,0:T(1,128)} %bitcast.72, ...), custom_call_target="tpu_custom_call" | custom-call | flops 6979321856 | bytes 83886080 | tf_op jit(solution)/shard_map/input_grad/pallas_call | solution.py:769
  555.2 25.5 %gather.2.refs_5_ = bf16[4,256,1408]{2,1,0:T(8,128)(2,1)S(1)} custom-call(bf16[256,1408]{1,0:T(8,128)(2,1)S(1)} %copy-done.4), custom_call_target="tpu_custom_call" | custom-call | bytes 57671680 | tf_op jit(solution)/shard_map/gather/pallas_call | solution.py:436
  580.9 1.2 slice_bitcast_fusion.2
  582.0 1.2 copy-done.3
  583.2 1.1 copy-done.5
  584.3 1.1 copy-done.7
  585.4 30.3 %spread.1 = (bf16[4,256,1664]{2,1,0:T(8,128)(2,1)S(1)}, bf16[256,11264]{1,0:T(8,128)(2,1)}, f32[256,128]{1,0:T(8,128)S(1)}) custom-call(bf16[256,1664]{1,0:T(8,128)(2,1)S(1)} %copy-done.3, bf16[256,1408]{1,0:T(8,128)(2,1)S(1)} %copy-done.5, bf16[256,1408]{1,0:T(8,128)(2,1)S(1)} %copy-done.7, bf16[256,1408]{1,0:T(8,128)(2,1)} %collective-permute-done.8.refs_3_, ...), custom_call_target="tpu_custom_call" | custom-call | bytes 68157440 | tf_op jit(solution)/shard_map/spread/pallas_call | solution.py:436
  615.7 3.4 assemble_columns.1
  620.0 1.6 collective-permute-start.10
  622.2 8.4 %convert_element_type.87 = f32[256,11264]{1,0:T(8,128)} convert(bf16[256,11264]{1,0:T(8,128)(2,1)} %get-tuple-element.127) | non-fusion elementwise | flops 2883584 | bytes 17301504 | tf_op jit(solution)/shard_map/convert_element_type | solution.py:1166
  631.2 21.7 %gather.3 = bf16[4,64,2048]{2,1,0:T(8,128)(2,1)S(1)} custom-call(bf16[64,2048]{1,0:T(8,128)(2,1)S(1)} %collective-permute-done.10.refs_0_), custom_call_target="tpu_custom_call" | custom-call | bytes 20971520 | tf_op jit(solution)/shard_map/gather/pallas_call | solution.py:436
  652.9 1.6 bitcast_convert_fusion
  655.5 1.3 copy.36
  (136 shorter events, 17.5 us)
Async XLA Ops:
  7.2 80.0 %copy-start = (bf16[704,2048]{1,0:T(8,128)(2,1)S(1)}, bf16[704,2048]{1,0:T(8,128)(2,1)}, u32[]{:S(2)}) copy-start(bf16[704,2048]{1,0:T(8,128)(2,1)} %param.21) | copy-start | bytes 8650756
  7.2 89.0 %all-gather.5.cloned.1.call-start = ((), (), s32[]{:S(2)}) async-start(), calls=%async_computation.5 | async-start | bytes 7667712 | tf_op jit(solution)/shard_map/all_gather | solution.py:1058
  8.2 11.5 %copy-start.28 = (bf16[256,16]{1,0:T(8,128)(2,1)}, bf16[256,16]{1,0:T(8,128)(2,1)S(1)}, u32[]{:S(2)}) copy-start(bf16[256,16]{1,0:T(8,128)(2,1)S(1)} %copy.26) | copy-start | bytes 24580
  10.5 130.2 %all-gather.7.cloned.1.call-start = ((), (), s32[]{:S(2)}) async-start(), calls=%async_computation.6 | async-start | bytes 2359296 | tf_op jit(solution)/shard_map/all_gather | solution.py:1058
  11.5 0.7 collective-permute-start.3
  12.9 6.9 %copy-start.35 = (bf16[256]{0:T(256)(128)(2,1)S(1)}, bf16[256]{0:T(256)(128)(2,1)}, u32[]{:S(2)}) copy-start(bf16[256]{0:T(256)(128)(2,1)} %param.13) | copy-start | bytes 1540
  12.9 6.9 %copy-start.33 = (bf16[256]{0:T(256)(128)(2,1)S(1)}, bf16[256]{0:T(256)(128)(2,1)}, u32[]{:S(2)}) copy-start(bf16[256]{0:T(256)(128)(2,1)} %param.19) | copy-start | bytes 1540
  13.0 6.9 %copy-start.32 = (bf16[256,12]{0,1:T(8,128)(2,1)S(1)}, bf16[256,12]{0,1:T(8,128)(2,1)}, u32[]{:S(2)}) copy-start(bf16[256,12]{0,1:T(8,128)(2,1)} %param.16) | copy-start | bytes 18436
  13.0 212.2 %all-gather.9.cloned.1.call-start = ((), (), s32[]{:S(2)}) async-start(), calls=%async_computation.7 | async-start | bytes 12976128 | tf_op jit(solution)/shard_map/all_gather | solution.py:1058
  19.7 70.1 %copy-start.37 = (bf16[128]{0:T(256)(128)(2,1)S(1)}, bf16[128]{0:T(256)(128)(2,1)}, u32[]{:S(2)}) copy-start(bf16[128]{0:T(256)(128)(2,1)} %param.17) | copy-start | bytes 772
  19.8 265.7 %all-gather.11.cloned.1.call-start = ((), (), s32[]{:S(2)}) async-start(), calls=%async_computation.8 | async-start | bytes 6488064 | tf_op jit(solution)/shard_map/all_gather | solution.py:1058
  83.6 51.5 %collective-permute-start.2 = (bf16[256,2048]{1,0:T(8,128)(2,1)}, bf16[256,2048]{1,0:T(8,128)(2,1)}, u32[]{:S(2)}, u32[]{:S(2)}) collective-permute-start(bf16[256,2048]{1,0:T(8,128)(2,1)} %bitcast.63), channel_id=1, source_target_pairs={{0,3},{1,2},{2,1},{3,0},{4,7},{5,6},{6,5},{7,4},{8,11},{9,10},{10,... | collective-permute-start | bytes 3145736 | tf_op jit(solution)/shard_map/ppermute | solution.py:853
  85.1 50.0 %collective-permute-start.1 = (bf16[256,2048]{1,0:T(8,128)(2,1)}, bf16[256,2048]{1,0:T(8,128)(2,1)}, u32[]{:S(2)}, u32[]{:S(2)}) collective-permute-start(bf16[256,2048]{1,0:T(8,128)(2,1)} %bitcast.64), channel_id=1, source_target_pairs={{0,2},{1,3},{2,0},{3,1},{4,6},{5,7},{6,4},{7,5},{8,10},{9,11},{10,... | collective-permute-start | bytes 3145736 | tf_op jit(solution)/shard_map/ppermute | solution.py:853
  85.1 50.0 %collective-permute-start = (bf16[256,2048]{1,0:T(8,128)(2,1)}, bf16[256,2048]{1,0:T(8,128)(2,1)}, u32[]{:S(2)}, u32[]{:S(2)}) collective-permute-start(bf16[256,2048]{1,0:T(8,128)(2,1)} %bitcast.65), channel_id=1, source_target_pairs={{0,1},{1,0},{2,3},{3,2},{4,5},{5,4},{6,7},{7,6},{8,9},{9,8},{10,11... | collective-permute-start | bytes 3145736 | tf_op jit(solution)/shard_map/ppermute | solution.py:853
  88.2 266.7 %reduce-scatter.6.cloned.1.call-start = ((), (), s32[]{:S(2)}) async-start(), calls=%async_computation.9 | async-start | bytes 6488064 | tf_op jit(solution)/shard_map/reduce_scatter | solution.py:1019
  89.9 6.3 copy-start.31
  96.2 11.0 %copy-start.23 = (bf16[1024,2048]{1,0:T(8,128)(2,1)S(1)}, bf16[1024,2048]{1,0:T(8,128)(2,1)}, u32[]{:S(2)}) copy-start(bf16[1024,2048]{1,0:T(8,128)(2,1)} %fusion.1) | copy-start | bytes 12582916
  107.2 24.9 %copy-start.11 = (bf16[1024,1536]{1,0:T(8,128)(2,1)}, bf16[1024,1536]{1,0:T(8,128)(2,1)S(1)}, u32[]{:S(2)}) copy-start(bf16[1024,1536]{1,0:T(8,128)(2,1)S(1)} %fusion.4.ahead_ref.proj_ref) | copy-start | bytes 9437188
  135.1 5.5 copy-start.8
  135.1 5.6 copy-start.13
  242.4 5.4 copy-start.22
  242.4 6.9 %copy-start.24 = (bf16[4,256,2048]{2,1,0:T(8,128)(2,1)S(1)}, bf16[4,256,2048]{2,1,0:T(8,128)(2,1)}, u32[]{:S(2)}) copy-start(bf16[4,256,2048]{2,1,0:T(8,128)(2,1)} %place.2) | copy-start | bytes 12582916
  257.7 183.9 %reduce-scatter.8.cloned.1.call-start = ((), (), s32[]{:S(2)}) async-start(), calls=%async_computation.10 | async-start | bytes 6488064 | tf_op jit(solution)/shard_map/reduce_scatter | solution.py:1019
  354.1 128.7 %reduce-scatter.10.cloned.1.call-start = ((), (), s32[]{:S(2)}) async-start(), calls=%async_computation.11 | async-start | bytes 6488064 | tf_op jit(solution)/shard_map/reduce_scatter | solution.py:1019
  354.8 92.6 %copy-start.9 = (bf16[1024,512]{1,0:T(8,128)(2,1)S(1)}, bf16[1024,512]{1,0:T(8,128)(2,1)}, u32[]{:S(2)}) copy-start(bf16[1024,512]{1,0:T(8,128)(2,1)} %copy-done.8) | copy-start | bytes 3145732
  354.9 225.9 %reduce-scatter.12.cloned.1.call-start = ((), (), s32[]{:S(2)}) async-start(), calls=%async_computation.12 | async-start | bytes 7667712 | tf_op jit(solution)/shard_map/reduce_scatter | solution.py:1019
  441.6 37.9 %collective-permute-start.6 = (bf16[176,2048]{1,0:T(8,128)(2,1)}, bf16[176,2048]{1,0:T(8,128)(2,1)}, u32[]{:S(2)}, u32[]{:S(2)}) collective-permute-start(bf16[176,2048]{1,0:T(8,128)(2,1)} %reduce-scatter.6.cloned.1.call-done.refs_0_), channel_id=1, source_target_pairs={{0,3},{1,2},{2,1},{3,0},{4,7},{5,6},{6,5},{7,4},{8,11},{9,10},{10,... | collective-permute-start | bytes 2162696 | tf_op jit(solution)/shard_map/ppermute | solution.py:853
  443.1 39.6 %collective-permute-start.5 = (bf16[176,2048]{1,0:T(8,128)(2,1)}, bf16[176,2048]{1,0:T(8,128)(2,1)}, u32[]{:S(2)}, u32[]{:S(2)}) collective-permute-start(bf16[176,2048]{1,0:T(8,128)(2,1)} %reduce-scatter.6.cloned.1.call-done.refs_0_), channel_id=1, source_target_pairs={{0,2},{1,3},{2,0},{3,1},{4,6},{5,7},{6,4},{7,5},{8,10},{9,11},{10,... | collective-permute-start | bytes 2162696 | tf_op jit(solution)/shard_map/ppermute | solution.py:853
  443.9 38.8 %collective-permute-start.4 = (bf16[176,2048]{1,0:T(8,128)(2,1)}, bf16[176,2048]{1,0:T(8,128)(2,1)}, u32[]{:S(2)}, u32[]{:S(2)}) collective-permute-start(bf16[176,2048]{1,0:T(8,128)(2,1)} %reduce-scatter.6.cloned.1.call-done.refs_0_), channel_id=1, source_target_pairs={{0,1},{1,0},{2,3},{3,2},{4,5},{5,4},{6,7},{7,6},{8,9},{9,8},{10,11... | collective-permute-start | bytes 2162696 | tf_op jit(solution)/shard_map/ppermute | solution.py:853
  445.2 58.4 %collective-permute-start.9 = (bf16[256,1408]{1,0:T(8,128)(2,1)}, bf16[256,1408]{1,0:T(8,128)(2,1)}, u32[]{:S(2)}, u32[]{:S(2)}) collective-permute-start(bf16[256,1408]{1,0:T(8,128)(2,1)} %reduce-scatter.8.cloned.1.call-done.refs_1_), channel_id=1, source_target_pairs={{0,3},{1,2},{2,1},{3,0},{4,7},{5,6},{6,5},{7,4},{8,11},{9,10},{10,... | collective-permute-start | bytes 2162696 | tf_op jit(solution)/shard_map/ppermute | solution.py:853
  446.6 57.8 %collective-permute-start.8 = (bf16[256,1408]{1,0:T(8,128)(2,1)}, bf16[256,1408]{1,0:T(8,128)(2,1)}, u32[]{:S(2)}, u32[]{:S(2)}) collective-permute-start(bf16[256,1408]{1,0:T(8,128)(2,1)} %reduce-scatter.8.cloned.1.call-done.refs_1_), channel_id=1, source_target_pairs={{0,2},{1,3},{2,0},{3,1},{4,6},{5,7},{6,4},{7,5},{8,10},{9,11},{10,... | collective-permute-start | bytes 2162696 | tf_op jit(solution)/shard_map/ppermute | solution.py:853
  453.4 5.5 copy-start.12
  453.4 5.5 copy-start.14
  453.4 5.5 copy-start.16
  453.4 5.5 copy-start.18
  453.4 5.5 copy-start.20
  479.5 25.0 %collective-permute-start.7 = (bf16[256,1408]{1,0:T(8,128)(2,1)}, bf16[256,1408]{1,0:T(8,128)(2,1)S(1)}, u32[]{:S(2)}, u32[]{:S(2)}) collective-permute-start(bf16[256,1408]{1,0:T(8,128)(2,1)} %reduce-scatter.8.cloned.1.call-done.refs_1_), channel_id=1, source_target_pairs={{0,1},{1,0},{2,3},{3,2},{4,5},{5,4},{6,7},{7,6},{8,9},{9,8},{10,11... | collective-permute-start | bytes 2162696 | tf_op jit(solution)/shard_map/ppermute | solution.py:853
  504.5 50.8 %copy-start.6 = (bf16[256,1408]{1,0:T(8,128)(2,1)}, bf16[256,1408]{1,0:T(8,128)(2,1)S(1)}, u32[]{:S(2)}) copy-start(bf16[256,1408]{1,0:T(8,128)(2,1)S(1)} %collective-permute-done.7.refs_2_) | copy-start | bytes 2162692
  504.5 115.5 %reduce-scatter.14.cloned.1.call-start = ((), (), s32[]{:S(2)}) async-start(), calls=%async_computation.13 | async-start | bytes 2359296 | tf_op jit(solution)/shard_map/reduce_scatter | solution.py:1019
  505.2 50.0 %copy-start.4 = (bf16[256,1408]{1,0:T(8,128)(2,1)S(1)}, bf16[256,1408]{1,0:T(8,128)(2,1)}, u32[]{:S(2)}) copy-start(bf16[256,1408]{1,0:T(8,128)(2,1)} %reduce-scatter.10.cloned.1.call-done.refs_0_) | copy-start | bytes 2162692
  555.2 25.6 %copy-start.29 = (bf16[256,16]{1,0:T(8,128)(2,1)S(1)}, bf16[256,16]{1,0:T(8,128)(2,1)}, u32[]{:S(2)}) copy-start(bf16[256,16]{1,0:T(8,128)(2,1)} %copy-done.28) | copy-start | bytes 24580
  585.4 30.3 %copy-start.2 = (bf16[256,6144]{1,0:T(8,128)(2,1)S(1)}, bf16[256,6144]{1,0:T(8,128)(2,1)}, u32[]{:S(2)}) copy-start(bf16[256,6144]{1,0:T(8,128)(2,1)} %weight_ref.1) | copy-start | bytes 9437188
  615.7 5.9 copy-start.34
  615.7 5.9 copy-start.36
  620.0 11.2 %collective-permute-start.10 = (bf16[64,2048]{1,0:T(8,128)(2,1)}, bf16[64,2048]{1,0:T(8,128)(2,1)S(1)}, u32[]{:S(2)}, u32[]{:S(2)}) collective-permute-start(bf16[64,2048]{1,0:T(8,128)(2,1)} %reduce-scatter.14.cloned.1.call-done), channel_id=1, source_target_pairs={{0,0},{4,1},{8,2},{12,3},{16,4},{20,5},{24,6},{28,7},{1,8},{5,9},{... | collective-permute-start | bytes 786440 | tf_op jit(solution)/shard_map/ppermute | solution.py:1152
  630.6 23.9 %copy-start.27 = (bf16[256,2048]{1,0:T(8,128)(2,1)S(1)}, bf16[256,2048]{1,0:T(8,128)(2,1)}, u32[]{:S(2)}) copy-start(bf16[256,2048]{1,0:T(8,128)(2,1)} %get-tuple-element.83) | copy-start | bytes 3145732
  630.6 24.9 %copy-start.26 = (f32[256,2048]{1,0:T(8,128)S(1)}, f32[256,2048]{1,0:T(8,128)}, u32[]{:S(2)}) copy-start(f32[256,2048]{1,0:T(8,128)} %get-tuple-element.110) | copy-start | bytes 6291460
  631.2 25.6 %copy-start.1 = (bf16[704,2048]{1,0:T(8,128)(2,1)S(1)}, bf16[704,2048]{1,0:T(8,128)(2,1)}, u32[]{:S(2)}) copy-start(bf16[704,2048]{1,0:T(8,128)(2,1)} %param.21) | copy-start | bytes 8650756
  (10 other events, 15.3 us)
Sparse Core Ops, SparseCore 0:
  10.6 74.1 all-gather.4
  87.0 28.3 all-gather.6
  117.6 107.6 all-gather.8
  226.7 58.7 all-gather.10
  288.2 63.5 reduce-scatter.5
  354.2 62.9 reduce-scatter.7
  419.5 63.2 reduce-scatter.9
  504.6 73.4 reduce-scatter.11
  581.0 36.2 reduce-scatter.13

commit v4 on v3

--- a/solution.py
+++ b/solution.py
@@ -586,8 +586,18 @@
 STEP = 16
 
 
-def reduce_rows_kernel(flip, gathers, totals, fills, epilogue, lefts, in_count, out_count, *refs):
-    left_refs, right_ref, extra = refs[:lefts], refs[lefts], refs[lefts + 1 : in_count]
+def reduce_rows_kernel(
+    flip, gathers, totals, fills, streamed, epilogue, lefts, in_count, out_count, *refs
+):
+    streams, refs = refs[-1], refs[:-1]
+    held_count = sum(streamed)
+    held, refs = refs[-held_count:], refs[:-held_count]
+    loads, inputs, spot = [], [], 0
+    for source, wanted in zip(refs[:in_count], streamed):
+        inputs.append(held[spot] if wanted else source)
+        loads.append((source, held[spot]) if wanted else None)
+        spot += wanted
+    left_refs, right_ref, extra = inputs[:lefts], inputs[lefts], inputs[lefts + 1 :]
     outs = refs[in_count : in_count + out_count]
     far, wide_x, wide_y, own, get_a, get_b, get_x, get_y, send, arrive = refs[
         in_count + out_count : in_count + out_count + 10
@@ -595,6 +605,44 @@
     rest_refs = refs[in_count + out_count + 10 :]
     near = neighbours()
     me, across, along, opposite = near
+    rows, width = own.shape
+    tiles = width // TILE
+    turns = (opposite, across, along, me)
+
+    def left_copy(index, turn):
+        source, target = loads[index]
+        here = pl.ds(pl.multiple_of(turns[turn] * rows, rows), rows)
+        return pltpu.make_async_copy(
+            source.at[here], target.at[here], streams.at[index * 4 + turn]
+        )
+
+    def right_copy(tile):
+        source, target = loads[lefts]
+        columns = pl.ds(pl.multiple_of(tile * TILE, TILE), TILE)
+        if flip:
+            source, target = source.at[columns], target.at[columns]
+        else:
+            source, target = source.at[:, columns], target.at[:, columns]
+        return pltpu.make_async_copy(source, target, streams.at[lefts * 4 + tile])
+
+    def extra_copy(index):
+        source, target = loads[lefts + 1 + index]
+        return pltpu.make_async_copy(source, target, streams.at[lefts * 4 + tiles + index])
+
+    def need(*indices):
+        for index in indices:
+            if loads[lefts + 1 + index] is not None:
+                extra_copy(index).wait()
+
+    for turn in range(4):
+        for index in range(lefts):
+            left_copy(index, turn).start()
+        if turn == 0:
+            for tile in range(tiles):
+                right_copy(tile).start()
+    for index in range(len(extra)):
+        if loads[lefts + 1 + index] is not None:
+            extra_copy(index).start()
     if totals:
         mine, boxes, send_t, arrive_t = rest_refs
         spots = [(axis, lax.axis_index(axis), lax.axis_size(axis)) for axis in ("seq", "fsdp")]
@@ -605,16 +653,19 @@
         shares = send_share(0, 0, spots[0], mine, boxes, send_t, arrive_t)
     else:
         greet(across, along)
-    rows, width = own.shape
     split = half_of(rows)
     head, rest = pl.ds(0, split), pl.ds(split, rows - split)
 
-    def part(block, store):
-        here = pl.ds(pl.multiple_of(block * rows, rows), rows)
-
-        @pl.loop(0, width // TILE)
+    def part(turn, store):
+        here = pl.ds(pl.multiple_of(turns[turn] * rows, rows), rows)
+        for index in range(lefts):
+            left_copy(index, turn).wait()
+
+        @pl.loop(0, tiles)
         def _(tile):
             columns = pl.ds(pl.multiple_of(tile * TILE, TILE), TILE)
+            if turn == 0:
+                right_copy(tile).wait()
             value, base = 0.0, 0
             for left_ref in left_refs:
                 depth = pl.ds(base, left_ref.shape[1])
@@ -641,7 +692,7 @@
             )
             store[there, :] = low(total)
 
-    part(opposite, far)
+    part(0, far)
     if totals:
         mine[1] = add_shares(0, spots[0][2], shares, boxes)
         shares = send_share(1, spots[0][2] - 1, spots[1], mine, boxes, send_t, arrive_t)
@@ -651,13 +702,14 @@
     ]
     copies[0].start()
     copies[1].start()
-    part(across, wide_x)
+    part(1, wide_x)
     copies.append(remote(wide_x.at[head], get_x.at[head], send, arrive, 2, across))
     copies[2].start()
-    part(along, wide_y)
+    part(2, wide_y)
     if fills:
         copies.append(remote(wide_y.at[rest], get_y.at[rest], send, arrive, 3, along))
         copies[3].start()
+        need(1, 2)
         term(extra[1], extra[2], outs[1])
     else:
         copies.append(remote(wide_y.at[rest], get_y.at[rest], send, arrive, 3, along))
@@ -671,8 +723,10 @@
     copies.append(remote(wide_x.at[rest], get_x.at[rest], send, arrive, 5, across))
     copies[5].start()
     if fills:
+        need(3)
         term(extra[1], extra[3], outs[2])
-    part(me, own)
+    part(3, own)
+    need(*([0] if fills else range(len(extra))))
     for copy in copies[2:]:
         copy.wait_recv()
     epilogue_prepare = rest_refs[0] if gathers else None
@@ -766,6 +820,12 @@
             pltpu.SemaphoreType.DMA((1,)),
         ]
         out_specs[0] = pl.BlockSpec(memory_space=pl.ANY)
+    inputs = [*lefts, right, *extra]
+    streamed = tuple(array.size > 2**16 for array in inputs)
+    scratch += [
+        pltpu.VMEM(array.shape, array.dtype) for array, wanted in zip(inputs, streamed) if wanted
+    ]
+    scratch.append(pltpu.SemaphoreType.DMA((len(lefts) * 4 + width // TILE + len(extra),)))
     return pl.pallas_call(
         functools.partial(
             reduce_rows_kernel,
@@ -773,13 +833,16 @@
             gathers,
             totals,
             mode == "fill",
+            streamed,
             epilogue,
             len(lefts),
             len(lefts) + 1 + len(extra),
             len(outs),
         ),
         out_shape=outs,
-        in_specs=in_vmem(len(lefts) + 1 + len(extra)),
+        in_specs=[
+            pl.BlockSpec(memory_space=pl.ANY if wanted else pltpu.VMEM) for wanted in streamed
+        ],
         out_specs=out_specs,
         scratch_shapes=scratch,
         compiler_params=pltpu.CompilerParams(
@@ -1052,7 +1115,6 @@
         for f in range(f_count)
         for i in range(side)
     ]
-    strip = rows // side
 
     def everywhere(block):
         return lax.all_gather(block, "fsdp", axis=0, tiled=True)
@@ -1062,14 +1124,15 @@
     ]
     beta_part = lax.dynamic_slice_in_dim(w_beta, s * heads, heads, 1)
     parts.append(jnp.pad(beta_part, ((0, 0), (0, DK - heads))))
+    parts.append(lax.dynamic_slice_in_dim(w_out, s * wide, wide, 1))
     qkv_part = everywhere(jnp.concatenate(parts, axis=1))
     small = jnp.concatenate([norm1_gain[None], norm2_gain[None], conv_weight.T], axis=0)
     small = jnp.pad(small, ((0, 16 - small.shape[0]), (0, 0)))
-    piece = lax.dynamic_slice_in_dim(w_out, s * strip, strip, 0)
-    piece = lax.ppermute(piece, ("fsdp", "seq"), homes)
     source_all, small = start_gathers(source, small)
     sent, source_all = lax.optimization_barrier((upstream, source_all))
-    out_part = everywhere(piece)
+    out_part = lax.all_to_all(
+        qkv_part[:, depth:], "seq", split_axis=0, concat_axis=1, tiled=True
+    )
     upstreams = [upstream] + [swap(sent, step) for step in range(1, side)]
     small = small.transpose(1, 0, 2).reshape(small.shape[1], width).astype(jnp.float32)
     gain_first = small[0:1]

time: 668 us -> 654 us (0.979)
  Pallas kernels: 470 us -> 433 us
  local copies, waits for them, and re-layouts: 28 us -> 38.6 us
  waiting for transfers between devices: 37.7 us -> 45.6 us
    pallas_call x1, Pallas kernels: 63.2 us -> 44.2 us  [start_gathers(): pl.pallas_call(start_kernel, out_shape=[jax.ShapeDtypeStruct((many,) + bl...]
    pallas_call x4, Pallas kernels: 268 us -> 250 us  [fused_reduce(): pl.pallas_call(functools.partial(reduce_rows_kernel, flip, gathers, total...]
    reduce_scatter x5, waiting for transfers between devices: 2.06 us -> 18 us  [fsdp_sum(): return lax.psum_scatter(low(term), 'fsdp', scatter_dimension=0, tiled=True)]
    all_gather x4 -> x3, waiting for transfers between devices: 33.9 us -> 26.9 us  [everywhere(): return lax.all_gather(block, 'fsdp', axis=0, tiled=True)]
    unnamed x82 -> x84, local copies, waits for them, and re-layouts: 17.4 us -> 22.2 us
  transfers between devices with their start and end apart: 20 -> 19, of which waited for: 4 -> 5; matrix products, arithmetic and copies ran while one was open for 16% -> 17% of each run, Pallas kernels for 68% -> 63%
where the time goes in v4:
time: 654 us; the launch traced here: 649 us
  Pallas kernels  433 us (66%)
  matrix products  79 us (12%)
  waiting for transfers between devices  45.6 us (7%)
  local copies, waits for them, and re-layouts  38.6 us (6%)
  other arithmetic  20.5 us (3%)
  starting transfers between devices  17.2 us (3%)
  between operations  14.9 us (2%)
    pallas_call x4, Pallas kernels, fused_reduce(): pl.pallas_call(functools.partial(reduce_rows_kernel, flip, gathers, total...  250 us
    dot_general x8, matrix products, dotf(): lax.dot_general(left, right, (dims, ((), ())), preferred_element_type=jnp...  79 us
    pallas_call x3, Pallas kernels, beside_gather(): pl.pallas_call(functools.partial(gather_kernel, count, len(operands), len...  77.5 us
    pallas_call x1, Pallas kernels, start_gathers(): pl.pallas_call(start_kernel, out_shape=[jax.ShapeDtypeStruct((many,) + bl...  44.2 us
    all_gather x3, waiting for transfers between devices, everywhere(): return lax.all_gather(block, 'fsdp', axis=0, tiled=True)  26.9 us
    unnamed x84, local copies, waits for them, and re-layouts  22.2 us
    pallas_call x1, Pallas kernels, mix_forward(): pl.pallas_call(functools.partial(forward_kernel, heads, taps), grid=(coun...  22.1 us
    pallas_call x1, Pallas kernels, mix_backward(): pl.pallas_call(functools.partial(backward_kernel, heads, taps), grid=(cou...  18.6 us
  transfers between devices with their start and end apart: 19, of which 5 were waited for; matrix products, arithmetic and copies ran while one was open for 17% of the time, Pallas kernels for 63%

profile of v4, /device:TPU:0, one launch (start us, length us, event | category | flops | bytes accessed | tf_op | source)
XLA Modules:
  0.0 649.3 jit_solution(5077078009083376742)
XLA Ops:
  8.3 1.7 dynamic-slice_dynamic-update-slice_fusion.3
  10.0 1.7 dynamic-slice_dynamic-update-slice_fusion.2
  11.7 1.7 dynamic-slice_dynamic-update-slice_fusion.1
  14.0 1.7 dynamic-slice_dynamic-update-slice_fusion
  15.8 6.7 %pick_columns.1 = bf16[256,2816]{1,0:T(8,128)(2,1)} custom-call(bf16[256,11264]{1,0:T(8,128)(2,1)} %refs_6_.1), custom_call_target="tpu_custom_call" | custom-call | tf_op jit(solution)/shard_map/pick_columns/pallas_call | solution.py:983
  23.2 44.2 %start_gathers.1 = (bf16[4,256,2048]{2,1,0:T(8,128)(2,1)}, bf16[8,16,256]{2,1,0:T(8,128)(2,1)}) custom-call(bf16[256,2048]{1,0:T(8,128)(2,1)} %bitcast.65, bf16[16,256]{1,0:T(8,128)(2,1)} %fusion.13.small_ref), custom_call_target="tpu_custom_call" | custom-call | bytes 83886080 | tf_op jit(solution)/shard_map/start_gathers/pallas_call | solution.py:561
  67.4 1.5 collective-permute-start.2
  69.6 1.4 collective-permute-start
  73.7 3.2 multiply_reduce_fusion
  77.0 3.0 fusion.1
  80.1 25.1 %all-gather.4.cloned.1.call-done.refs_1_ = bf16[2048,2176]{1,0:T(8,128)(2,1)} async-done(((bf16[256,2176]{1,0:T(8,128)(2,1)}), bf16[2048,2176]{1,0:T(8,128)(2,1)}) %all-gather.4.cloned.1.call-update) | async-done | bytes 8912912 | tf_op jit(solution)/shard_map/all_gather | solution.py:1120
  105.1 3.0 slice.68
  108.2 4.5 all-to-all-start
  112.9 11.2 %fusion.4.ahead_ref.proj_ref = bf16[1024,1536]{1,0:T(8,128)(2,1)S(1)} fusion(bf16[1024,2048]{1,0:T(8,128)(2,1)} %fusion.1, bf16[2048,2176]{1,0:T(8,128)(2,1)} %all-gather.4.cloned.1.call-done.refs_1_), kind=kOutput, calls=%fused_computation.12 | convolution fusion | flops 6444023808 | bytes 13631488 | tf_op jit(solution)/shard_map/dot_general | solution.py:18
  124.1 2.7 fusion.7.logit_ref
  126.8 22.1 %mix_forward.1 = (bf16[1024,512]{1,0:T(8,128)(2,1)S(1)}, bf16[1024,512]{1,0:T(8,128)(2,1)S(1)}, bf16[1024,512]{1,0:T(8,128)(2,1)S(1)}, bf16[8,4,128,128]{3,2,1,0:T(8,128)(2,1)S(1)}, bf16[8,4,128,128]{3,2,1,0:T(8,128)(2,1)S(1)}) custom-call(bf16[1024,1536]{1,0:T(8,128)(2,1)S(1)} %fusion.4.ahead_ref.proj_ref, bf16[1024,1536]{1,0:T(8,128)(2,1)S(1)} %fusion.4.ahead_ref.proj_ref, ...), custom_call_target="tpu_custom_call" | custom-call | flops 20971520000 | bytes 8388608 | tf_op jit(solution)/shard_map/mix_forward/pallas_call | solution.py:267
  152.0 5.6 place.2
  157.6 3.2 copy.32
  160.8 79.4 %out_and_norm.1 = (bf16[4,256,2048]{2,1,0:T(8,128)(2,1)}, f32[256,2048]{1,0:T(8,128)}) custom-call(bf16[1024,512]{1,0:T(8,128)(2,1)} %copy-done.8, bf16[512,2048]{1,0:T(8,128)(2,1)} %bitcast.62, bf16[256,2048]{1,0:T(8,128)(2,1)} %bitcast.66, f32[1,2048]{1,0:T(1,128)} %bitcast.81), custom_call_target="tpu_custom_call" | custom-call | flops 2147483648 | bytes 167772160 | tf_op jit(solution)/shard_map/out_and_norm/pallas_call | solution.py:829
  240.2 17.3 %fusion.15 = f32[1024,2816]{1,0:T(8,128)S(1)} fusion(bf16[1024,2048]{1,0:T(8,128)(2,1)} %bitcast.85, bf16[2048,2816]{1,0:T(8,128)(2,1)} %all-gather.6.cloned.1.call-done.refs_2_), kind=kOutput, calls=%fused_computation.42 | convolution fusion | flops 11811160064 | bytes 27262976 | tf_op jit(solution)/shard_map/dot_general | solution.py:18
  257.6 2.0 multiply_convert_fusion.2.refs_0_
  259.6 3.3 copy-done.22
  263.0 1.6 copy-done.25
  264.6 8.1 %convolution_convert_fusion.1 = bf16[1408,2048]{1,0:T(8,128)(2,1)} fusion(bf16[1024,1408]{1,0:T(8,128)(2,1)S(1)} %multiply_convert_fusion.2.refs_0_, bf16[1024,2048]{1,0:T(8,128)(2,1)S(1)} %bitcast.61), kind=kOutput, calls=%fused_computation.5 | convolution fusion | flops 5908463616 | bytes 12845056 | tf_op jit(solution)/shard_map/dot_general | solution.py:18
  272.8 1.9 all-gather.8.cloned.1.call-done.refs_1_
  274.6 15.6 %multiply_convert_fusion = (bf16[1024,1408]{1,0:T(8,128)(2,1)}, bf16[1024,1408]{1,0:T(8,128)(2,1)}) fusion(f32[1024,2816]{1,0:T(8,128)} %copy-done.22, bf16[1024,2048]{1,0:T(8,128)(2,1)} %bitcast.60, bf16[1408,2048]{1,0:T(8,128)(2,1)} %all-gather.8.cloned.1.call-done.refs_1_), kind=kOutput, calls=%fused_computation.8 | convolution fusion | flops 5924323328 | bytes 27262976 | tf_op jit(solution)/shard_map/dot_general | solution.py:18
  290.3 46.2 %down_and_terms.1 = (bf16[256,2048]{1,0:T(8,128)(2,1)}, bf16[2048,1408]{1,0:T(8,128)(2,1)}, bf16[2048,1408]{1,0:T(8,128)(2,1)}) custom-call(bf16[1024,1408]{1,0:T(8,128)(2,1)} %copy-done.25, bf16[1408,2048]{1,0:T(8,128)(2,1)} %all-gather.8.cloned.1.call-done.refs_1_, f32[256,2048]{1,0:T(8,128)} %get-tuple-element.77.refs_2_.refs_3_, ...), custom_call_target="tpu_custom_call" | custom-call | flops 5905580032 | bytes 83886080 | tf_op jit(solution)/shard_map/down_and_terms/pallas_call | solution.py:829
  337.2 3.8 reduce-scatter.6.cloned.1.call-done.refs_0_
  341.0 79.3 %branch_grad.1 = (bf16[4,256,2048]{2,1,0:T(8,128)(2,1)}, f32[256,2048]{1,0:T(8,128)}) custom-call(bf16[1024,1408]{1,0:T(8,128)(2,1)} %get-tuple-element.88.refs_4_.refs_0_, bf16[1024,1408]{1,0:T(8,128)(2,1)} %get-tuple-element.89.refs_5_.refs_1_, bf16[2048,2816]{1,0:T(8,128)(2,1)} %all-gather.6.cloned.1.call-done.refs_2_, ...), custom_call_target="tpu_custom_call" | custom-call | flops 11811160064 | bytes 167772160 | tf_op jit(solution)/shard_map/branch_grad/pallas_call | solution.py:829
  420.3 1.5 collective-permute-start.5
  423.8 1.5 collective-permute-start.8
  426.2 6.0 convolution_convert_fusion.2
  432.2 5.4 fusion.16.grad_ref
  437.7 18.6 %mix_backward.1 = (bf16[1024,1664]{1,0:T(8,128)(2,1)S(1)}, f32[12,512]{1,0:T(8,128)S(1)}, f32[1,128]{1,0:T(1,128)S(1)}) custom-call(bf16[1024,1536]{1,0:T(8,128)(2,1)S(1)} %copy-done.12, bf16[1024,1536]{1,0:T(8,128)(2,1)S(1)} %copy-done.12, f32[1024,128]{1,0:T(8,128)S(1)} %fusion.7.logit_ref, f32[12,512]{1,0:T(8,128)S(1)} %constant_dynamic-slice_fusion.1.table_ref, ...), custom_call_target="tpu_custom_call" | custom-call | flops 20971520000 | bytes 13631488 | tf_op jit(solution)/shard_map/mix_backward/pallas_call | solution.py:302
  456.4 1.7 copy-done.10
  459.4 12.4 %reduce-scatter.10.cloned.1.call-done.refs_0_ = bf16[256,1408]{1,0:T(8,128)(2,1)} async-done(((bf16[2048,1408]{1,0:T(8,128)(2,1)}), bf16[256,1408]{1,0:T(8,128)(2,1)}) %reduce-scatter.10.cloned.1.call-update) | async-done | bytes 720912 | tf_op jit(solution)/shard_map/reduce_scatter | solution.py:1082
  471.8 12.6 %convolution_convert_fusion = bf16[2048,1664]{1,0:T(8,128)(2,1)} fusion(bf16[1024,2048]{1,0:T(8,128)(2,1)} %fusion.1, bf16[1024,1664]{1,0:T(8,128)(2,1)} %copy-done.10), kind=kOutput, calls=%fused_computation.4 | convolution fusion | flops 6982729728 | bytes 14417920 | tf_op jit(solution)/shard_map/dot_general | solution.py:18
  484.4 3.2 dynamic_update_slice.3
  487.6 5.0 place.3
  493.4 45.4 %input_grad.1 = (f32[256,2048]{1,0:T(8,128)}, f32[8,128]{1,0:T(8,128)}) custom-call(bf16[1024,1664]{1,0:T(8,128)(2,1)} %copy-done.10, bf16[2048,2176]{1,0:T(8,128)(2,1)} %all-gather.4.cloned.1.call-done.refs_1_, bf16[256,2048]{1,0:T(8,128)(2,1)} %bitcast.67, f32[256,2048]{1,0:T(8,128)} %get-tuple-element.107.refs_3_, f32[1,2048]{1,0:T(1,128)} %bitcast.78, ...), custom_call_target="tpu_custom_call" | custom-call | flops 6979321856 | bytes 83886080 | tf_op jit(solution)/shard_map/input_grad/pallas_call | solution.py:829
  538.8 25.2 %gather.2.refs_5_ = bf16[4,256,1408]{2,1,0:T(8,128)(2,1)S(1)} custom-call(bf16[256,1408]{1,0:T(8,128)(2,1)S(1)} %copy-done.4), custom_call_target="tpu_custom_call" | custom-call | bytes 57671680 | tf_op jit(solution)/shard_map/gather/pallas_call | solution.py:436
  564.0 1.8 reduce-scatter.12.cloned.1.call-done.refs_0_
  570.5 31.0 %spread.1 = (bf16[4,256,1664]{2,1,0:T(8,128)(2,1)S(1)}, bf16[256,11264]{1,0:T(8,128)(2,1)}, f32[256,128]{1,0:T(8,128)S(1)}) custom-call(bf16[256,1664]{1,0:T(8,128)(2,1)S(1)} %copy-done.3, bf16[256,1408]{1,0:T(8,128)(2,1)S(1)} %copy-done.5, bf16[256,1408]{1,0:T(8,128)(2,1)S(1)} %copy-done.7, bf16[256,1408]{1,0:T(8,128)(2,1)} %collective-permute-done.7.refs_3_, ...), custom_call_target="tpu_custom_call" | custom-call | bytes 68157440 | tf_op jit(solution)/shard_map/spread/pallas_call | solution.py:436
  601.5 3.4 assemble_columns.1
  605.8 1.6 collective-permute-start.9
  608.0 8.4 %convert_element_type.87 = f32[256,11264]{1,0:T(8,128)} convert(bf16[256,11264]{1,0:T(8,128)(2,1)} %get-tuple-element.127) | non-fusion elementwise | flops 2883584 | bytes 17301504 | tf_op jit(solution)/shard_map/convert_element_type | solution.py:1229
  617.0 21.3 %gather.3 = bf16[4,64,2048]{2,1,0:T(8,128)(2,1)S(1)} custom-call(bf16[64,2048]{1,0:T(8,128)(2,1)S(1)} %collective-permute-done.9.refs_0_), custom_call_target="tpu_custom_call" | custom-call | bytes 20971520 | tf_op jit(solution)/shard_map/gather/pallas_call | solution.py:436
  638.4 1.6 bitcast_convert_fusion
  (135 shorter events, 23.9 us)
Async XLA Ops:
  7.2 63.8 %copy-start = (bf16[704,2048]{1,0:T(8,128)(2,1)S(1)}, bf16[704,2048]{1,0:T(8,128)(2,1)}, u32[]{:S(2)}) copy-start(bf16[704,2048]{1,0:T(8,128)(2,1)} %param.21) | copy-start | bytes 8650756
  7.2 97.9 %all-gather.4.cloned.1.call-start = ((), (), s32[]{:S(2)}) async-start(), calls=%async_computation.6 | async-start | bytes 10027008 | tf_op jit(solution)/shard_map/all_gather | solution.py:1120
  8.2 14.3 %copy-start.28 = (bf16[256,16]{1,0:T(8,128)(2,1)}, bf16[256,16]{1,0:T(8,128)(2,1)S(1)}, u32[]{:S(2)}) copy-start(bf16[256,16]{1,0:T(8,128)(2,1)S(1)} %copy.27) | copy-start | bytes 24580
  15.7 6.9 %copy-start.34 = (bf16[256]{0:T(256)(128)(2,1)S(1)}, bf16[256]{0:T(256)(128)(2,1)}, u32[]{:S(2)}) copy-start(bf16[256]{0:T(256)(128)(2,1)} %param.13) | copy-start | bytes 1540
  15.7 6.9 %copy-start.32 = (bf16[256]{0:T(256)(128)(2,1)S(1)}, bf16[256]{0:T(256)(128)(2,1)}, u32[]{:S(2)}) copy-start(bf16[256]{0:T(256)(128)(2,1)} %param.19) | copy-start | bytes 1540
  15.7 6.9 %copy-start.31 = (bf16[256,12]{0,1:T(8,128)(2,1)S(1)}, bf16[256,12]{0,1:T(8,128)(2,1)}, u32[]{:S(2)}) copy-start(bf16[256,12]{0,1:T(8,128)(2,1)} %param.16) | copy-start | bytes 18436
  15.7 224.5 %all-gather.6.cloned.1.call-start = ((), (), s32[]{:S(2)}) async-start(), calls=%async_computation.7 | async-start | bytes 12976128 | tf_op jit(solution)/shard_map/all_gather | solution.py:1120
  22.5 51.2 %copy-start.36 = (bf16[128]{0:T(256)(128)(2,1)S(1)}, bf16[128]{0:T(256)(128)(2,1)}, u32[]{:S(2)}) copy-start(bf16[128]{0:T(256)(128)(2,1)} %param.17) | copy-start | bytes 772
  22.5 252.1 %all-gather.8.cloned.1.call-start = ((), (), s32[]{:S(2)}) async-start(), calls=%async_computation.8 | async-start | bytes 6488064 | tf_op jit(solution)/shard_map/all_gather | solution.py:1120
  67.4 84.5 %collective-permute-start.2 = (bf16[256,2048]{1,0:T(8,128)(2,1)}, bf16[256,2048]{1,0:T(8,128)(2,1)}, u32[]{:S(2)}, u32[]{:S(2)}) collective-permute-start(bf16[256,2048]{1,0:T(8,128)(2,1)} %bitcast.69), channel_id=1, source_target_pairs={{0,3},{1,2},{2,1},{3,0},{4,7},{5,6},{6,5},{7,4},{8,11},{9,10},{10,... | collective-permute-start | bytes 3145736 | tf_op jit(solution)/shard_map/ppermute | solution.py:916
  68.9 83.1 %collective-permute-start.1 = (bf16[256,2048]{1,0:T(8,128)(2,1)}, bf16[256,2048]{1,0:T(8,128)(2,1)}, u32[]{:S(2)}, u32[]{:S(2)}) collective-permute-start(bf16[256,2048]{1,0:T(8,128)(2,1)} %bitcast.70), channel_id=1, source_target_pairs={{0,2},{1,3},{2,0},{3,1},{4,6},{5,7},{6,4},{7,5},{8,10},{9,11},{10,... | collective-permute-start | bytes 3145736 | tf_op jit(solution)/shard_map/ppermute | solution.py:916
  69.6 82.4 %collective-permute-start = (bf16[256,2048]{1,0:T(8,128)(2,1)}, bf16[256,2048]{1,0:T(8,128)(2,1)}, u32[]{:S(2)}, u32[]{:S(2)}) collective-permute-start(bf16[256,2048]{1,0:T(8,128)(2,1)} %bitcast.71), channel_id=1, source_target_pairs={{0,1},{1,0},{2,3},{3,2},{4,5},{5,4},{6,7},{7,6},{8,9},{9,8},{10,11... | collective-permute-start | bytes 3145736 | tf_op jit(solution)/shard_map/ppermute | solution.py:916
  72.0 5.0 copy-start.21
  73.6 6.4 copy-start.30
  108.2 49.4 %all-to-all-start = ((bf16[4,512,512]{2,1,0:T(8,128)(2,1)}), bf16[4,512,512]{2,1,0:T(8,128)(2,1)}, u32[]{:S(2)}, u32[]{:S(2)}) async-start(bf16[4,512,512]{2,1,0:T(8,128)(2,1)} %bitcast.7), calls=%async_computation | async-start | bytes 4194304 | tf_op jit(solution)/shard_map/all_to_all | solution.py:1133
  112.7 228.3 %reduce-scatter.6.cloned.1.call-start = ((), (), s32[]{:S(2)}) async-start(), calls=%async_computation.9 | async-start | bytes 6488064 | tf_op jit(solution)/shard_map/reduce_scatter | solution.py:1082
  112.9 11.2 %copy-start.23 = (bf16[1024,2048]{1,0:T(8,128)(2,1)S(1)}, bf16[1024,2048]{1,0:T(8,128)(2,1)}, u32[]{:S(2)}) copy-start(bf16[1024,2048]{1,0:T(8,128)(2,1)} %fusion.1) | copy-start | bytes 12582916
  124.1 24.9 %copy-start.11 = (bf16[1024,1536]{1,0:T(8,128)(2,1)}, bf16[1024,1536]{1,0:T(8,128)(2,1)S(1)}, u32[]{:S(2)}) copy-start(bf16[1024,1536]{1,0:T(8,128)(2,1)S(1)} %fusion.4.ahead_ref.proj_ref) | copy-start | bytes 9437188
  152.0 5.6 copy-start.8
  152.0 5.6 copy-start.13
  257.5 5.4 copy-start.22
  257.6 7.0 %copy-start.24 = (bf16[4,256,2048]{2,1,0:T(8,128)(2,1)S(1)}, bf16[4,256,2048]{2,1,0:T(8,128)(2,1)}, u32[]{:S(2)}) copy-start(bf16[4,256,2048]{2,1,0:T(8,128)(2,1)} %place.2) | copy-start | bytes 12582916
  272.7 147.5 %reduce-scatter.8.cloned.1.call-start = ((), (), s32[]{:S(2)}) async-start(), calls=%async_computation.10 | async-start | bytes 6488064 | tf_op jit(solution)/shard_map/reduce_scatter | solution.py:1082
  336.6 135.2 %reduce-scatter.10.cloned.1.call-start = ((), (), s32[]{:S(2)}) async-start(), calls=%async_computation.11 | async-start | bytes 6488064 | tf_op jit(solution)/shard_map/reduce_scatter | solution.py:1082
  337.1 89.1 %copy-start.9 = (bf16[1024,512]{1,0:T(8,128)(2,1)S(1)}, bf16[1024,512]{1,0:T(8,128)(2,1)}, u32[]{:S(2)}) copy-start(bf16[1024,512]{1,0:T(8,128)(2,1)} %copy-done.8) | copy-start | bytes 3145732
  337.1 228.7 %reduce-scatter.12.cloned.1.call-start = ((), (), s32[]{:S(2)}) async-start(), calls=%async_computation.12 | async-start | bytes 7667712 | tf_op jit(solution)/shard_map/reduce_scatter | solution.py:1082
  420.3 38.0 %collective-permute-start.5 = (bf16[176,2048]{1,0:T(8,128)(2,1)}, bf16[176,2048]{1,0:T(8,128)(2,1)}, u32[]{:S(2)}, u32[]{:S(2)}) collective-permute-start(bf16[176,2048]{1,0:T(8,128)(2,1)} %reduce-scatter.6.cloned.1.call-done.refs_0_), channel_id=1, source_target_pairs={{0,3},{1,2},{2,1},{3,0},{4,7},{5,6},{6,5},{7,4},{8,11},{9,10},{10,... | collective-permute-start | bytes 2162696 | tf_op jit(solution)/shard_map/ppermute | solution.py:916
  421.8 50.0 %collective-permute-start.4 = (bf16[176,2048]{1,0:T(8,128)(2,1)}, bf16[176,2048]{1,0:T(8,128)(2,1)}, u32[]{:S(2)}, u32[]{:S(2)}) collective-permute-start(bf16[176,2048]{1,0:T(8,128)(2,1)} %reduce-scatter.6.cloned.1.call-done.refs_0_), channel_id=1, source_target_pairs={{0,2},{1,3},{2,0},{3,1},{4,6},{5,7},{6,4},{7,5},{8,10},{9,11},{10,... | collective-permute-start | bytes 2162696 | tf_op jit(solution)/shard_map/ppermute | solution.py:916
  422.7 49.1 %collective-permute-start.3 = (bf16[176,2048]{1,0:T(8,128)(2,1)}, bf16[176,2048]{1,0:T(8,128)(2,1)}, u32[]{:S(2)}, u32[]{:S(2)}) collective-permute-start(bf16[176,2048]{1,0:T(8,128)(2,1)} %reduce-scatter.6.cloned.1.call-done.refs_0_), channel_id=1, source_target_pairs={{0,1},{1,0},{2,3},{3,2},{4,5},{5,4},{6,7},{7,6},{8,9},{9,8},{10,11... | collective-permute-start | bytes 2162696 | tf_op jit(solution)/shard_map/ppermute | solution.py:916
  423.8 68.8 %collective-permute-start.8 = (bf16[256,1408]{1,0:T(8,128)(2,1)}, bf16[256,1408]{1,0:T(8,128)(2,1)}, u32[]{:S(2)}, u32[]{:S(2)}) collective-permute-start(bf16[256,1408]{1,0:T(8,128)(2,1)} %reduce-scatter.8.cloned.1.call-done.refs_1_), channel_id=1, source_target_pairs={{0,3},{1,2},{2,1},{3,0},{4,7},{5,6},{6,5},{7,4},{8,11},{9,10},{10,... | collective-permute-start | bytes 2162696 | tf_op jit(solution)/shard_map/ppermute | solution.py:916
  425.3 67.3 %collective-permute-start.7 = (bf16[256,1408]{1,0:T(8,128)(2,1)}, bf16[256,1408]{1,0:T(8,128)(2,1)}, u32[]{:S(2)}, u32[]{:S(2)}) collective-permute-start(bf16[256,1408]{1,0:T(8,128)(2,1)} %reduce-scatter.8.cloned.1.call-done.refs_1_), channel_id=1, source_target_pairs={{0,2},{1,3},{2,0},{3,1},{4,6},{5,7},{6,4},{7,5},{8,10},{9,11},{10,... | collective-permute-start | bytes 2162696 | tf_op jit(solution)/shard_map/ppermute | solution.py:916
  432.2 5.5 copy-start.12
  432.2 5.5 copy-start.14
  432.2 5.5 copy-start.16
  432.2 5.5 copy-start.18
  432.2 5.5 copy-start.20
  458.2 34.4 %collective-permute-start.6 = (bf16[256,1408]{1,0:T(8,128)(2,1)}, bf16[256,1408]{1,0:T(8,128)(2,1)S(1)}, u32[]{:S(2)}, u32[]{:S(2)}) collective-permute-start(bf16[256,1408]{1,0:T(8,128)(2,1)} %reduce-scatter.8.cloned.1.call-done.refs_1_), channel_id=1, source_target_pairs={{0,1},{1,0},{2,3},{3,2},{4,5},{5,4},{6,7},{7,6},{8,9},{9,8},{10,11... | collective-permute-start | bytes 2162696 | tf_op jit(solution)/shard_map/ppermute | solution.py:916
  492.6 46.2 %copy-start.6 = (bf16[256,1408]{1,0:T(8,128)(2,1)}, bf16[256,1408]{1,0:T(8,128)(2,1)S(1)}, u32[]{:S(2)}) copy-start(bf16[256,1408]{1,0:T(8,128)(2,1)S(1)} %collective-permute-done.6.refs_2_) | copy-start | bytes 2162692
  492.6 113.2 %reduce-scatter.14.cloned.1.call-start = ((), (), s32[]{:S(2)}) async-start(), calls=%async_computation.13 | async-start | bytes 2359296 | tf_op jit(solution)/shard_map/reduce_scatter | solution.py:1082
  493.4 45.4 %copy-start.4 = (bf16[256,1408]{1,0:T(8,128)(2,1)S(1)}, bf16[256,1408]{1,0:T(8,128)(2,1)}, u32[]{:S(2)}) copy-start(bf16[256,1408]{1,0:T(8,128)(2,1)} %reduce-scatter.10.cloned.1.call-done.refs_0_) | copy-start | bytes 2162692
  538.8 27.0 %copy-start.29 = (bf16[256,16]{1,0:T(8,128)(2,1)S(1)}, bf16[256,16]{1,0:T(8,128)(2,1)}, u32[]{:S(2)}) copy-start(bf16[256,16]{1,0:T(8,128)(2,1)} %copy-done.28) | copy-start | bytes 24580
  570.5 31.1 %copy-start.2 = (bf16[256,6144]{1,0:T(8,128)(2,1)S(1)}, bf16[256,6144]{1,0:T(8,128)(2,1)}, u32[]{:S(2)}) copy-start(bf16[256,6144]{1,0:T(8,128)(2,1)} %weight_ref.1) | copy-start | bytes 9437188
  601.5 5.9 copy-start.33
  601.5 5.9 copy-start.35
  605.8 11.2 %collective-permute-start.9 = (bf16[64,2048]{1,0:T(8,128)(2,1)}, bf16[64,2048]{1,0:T(8,128)(2,1)S(1)}, u32[]{:S(2)}, u32[]{:S(2)}) collective-permute-start(bf16[64,2048]{1,0:T(8,128)(2,1)} %reduce-scatter.14.cloned.1.call-done), channel_id=1, source_target_pairs={{0,0},{4,1},{8,2},{12,3},{16,4},{20,5},{24,6},{28,7},{1,8},{5,9},{... | collective-permute-start | bytes 786440 | tf_op jit(solution)/shard_map/ppermute | solution.py:1215
  616.4 23.6 %copy-start.27 = (bf16[256,2048]{1,0:T(8,128)(2,1)S(1)}, bf16[256,2048]{1,0:T(8,128)(2,1)}, u32[]{:S(2)}) copy-start(bf16[256,2048]{1,0:T(8,128)(2,1)} %get-tuple-element.83) | copy-start | bytes 3145732
  616.4 24.6 %copy-start.26 = (f32[256,2048]{1,0:T(8,128)S(1)}, f32[256,2048]{1,0:T(8,128)}, u32[]{:S(2)}) copy-start(f32[256,2048]{1,0:T(8,128)} %get-tuple-element.110) | copy-start | bytes 6291460
  617.0 25.3 %copy-start.1 = (bf16[704,2048]{1,0:T(8,128)(2,1)S(1)}, bf16[704,2048]{1,0:T(8,128)(2,1)}, u32[]{:S(2)}) copy-start(bf16[704,2048]{1,0:T(8,128)(2,1)} %param.21) | copy-start | bytes 8650756
  (8 other events, 9.8 us)
Sparse Core Ops, SparseCore 0:
  15.8 89.2 all-gather.3
  107.3 106.8 all-gather.5
  215.9 58.7 all-gather.7
  277.4 63.5 reduce-scatter.5
  343.1 63.2 reduce-scatter.7
  408.5 63.1 reduce-scatter.9
  492.8 73.0 reduce-scatter.11
  568.7 34.0 reduce-scatter.13

commit v5 on v4

--- a/solution.py
+++ b/solution.py
@@ -962,6 +962,32 @@
     )
 
 
+def pack_kernel(wide, qkv_ref, beta_ref, out_ref, packed_ref):
+    width = out_ref.shape[1]
+    base = lax.axis_index("seq") * wide
+    for part in range(3):
+        columns = pl.ds(pl.multiple_of(part * width + base, DK), wide)
+        packed_ref[:, pl.ds(part * wide, wide)] = qkv_ref[:, columns]
+    packed_ref[:, pl.ds(3 * wide, DK)] = beta_ref[...]
+    columns = pl.ds(pl.multiple_of(base, DK), wide)
+    packed_ref[:, pl.ds(3 * wide + DK, wide)] = out_ref[:, columns]
+
+
+def pack_parts(w_qkv, beta_part, w_out, wide):
+    rows = w_qkv.shape[0]
+    tile = 64
+    widths = (w_qkv.shape[1], DK, w_out.shape[1], 4 * wide + DK)
+    specs = [pl.BlockSpec((tile, size), lambda i: (i, 0)) for size in widths]
+    return pl.pallas_call(
+        functools.partial(pack_kernel, wide),
+        grid=(rows // tile,),
+        out_shape=jax.ShapeDtypeStruct((rows, widths[3]), w_qkv.dtype),
+        in_specs=specs[:3],
+        out_specs=specs[3],
+        name="pack_parts",
+    )(w_qkv, beta_part, w_out)
+
+
 def pick_kernel(side, share, source_ref, target_ref):
     me = lax.axis_index("seq")
     count = target_ref.shape[1] // share
@@ -1119,13 +1145,9 @@
     def everywhere(block):
         return lax.all_gather(block, "fsdp", axis=0, tiled=True)
 
-    parts = [
-        lax.dynamic_slice_in_dim(w_qkv, part * width + s * wide, wide, 1) for part in range(3)
-    ]
     beta_part = lax.dynamic_slice_in_dim(w_beta, s * heads, heads, 1)
-    parts.append(jnp.pad(beta_part, ((0, 0), (0, DK - heads))))
-    parts.append(lax.dynamic_slice_in_dim(w_out, s * wide, wide, 1))
-    qkv_part = everywhere(jnp.concatenate(parts, axis=1))
+    beta_part = jnp.pad(beta_part, ((0, 0), (0, DK - heads)))
+    qkv_part = everywhere(pack_parts(w_qkv, beta_part, w_out, wide))
     small = jnp.concatenate([norm1_gain[None], norm2_gain[None], conv_weight.T], axis=0)
     small = jnp.pad(small, ((0, 16 - small.shape[0]), (0, 0)))
     source_all, small = start_gathers(source, small)

time: 654 us -> 654 us (level)
    unnamed x84 -> x86, local copies, waits for them, and re-layouts: 22.2 us -> 21.8 us
where the time goes in v5:
time: 654 us; the launch traced here: 649 us
  Pallas kernels  437 us (67%)
  matrix products  79.1 us (12%)
  waiting for transfers between devices  43.7 us (7%)
  local copies, waits for them, and re-layouts  35.6 us (5%)
  other arithmetic  22.5 us (3%)
  starting transfers between devices  16.4 us (3%)
  between operations  14.9 us (2%)
    pallas_call x4, Pallas kernels, fused_reduce(): pl.pallas_call(functools.partial(reduce_rows_kernel, flip, gathers, total...  250 us
    dot_general x8, matrix products, dotf(): lax.dot_general(left, right, (dims, ((), ())), preferred_element_type=jnp...  79.1 us
    pallas_call x3, Pallas kernels, beside_gather(): pl.pallas_call(functools.partial(gather_kernel, count, len(operands), len...  77.5 us
    pallas_call x1, Pallas kernels, start_gathers(): pl.pallas_call(start_kernel, out_shape=[jax.ShapeDtypeStruct((many,) + bl...  44.2 us
    all_gather x3, waiting for transfers between devices, everywhere(): return lax.all_gather(block, 'fsdp', axis=0, tiled=True)  25.3 us
    pallas_call x1, Pallas kernels, mix_forward(): pl.pallas_call(functools.partial(forward_kernel, heads, taps), grid=(coun...  22 us
    unnamed x86, local copies, waits for them, and re-layouts  21.8 us
    pallas_call x1, Pallas kernels, mix_backward(): pl.pallas_call(functools.partial(backward_kernel, heads, taps), grid=(cou...  18.6 us
  transfers between devices with their start and end apart: 19, of which 5 were waited for; matrix products, arithmetic and copies ran while one was open for 17% of the time, Pallas kernels for 63%

profile of v5, /device:TPU:0, one launch (start us, length us, event | category | flops | bytes accessed | tf_op | source)
XLA Modules:
  0.0 648.8 jit_solution(7225100690230397855)
XLA Ops:
  9.0 4.0 pack_parts.1
  13.0 6.7 %pick_columns.1 = bf16[256,2816]{1,0:T(8,128)(2,1)} custom-call(bf16[256,11264]{1,0:T(8,128)(2,1)} %refs_6_.1), custom_call_target="tpu_custom_call" | custom-call | tf_op jit(solution)/shard_map/pick_columns/pallas_call | solution.py:1009
  20.5 44.2 %start_gathers.1 = (bf16[4,256,2048]{2,1,0:T(8,128)(2,1)}, bf16[8,16,256]{2,1,0:T(8,128)(2,1)}) custom-call(bf16[256,2048]{1,0:T(8,128)(2,1)} %bitcast.67, bf16[16,256]{1,0:T(8,128)(2,1)} %fusion.13.small_ref), custom_call_target="tpu_custom_call" | custom-call | bytes 83886080 | tf_op jit(solution)/shard_map/start_gathers/pallas_call | solution.py:561
  64.7 1.5 collective-permute-start.2
  66.8 1.4 collective-permute-start
  70.8 3.1 multiply_reduce_fusion
  74.1 5.2 fusion.1
  79.3 23.1 %all-gather.4.cloned.1.call-done.refs_1_ = bf16[2048,2176]{1,0:T(8,128)(2,1)} async-done(((bf16[256,2176]{1,0:T(8,128)(2,1)}), bf16[2048,2176]{1,0:T(8,128)(2,1)}) %all-gather.4.cloned.1.call-update) | async-done | bytes 8912912 | tf_op jit(solution)/shard_map/all_gather | solution.py:1146
  102.4 3.0 slice.68
  105.4 3.6 all-to-all-start
  109.3 11.1 %fusion.4.ahead_ref.proj_ref = bf16[1024,1536]{1,0:T(8,128)(2,1)S(1)} fusion(bf16[1024,2048]{1,0:T(8,128)(2,1)} %fusion.1, bf16[2048,2176]{1,0:T(8,128)(2,1)} %all-gather.4.cloned.1.call-done.refs_1_), kind=kOutput, calls=%fused_computation.12 | convolution fusion | flops 6444023808 | bytes 13631488 | tf_op jit(solution)/shard_map/dot_general | solution.py:18
  120.4 2.7 fusion.7.logit_ref
  123.1 22.0 %mix_forward.1 = (bf16[1024,512]{1,0:T(8,128)(2,1)S(1)}, bf16[1024,512]{1,0:T(8,128)(2,1)S(1)}, bf16[1024,512]{1,0:T(8,128)(2,1)S(1)}, bf16[8,4,128,128]{3,2,1,0:T(8,128)(2,1)S(1)}, bf16[8,4,128,128]{3,2,1,0:T(8,128)(2,1)S(1)}) custom-call(bf16[1024,1536]{1,0:T(8,128)(2,1)S(1)} %fusion.4.ahead_ref.proj_ref, bf16[1024,1536]{1,0:T(8,128)(2,1)S(1)} %fusion.4.ahead_ref.proj_ref, ...), custom_call_target="tpu_custom_call" | custom-call | flops 20971520000 | bytes 8388608 | tf_op jit(solution)/shard_map/mix_forward/pallas_call | solution.py:267
  150.1 4.9 place.2
  155.0 1.6 copy.32
  156.7 79.5 %out_and_norm.1 = (bf16[4,256,2048]{2,1,0:T(8,128)(2,1)}, f32[256,2048]{1,0:T(8,128)}) custom-call(bf16[1024,512]{1,0:T(8,128)(2,1)} %copy-done.13, bf16[512,2048]{1,0:T(8,128)(2,1)} %bitcast.64, bf16[256,2048]{1,0:T(8,128)(2,1)} %bitcast.68, f32[1,2048]{1,0:T(1,128)} %bitcast.83), custom_call_target="tpu_custom_call" | custom-call | flops 2147483648 | bytes 167772160 | tf_op jit(solution)/shard_map/out_and_norm/pallas_call | solution.py:829
  236.2 17.3 %fusion.15 = f32[1024,2816]{1,0:T(8,128)S(1)} fusion(bf16[1024,2048]{1,0:T(8,128)(2,1)} %bitcast.87, bf16[2048,2816]{1,0:T(8,128)(2,1)} %all-gather.6.cloned.1.call-done.refs_2_), kind=kOutput, calls=%fused_computation.37 | convolution fusion | flops 11811160064 | bytes 27262976 | tf_op jit(solution)/shard_map/dot_general | solution.py:18
  253.5 4.4 copy-done.25
  257.9 2.0 multiply_convert_fusion.2.refs_0_
  260.0 1.6 copy-done.28
  261.6 8.1 %convolution_convert_fusion.1 = bf16[1408,2048]{1,0:T(8,128)(2,1)} fusion(bf16[1024,1408]{1,0:T(8,128)(2,1)S(1)} %multiply_convert_fusion.2.refs_0_, bf16[1024,2048]{1,0:T(8,128)(2,1)S(1)} %bitcast.63), kind=kOutput, calls=%fused_computation.5 | convolution fusion | flops 5908463616 | bytes 12845056 | tf_op jit(solution)/shard_map/dot_general | solution.py:18
  269.7 2.2 all-gather.8.cloned.1.call-done.refs_1_
  271.9 15.6 %multiply_convert_fusion = (bf16[1024,1408]{1,0:T(8,128)(2,1)}, bf16[1024,1408]{1,0:T(8,128)(2,1)}) fusion(f32[1024,2816]{1,0:T(8,128)} %copy-done.25, bf16[1024,2048]{1,0:T(8,128)(2,1)} %bitcast.62, bf16[1408,2048]{1,0:T(8,128)(2,1)} %all-gather.8.cloned.1.call-done.refs_1_), kind=kOutput, calls=%fused_computation.8 | convolution fusion | flops 5924323328 | bytes 27262976 | tf_op jit(solution)/shard_map/dot_general | solution.py:18
  287.5 46.2 %down_and_terms.1 = (bf16[256,2048]{1,0:T(8,128)(2,1)}, bf16[2048,1408]{1,0:T(8,128)(2,1)}, bf16[2048,1408]{1,0:T(8,128)(2,1)}) custom-call(bf16[1024,1408]{1,0:T(8,128)(2,1)} %copy-done.28, bf16[1408,2048]{1,0:T(8,128)(2,1)} %all-gather.8.cloned.1.call-done.refs_1_, f32[256,2048]{1,0:T(8,128)} %get-tuple-element.77.refs_2_.refs_3_, ...), custom_call_target="tpu_custom_call" | custom-call | flops 5905580032 | bytes 83886080 | tf_op jit(solution)/shard_map/down_and_terms/pallas_call | solution.py:829
  334.4 3.8 reduce-scatter.6.cloned.1.call-done.refs_0_
  338.2 79.3 %branch_grad.1 = (bf16[4,256,2048]{2,1,0:T(8,128)(2,1)}, f32[256,2048]{1,0:T(8,128)}) custom-call(bf16[1024,1408]{1,0:T(8,128)(2,1)} %get-tuple-element.88.refs_4_.refs_0_, bf16[1024,1408]{1,0:T(8,128)(2,1)} %get-tuple-element.89.refs_5_.refs_1_, bf16[2048,2816]{1,0:T(8,128)(2,1)} %all-gather.6.cloned.1.call-done.refs_2_, ...), custom_call_target="tpu_custom_call" | custom-call | flops 11811160064 | bytes 167772160 | tf_op jit(solution)/shard_map/branch_grad/pallas_call | solution.py:829
  417.6 1.5 collective-permute-start.5
  421.1 1.5 collective-permute-start.8
  423.5 6.3 convolution_convert_fusion.2
  429.8 5.4 fusion.16.grad_ref
  435.3 18.6 %mix_backward.1 = (bf16[1024,1664]{1,0:T(8,128)(2,1)S(1)}, f32[12,512]{1,0:T(8,128)S(1)}, f32[1,128]{1,0:T(1,128)S(1)}) custom-call(bf16[1024,1536]{1,0:T(8,128)(2,1)S(1)} %copy-done.16, bf16[1024,1536]{1,0:T(8,128)(2,1)S(1)} %copy-done.16, f32[1024,128]{1,0:T(8,128)S(1)} %fusion.7.logit_ref, f32[12,512]{1,0:T(8,128)S(1)} %constant_dynamic-slice_fusion.1.table_ref, ...), custom_call_target="tpu_custom_call" | custom-call | flops 20971520000 | bytes 13631488 | tf_op jit(solution)/shard_map/mix_backward/pallas_call | solution.py:302
  453.8 1.7 copy-done.14
  455.7 1.2 collective-permute-start.6
  456.9 12.1 %reduce-scatter.10.cloned.1.call-done.refs_0_ = bf16[256,1408]{1,0:T(8,128)(2,1)} async-done(((bf16[2048,1408]{1,0:T(8,128)(2,1)}), bf16[256,1408]{1,0:T(8,128)(2,1)}) %reduce-scatter.10.cloned.1.call-update) | async-done | bytes 720912 | tf_op jit(solution)/shard_map/reduce_scatter | solution.py:1108
  469.0 12.6 %convolution_convert_fusion = bf16[2048,1664]{1,0:T(8,128)(2,1)} fusion(bf16[1024,2048]{1,0:T(8,128)(2,1)} %fusion.1, bf16[1024,1664]{1,0:T(8,128)(2,1)} %copy-done.14), kind=kOutput, calls=%fused_computation.4 | convolution fusion | flops 6982729728 | bytes 14417920 | tf_op jit(solution)/shard_map/dot_general | solution.py:18
  481.7 3.2 dynamic_update_slice.3
  484.9 5.0 place.3
  490.7 45.4 %input_grad.1 = (f32[256,2048]{1,0:T(8,128)}, f32[8,128]{1,0:T(8,128)}) custom-call(bf16[1024,1664]{1,0:T(8,128)(2,1)} %copy-done.14, bf16[2048,2176]{1,0:T(8,128)(2,1)} %all-gather.4.cloned.1.call-done.refs_1_, bf16[256,2048]{1,0:T(8,128)(2,1)} %bitcast.69, f32[256,2048]{1,0:T(8,128)} %get-tuple-element.107.refs_3_, f32[1,2048]{1,0:T(1,128)} %bitcast.80, ...), custom_call_target="tpu_custom_call" | custom-call | flops 6979321856 | bytes 83886080 | tf_op jit(solution)/shard_map/input_grad/pallas_call | solution.py:829
  536.2 25.2 %gather.2.refs_5_ = bf16[4,256,1408]{2,1,0:T(8,128)(2,1)S(1)} custom-call(bf16[256,1408]{1,0:T(8,128)(2,1)S(1)} %copy-done.4), custom_call_target="tpu_custom_call" | custom-call | bytes 57671680 | tf_op jit(solution)/shard_map/gather/pallas_call | solution.py:436
  561.3 1.8 reduce-scatter.12.cloned.1.call-done.refs_0_
  563.2 1.2 slice_bitcast_fusion.2
  570.0 31.0 %spread.1 = (bf16[4,256,1664]{2,1,0:T(8,128)(2,1)S(1)}, bf16[256,11264]{1,0:T(8,128)(2,1)}, f32[256,128]{1,0:T(8,128)S(1)}) custom-call(bf16[256,1664]{1,0:T(8,128)(2,1)S(1)} %copy-done.3, bf16[256,1408]{1,0:T(8,128)(2,1)S(1)} %copy-done.6, bf16[256,1408]{1,0:T(8,128)(2,1)S(1)} %copy-done.12, bf16[256,1408]{1,0:T(8,128)(2,1)S(1)} %copy-done.10, ...), custom_call_target="tpu_custom_call" | custom-call | bytes 68157440 | tf_op jit(solution)/shard_map/spread/pallas_call | solution.py:436
  601.0 3.4 assemble_columns.1
  605.3 1.6 collective-permute-start.9
  607.5 8.4 %convert_element_type.87 = f32[256,11264]{1,0:T(8,128)} convert(bf16[256,11264]{1,0:T(8,128)(2,1)} %get-tuple-element.127) | non-fusion elementwise | flops 2883584 | bytes 17301504 | tf_op jit(solution)/shard_map/convert_element_type | solution.py:1251
  616.5 21.3 %gather.3 = bf16[4,64,2048]{2,1,0:T(8,128)(2,1)S(1)} custom-call(bf16[64,2048]{1,0:T(8,128)(2,1)S(1)} %collective-permute-done.9.refs_0_), custom_call_target="tpu_custom_call" | custom-call | bytes 20971520 | tf_op jit(solution)/shard_map/gather/pallas_call | solution.py:436
  637.8 1.6 bitcast_convert_fusion
  640.5 1.3 copy.39
  (138 shorter events, 24.2 us)
Async XLA Ops:
  7.2 61.1 %copy-start = (bf16[704,2048]{1,0:T(8,128)(2,1)S(1)}, bf16[704,2048]{1,0:T(8,128)(2,1)}, u32[]{:S(2)}) copy-start(bf16[704,2048]{1,0:T(8,128)(2,1)} %param.21) | copy-start | bytes 8650756
  7.2 95.2 %all-gather.4.cloned.1.call-start = ((), (), s32[]{:S(2)}) async-start(), calls=%async_computation.6 | async-start | bytes 10027008 | tf_op jit(solution)/shard_map/all_gather | solution.py:1146
  8.2 11.5 %copy-start.31 = (bf16[256,16]{1,0:T(8,128)(2,1)}, bf16[256,16]{1,0:T(8,128)(2,1)S(1)}, u32[]{:S(2)}) copy-start(bf16[256,16]{1,0:T(8,128)(2,1)S(1)} %copy.27) | copy-start | bytes 24580
  12.9 6.9 %copy-start.37 = (bf16[256]{0:T(256)(128)(2,1)S(1)}, bf16[256]{0:T(256)(128)(2,1)}, u32[]{:S(2)}) copy-start(bf16[256]{0:T(256)(128)(2,1)} %param.13) | copy-start | bytes 1540
  12.9 6.9 %copy-start.35 = (bf16[256]{0:T(256)(128)(2,1)S(1)}, bf16[256]{0:T(256)(128)(2,1)}, u32[]{:S(2)}) copy-start(bf16[256]{0:T(256)(128)(2,1)} %param.19) | copy-start | bytes 1540
  13.0 6.9 %copy-start.34 = (bf16[256,12]{0,1:T(8,128)(2,1)S(1)}, bf16[256,12]{0,1:T(8,128)(2,1)}, u32[]{:S(2)}) copy-start(bf16[256,12]{0,1:T(8,128)(2,1)} %param.16) | copy-start | bytes 18436
  13.0 223.2 %all-gather.6.cloned.1.call-start = ((), (), s32[]{:S(2)}) async-start(), calls=%async_computation.7 | async-start | bytes 12976128 | tf_op jit(solution)/shard_map/all_gather | solution.py:1146
  19.7 51.0 %copy-start.39 = (bf16[128]{0:T(256)(128)(2,1)S(1)}, bf16[128]{0:T(256)(128)(2,1)}, u32[]{:S(2)}) copy-start(bf16[128]{0:T(256)(128)(2,1)} %param.17) | copy-start | bytes 772
  19.8 252.1 %all-gather.8.cloned.1.call-start = ((), (), s32[]{:S(2)}) async-start(), calls=%async_computation.8 | async-start | bytes 6488064 | tf_op jit(solution)/shard_map/all_gather | solution.py:1146
  64.7 85.4 %collective-permute-start.2 = (bf16[256,2048]{1,0:T(8,128)(2,1)}, bf16[256,2048]{1,0:T(8,128)(2,1)}, u32[]{:S(2)}, u32[]{:S(2)}) collective-permute-start(bf16[256,2048]{1,0:T(8,128)(2,1)} %bitcast.71), channel_id=1, source_target_pairs={{0,3},{1,2},{2,1},{3,0},{4,7},{5,6},{6,5},{7,4},{8,11},{9,10},{10,... | collective-permute-start | bytes 3145736 | tf_op jit(solution)/shard_map/ppermute | solution.py:916
  66.2 83.9 %collective-permute-start.1 = (bf16[256,2048]{1,0:T(8,128)(2,1)}, bf16[256,2048]{1,0:T(8,128)(2,1)}, u32[]{:S(2)}, u32[]{:S(2)}) collective-permute-start(bf16[256,2048]{1,0:T(8,128)(2,1)} %bitcast.72), channel_id=1, source_target_pairs={{0,2},{1,3},{2,0},{3,1},{4,6},{5,7},{6,4},{7,5},{8,10},{9,11},{10,... | collective-permute-start | bytes 3145736 | tf_op jit(solution)/shard_map/ppermute | solution.py:916
  66.8 83.3 %collective-permute-start = (bf16[256,2048]{1,0:T(8,128)(2,1)}, bf16[256,2048]{1,0:T(8,128)(2,1)}, u32[]{:S(2)}, u32[]{:S(2)}) collective-permute-start(bf16[256,2048]{1,0:T(8,128)(2,1)} %bitcast.73), channel_id=1, source_target_pairs={{0,1},{1,0},{2,3},{3,2},{4,5},{5,4},{6,7},{7,6},{8,9},{9,8},{10,11... | collective-permute-start | bytes 3145736 | tf_op jit(solution)/shard_map/ppermute | solution.py:916
  70.7 8.6 %copy-start.33 = (f32[1,8,256]{2,0,1:T(1,128)}, f32[1,8,256]{2,0,1:T(1,128)S(1)}, u32[]{:S(2)}) copy-start(f32[1,8,256]{2,0,1:T(1,128)S(1)} %get-tuple-element.132) | copy-start | bytes 24580
  105.4 49.6 %all-to-all-start = ((bf16[4,512,512]{2,1,0:T(8,128)(2,1)}), bf16[4,512,512]{2,1,0:T(8,128)(2,1)S(1)}, u32[]{:S(2)}, u32[]{:S(2)}) async-start(bf16[4,512,512]{2,1,0:T(8,128)(2,1)} %bitcast.60), calls=%async_computation | async-start | bytes 4194304 | tf_op jit(solution)/shard_map/all_to_all | solution.py:1155
  109.1 229.2 %reduce-scatter.6.cloned.1.call-start = ((), (), s32[]{:S(2)}) async-start(), calls=%async_computation.9 | async-start | bytes 6488064 | tf_op jit(solution)/shard_map/reduce_scatter | solution.py:1108
  109.3 11.1 %copy-start.26 = (bf16[1024,2048]{1,0:T(8,128)(2,1)S(1)}, bf16[1024,2048]{1,0:T(8,128)(2,1)}, u32[]{:S(2)}) copy-start(bf16[1024,2048]{1,0:T(8,128)(2,1)} %fusion.1) | copy-start | bytes 12582916
  120.4 24.8 %copy-start.15 = (bf16[1024,1536]{1,0:T(8,128)(2,1)}, bf16[1024,1536]{1,0:T(8,128)(2,1)S(1)}, u32[]{:S(2)}) copy-start(bf16[1024,1536]{1,0:T(8,128)(2,1)S(1)} %fusion.4.ahead_ref.proj_ref) | copy-start | bytes 9437188
  253.5 4.4 copy-start.25
  257.9 3.6 copy-start.27
  269.7 147.9 %reduce-scatter.8.cloned.1.call-start = ((), (), s32[]{:S(2)}) async-start(), calls=%async_computation.10 | async-start | bytes 6488064 | tf_op jit(solution)/shard_map/reduce_scatter | solution.py:1108
  333.8 135.2 %reduce-scatter.10.cloned.1.call-start = ((), (), s32[]{:S(2)}) async-start(), calls=%async_computation.11 | async-start | bytes 6488064 | tf_op jit(solution)/shard_map/reduce_scatter | solution.py:1108
  334.4 228.7 %reduce-scatter.12.cloned.1.call-start = ((), (), s32[]{:S(2)}) async-start(), calls=%async_computation.12 | async-start | bytes 7667712 | tf_op jit(solution)/shard_map/reduce_scatter | solution.py:1108
  417.6 38.2 %collective-permute-start.5 = (bf16[176,2048]{1,0:T(8,128)(2,1)}, bf16[176,2048]{1,0:T(8,128)(2,1)}, u32[]{:S(2)}, u32[]{:S(2)}) collective-permute-start(bf16[176,2048]{1,0:T(8,128)(2,1)} %reduce-scatter.6.cloned.1.call-done.refs_0_), channel_id=1, source_target_pairs={{0,3},{1,2},{2,1},{3,0},{4,7},{5,6},{6,5},{7,4},{8,11},{9,10},{10,... | collective-permute-start | bytes 2162696 | tf_op jit(solution)/shard_map/ppermute | solution.py:916
  419.1 49.9 %collective-permute-start.4 = (bf16[176,2048]{1,0:T(8,128)(2,1)}, bf16[176,2048]{1,0:T(8,128)(2,1)}, u32[]{:S(2)}, u32[]{:S(2)}) collective-permute-start(bf16[176,2048]{1,0:T(8,128)(2,1)} %reduce-scatter.6.cloned.1.call-done.refs_0_), channel_id=1, source_target_pairs={{0,2},{1,3},{2,0},{3,1},{4,6},{5,7},{6,4},{7,5},{8,10},{9,11},{10,... | collective-permute-start | bytes 2162696 | tf_op jit(solution)/shard_map/ppermute | solution.py:916
  420.0 49.1 %collective-permute-start.3 = (bf16[176,2048]{1,0:T(8,128)(2,1)}, bf16[176,2048]{1,0:T(8,128)(2,1)}, u32[]{:S(2)}, u32[]{:S(2)}) collective-permute-start(bf16[176,2048]{1,0:T(8,128)(2,1)} %reduce-scatter.6.cloned.1.call-done.refs_0_), channel_id=1, source_target_pairs={{0,1},{1,0},{2,3},{3,2},{4,5},{5,4},{6,7},{7,6},{8,9},{9,8},{10,11... | collective-permute-start | bytes 2162696 | tf_op jit(solution)/shard_map/ppermute | solution.py:916
  421.1 68.7 %collective-permute-start.8 = (bf16[256,1408]{1,0:T(8,128)(2,1)}, bf16[256,1408]{1,0:T(8,128)(2,1)S(1)}, u32[]{:S(2)}, u32[]{:S(2)}) collective-permute-start(bf16[256,1408]{1,0:T(8,128)(2,1)} %reduce-scatter.8.cloned.1.call-done.refs_1_), channel_id=1, source_target_pairs={{0,3},{1,2},{2,1},{3,0},{4,7},{5,6},{6,5},{7,4},{8,11},{9,10},{10,... | collective-permute-start | bytes 2162696 | tf_op jit(solution)/shard_map/ppermute | solution.py:916
  422.6 67.3 %collective-permute-start.7 = (bf16[256,1408]{1,0:T(8,128)(2,1)}, bf16[256,1408]{1,0:T(8,128)(2,1)S(1)}, u32[]{:S(2)}, u32[]{:S(2)}) collective-permute-start(bf16[256,1408]{1,0:T(8,128)(2,1)} %reduce-scatter.8.cloned.1.call-done.refs_1_), channel_id=1, source_target_pairs={{0,2},{1,3},{2,0},{3,1},{4,6},{5,7},{6,4},{7,5},{8,10},{9,11},{10,... | collective-permute-start | bytes 2162696 | tf_op jit(solution)/shard_map/ppermute | solution.py:916
  429.8 5.5 copy-start.16
  429.8 5.5 copy-start.18
  429.8 5.5 copy-start.20
  429.8 5.5 copy-start.22
  429.8 5.5 copy-start.24
  435.3 20.5 %copy-start.5 = (bf16[256,1408]{1,0:T(8,128)(2,1)S(1)}, bf16[256,1408]{1,0:T(8,128)(2,1)}, u32[]{:S(2)}) copy-start(bf16[256,1408]{1,0:T(8,128)(2,1)} %reduce-scatter.8.cloned.1.call-done.refs_1_) | copy-start | bytes 2162692
  453.8 1.7 copy-start.14
  455.7 34.1 %collective-permute-start.6 = (bf16[256,1408]{1,0:T(8,128)(2,1)S(1)}, bf16[256,1408]{1,0:T(8,128)(2,1)S(1)}, u32[]{:S(2)}, u32[]{:S(2)}) collective-permute-start(bf16[256,1408]{1,0:T(8,128)(2,1)S(1)} %copy-done.5), channel_id=1, source_target_pairs={{0,1},{1,0},{2,3},{3,2},{4,5},{5,4},{6,7},{7,6},{8,9},{9,8},{10,11... | collective-permute-start | bytes 2162696 | tf_op jit(solution)/shard_map/ppermute | solution.py:916
  489.9 46.3 %copy-start.7 = (bf16[256,1408]{1,0:T(8,128)(2,1)}, bf16[256,1408]{1,0:T(8,128)(2,1)S(1)}, u32[]{:S(2)}) copy-start(bf16[256,1408]{1,0:T(8,128)(2,1)S(1)} %collective-permute-done.8.refs_4_) | copy-start | bytes 2162692
  489.9 46.3 %copy-start.9 = (bf16[256,1408]{1,0:T(8,128)(2,1)}, bf16[256,1408]{1,0:T(8,128)(2,1)S(1)}, u32[]{:S(2)}) copy-start(bf16[256,1408]{1,0:T(8,128)(2,1)S(1)} %collective-permute-done.7.refs_3_) | copy-start | bytes 2162692
  489.9 46.2 %copy-start.11 = (bf16[256,1408]{1,0:T(8,128)(2,1)}, bf16[256,1408]{1,0:T(8,128)(2,1)S(1)}, u32[]{:S(2)}) copy-start(bf16[256,1408]{1,0:T(8,128)(2,1)S(1)} %collective-permute-done.6.refs_2_) | copy-start | bytes 2162692
  489.9 115.3 %reduce-scatter.14.cloned.1.call-start = ((), (), s32[]{:S(2)}) async-start(), calls=%async_computation.13 | async-start | bytes 2359296 | tf_op jit(solution)/shard_map/reduce_scatter | solution.py:1108
  490.7 45.5 %copy-start.4 = (bf16[256,1408]{1,0:T(8,128)(2,1)S(1)}, bf16[256,1408]{1,0:T(8,128)(2,1)}, u32[]{:S(2)}) copy-start(bf16[256,1408]{1,0:T(8,128)(2,1)} %reduce-scatter.10.cloned.1.call-done.refs_0_) | copy-start | bytes 2162692
  536.1 27.0 %copy-start.32 = (bf16[256,16]{1,0:T(8,128)(2,1)S(1)}, bf16[256,16]{1,0:T(8,128)(2,1)}, u32[]{:S(2)}) copy-start(bf16[256,16]{1,0:T(8,128)(2,1)} %copy-done.31) | copy-start | bytes 24580
  570.0 31.0 %copy-start.2 = (bf16[256,6144]{1,0:T(8,128)(2,1)S(1)}, bf16[256,6144]{1,0:T(8,128)(2,1)}, u32[]{:S(2)}) copy-start(bf16[256,6144]{1,0:T(8,128)(2,1)} %weight_ref.1) | copy-start | bytes 9437188
  601.0 5.9 copy-start.36
  601.0 5.9 copy-start.38
  605.3 11.2 %collective-permute-start.9 = (bf16[64,2048]{1,0:T(8,128)(2,1)}, bf16[64,2048]{1,0:T(8,128)(2,1)S(1)}, u32[]{:S(2)}, u32[]{:S(2)}) collective-permute-start(bf16[64,2048]{1,0:T(8,128)(2,1)} %reduce-scatter.14.cloned.1.call-done), channel_id=1, source_target_pairs={{0,0},{4,1},{8,2},{12,3},{16,4},{20,5},{24,6},{28,7},{1,8},{5,9},{... | collective-permute-start | bytes 786440 | tf_op jit(solution)/shard_map/ppermute | solution.py:1237
  615.9 23.6 %copy-start.30 = (bf16[256,2048]{1,0:T(8,128)(2,1)S(1)}, bf16[256,2048]{1,0:T(8,128)(2,1)}, u32[]{:S(2)}) copy-start(bf16[256,2048]{1,0:T(8,128)(2,1)} %get-tuple-element.83) | copy-start | bytes 3145732
  615.9 24.6 %copy-start.29 = (f32[256,2048]{1,0:T(8,128)S(1)}, f32[256,2048]{1,0:T(8,128)}, u32[]{:S(2)}) copy-start(f32[256,2048]{1,0:T(8,128)} %get-tuple-element.110) | copy-start | bytes 6291460
  616.5 25.3 %copy-start.1 = (bf16[704,2048]{1,0:T(8,128)(2,1)S(1)}, bf16[704,2048]{1,0:T(8,128)(2,1)}, u32[]{:S(2)}) copy-start(bf16[704,2048]{1,0:T(8,128)(2,1)} %param.21) | copy-start | bytes 8650756
  (11 other events, 12.2 us)
Sparse Core Ops, SparseCore 0:
  13.1 89.2 all-gather.3
  104.6 106.8 all-gather.5
  213.2 58.7 all-gather.7
  274.6 63.5 reduce-scatter.5
  340.4 63.2 reduce-scatter.7
  405.8 63.1 reduce-scatter.9
  490.1 73.0 reduce-scatter.11
  566.0 34.0 reduce-scatter.13
